TPU v7x, 128 devices: a whole 4x4x4 slice. The times are simulated.
128 devices in a mesh: dom: 64 (over x, z, y), feat: 2 (over core).
Axes of the slice: x: 4, y: 4, z: 4, core: 2. Of those that a mesh axis runs over, the one named last changes fastest.
Arguments:
- features: bfloat16 [262144, 256], P('dom', 'feat')
- send_rows: int32 [64, 64, 128], P('dom'), may hold values from 0 to 4095
- send_counts: int32 [64, 64], P('dom'), may hold values from 0 to 128, as said below
- tile_src: int32 [2048, 24], P('dom'), may hold values from 0 to 95
- edge_codes: int32 [2048, 24, 512], P('dom'), may hold values from 0 to 16383
- degrees: int32 [262144], P('dom'), may hold values from 16 to 511
- w_self: bfloat16 [256, 256], replicated, may hold values from -0.375 to 0.375
- w_neigh: bfloat16 [256, 256], replicated, may hold values from -0.375 to 0.375
- gamma: float32 [256], P('feat'), may hold values from 0.1 to 1.9
- beta: float32 [256], P('feat'), may hold values from -4 to 4
Outputs:
- node_out: bfloat16 [262144, 256], P('dom', 'feat')
Inputs may be any that keep to these rules, and one draw needn't show every extreme that they name: `send_rows`: entries are rows of the sending partition; repeats may occur. send_counts[d, d] is 0, and send_counts[d, (d + 1) % 64] is 128 for every d. `tile_src`: source tile numbers below 32 are the partition's own tiles; the rest are received rows. `edge_codes`: A code i * 128 + j is an edge from column j of the source tile to row i of the destination tile; repeated codes count as several edges.
All inputs are finite; a program needn't handle non-finite values.
Results may differ from a plain program's by a relative error of at most 0.0007.
Values may be sent and summed in bfloat16 or wider, within the bound.
No kernel may reach another device: no remote copies, remote signals or barrier semaphores. Data moves between devices by JAX's collectives and lax.ppermute only.
A program may use at most 64 MiB of HBM per device.

v0:
```python
import math

import jax
import jax.numpy as jnp
from jax import lax
from jax.sharding import PartitionSpec as P

TILE = 128


def local(
    features, send_rows, send_counts, tile_src, edge_codes, degrees, w_self, w_neigh, gamma, beta
):
    row_count, half_width = features.shape
    peer_count = lax.axis_size("dom")
    slot_count = send_rows.shape[2]
    slot_rows = send_rows[0]
    picked = features[slot_rows.reshape(-1)].reshape(peer_count, slot_count, half_width)
    live = jnp.arange(slot_count, dtype=jnp.int32)[None, :] < send_counts[0][:, None]
    outgoing = jnp.where(live[:, :, None], picked, jnp.zeros_like(picked))
    incoming = lax.all_to_all(outgoing, "dom", split_axis=0, concat_axis=0, tiled=True)
    sources = jnp.concatenate(
        [features, incoming.reshape(peer_count * slot_count, half_width)], axis=0
    )
    sources = sources.reshape(-1, TILE, half_width)
    dest_tiles = row_count // TILE
    per_tile = tile_src.shape[1]
    edge_count = edge_codes.shape[2]
    group_size = math.gcd(dest_tiles, 4)
    codes_all = edge_codes.reshape(dest_tiles // group_size, group_size, per_tile, edge_count)
    index_all = tile_src.reshape(dest_tiles // group_size, group_size, per_tile)
    tile_ids = jnp.arange(TILE, dtype=jnp.int32)

    def one_group(pair):
        codes, indices = pair
        dest_hot = ((codes // TILE)[..., None] == tile_ids).astype(jnp.bfloat16)
        source_hot = ((codes % TILE)[..., None] == tile_ids).astype(jnp.bfloat16)
        adjacency = jnp.einsum(
            "gkei,gkej->gkij", dest_hot, source_hot, preferred_element_type=jnp.float32
        ).astype(jnp.bfloat16)
        gathered = sources[indices]
        return jnp.einsum("gkij,gkjc->gic", adjacency, gathered, preferred_element_type=jnp.float32)

    sums = lax.map(one_group, (codes_all, index_all)).reshape(row_count, half_width)
    agg = (sums / degrees.astype(jnp.float32)[:, None]).astype(jnp.bfloat16)
    offset = lax.axis_index("feat") * half_width
    self_rows = lax.dynamic_slice_in_dim(w_self, offset, half_width, 0)
    neigh_rows = lax.dynamic_slice_in_dim(w_neigh, offset, half_width, 0)
    partial_value = jnp.dot(features, self_rows, preferred_element_type=jnp.float32) + jnp.dot(
        agg, neigh_rows, preferred_element_type=jnp.float32
    )
    pre = lax.psum_scatter(partial_value, "feat", scatter_dimension=1, tiled=True)
    node_total = float(row_count * peer_count)
    column_sum = lax.psum(jnp.sum(pre, axis=0), "dom")
    mean = column_sum / node_total
    centred = pre - mean
    square_sum = lax.psum(jnp.sum(centred * centred, axis=0), "dom")
    var = square_sum / node_total
    normed = gamma * (pre - mean) / jnp.sqrt(var + 1e-05) + beta
    return jnp.maximum(normed, 0.0).astype(jnp.bfloat16)


def solution(mesh):
    return jax.shard_map(
        local,
        mesh=mesh,
        in_specs=(
            P("dom", "feat"),
            P("dom", None, None),
            P("dom", None),
            P("dom", None),
            P("dom", None, None),
            P("dom"),
            P(),
            P(),
            P("feat"),
            P("feat"),
        ),
        out_specs=P("dom", "feat"),
        check_vma=False,
    )
```

profile of v0, /device:TPU:0, one launch (start us, length us, event | category | flops | bytes accessed | tf_op | source)
XLA Modules:
  0.0 801.5 jit_solution(3156116694202169208)
XLA Ops:
  6.5 0.8 compare_select_fusion.1
  7.4 0.7 iota_compare_fusion.20
  8.1 23.3 %gather_fusion.1 = bf16[8192,128]{1,0:T(8,128)(2,1)S(1)} fusion(bf16[4096,128]{1,0:T(8,128)(2,1)} %param.12, s32[8192]{0:T(1024)S(1)} %broadcast_clamp_fusion), kind=kCustom, calls=%fused_computation.1 | custom fusion | bytes 4227072 | tf_op jit(solution)/shard_map/gather | solution.py:18
  31.4 2.7 broadcast_select_fusion
  34.1 11.6 %all-to-all-start = ((bf16[64,128,128]{2,1,0:T(8,128)(2,1)}), bf16[64,128,128]{2,1,0:T(8,128)(2,1)S(1)}, u32[]{:S(2)}, u32[]{:S(2)}) async-start(bf16[64,128,128]{2,1,0:T(8,128)(2,1)} %broadcast_select_fusion), calls=%async_computation | async-start | bytes 4194304 | tf_op jit(solution)/shard_map/all_to_all | solution.py:21
  45.9 29.4 %all-to-all-done = bf16[64,128,128]{2,1,0:T(8,128)(2,1)S(1)} async-done(((bf16[64,128,128]{2,1,0:T(8,128)(2,1)}), bf16[64,128,128]{2,1,0:T(8,128)(2,1)S(1)}, u32[]{:S(2)}, u32[]{:S(2)}) %all-to-all-start) | async-done | bytes 2097184 | tf_op jit(solution)/shard_map/all_to_all | solution.py:21
  75.3 8.5 %pad_maximum_fusion = bf16[12288,128]{1,0:T(8,128)(2,1)} fusion(bf16[8192,128]{1,0:T(8,128)(2,1)S(1)} %bitcast.72, bf16[4096,128]{1,0:T(8,128)(2,1)S(1)} %copy-done.1), kind=kLoop, calls=%fused_computation.26 | loop fusion | flops 6291456 | bytes 6291456 | tf_op jit(solution)/shard_map/concatenate | solution.py:22
  83.8 339.2 %while.14 = (s32[]{:T(128)}, f32[8,4,128,128]{3,2,1,0:T(8,128)}, s32[8,4,24,512]{3,2,1,0:T(8,128)}, s32[8,4,24]{2,1,0:T(4,128)S(1)}, bf16[96,128,128]{2,1,0:T(8,128)(2,1)}, /*index=5*/s32[]{:T(128)}) while((s32[]{:T(128)}, f32[8,4,128,128]{3,2,1,0:T(8,128)}, s32[8,4,24,512]{3,2,1,0:T(8,128)}, ...), condition=%wide.region_1.2_spmd.clone.clone, body=%wide.region_0.1_spmd.clone.clone.sunk | while | flops 2028651776 | bytes 17275728 | solution.py:44
  83.8 1.1 add_select_fusion.4
  84.8 1.0 add_select_fusion.5
  85.8 31.0 %fusion.37 = bf16[4,24,128,128]{3,2,1,0:T(8,128)(2,1)} fusion(s32[4,24,512]{2,1,0:T(8,128)S(1)} %add_select_fusion.5, s32[4,24,512]{2,1,0:T(8,128)S(1)} %get-tuple-element.163), kind=kOutput, calls=%fused_computation.9.clone.clone.clone.clone.clone.1.clone.1 | convolution fusion | flops 1624768512 | bytes 3538944 | tf_op jit(solution)/shard_map/while/body/eval_jaxpr/gkei,gkej->gkij/dot_general | solution.py:38
  116.9 0.1 reshape.194
  117.0 4.6 gather_fusion
  121.6 4.5 fusion.38
  126.1 1.1 add_select_fusion.4
  127.2 1.0 add_select_fusion.5
  128.2 31.0 %fusion.37 = bf16[4,24,128,128]{3,2,1,0:T(8,128)(2,1)} fusion(s32[4,24,512]{2,1,0:T(8,128)S(1)} %add_select_fusion.5, s32[4,24,512]{2,1,0:T(8,128)S(1)} %get-tuple-element.163), kind=kOutput, calls=%fused_computation.9.clone.clone.clone.clone.clone.1.clone.1 | convolution fusion | flops 1624768512 | bytes 3538944 | tf_op jit(solution)/shard_map/while/body/eval_jaxpr/gkei,gkej->gkij/dot_general | solution.py:38
  159.3 0.1 reshape.194
  159.4 4.6 gather_fusion
  164.0 4.5 fusion.38
  168.5 1.1 add_select_fusion.4
  169.6 1.0 add_select_fusion.5
  170.6 31.0 %fusion.37 = bf16[4,24,128,128]{3,2,1,0:T(8,128)(2,1)} fusion(s32[4,24,512]{2,1,0:T(8,128)S(1)} %add_select_fusion.5, s32[4,24,512]{2,1,0:T(8,128)S(1)} %get-tuple-element.163), kind=kOutput, calls=%fused_computation.9.clone.clone.clone.clone.clone.1.clone.1 | convolution fusion | flops 1624768512 | bytes 3538944 | tf_op jit(solution)/shard_map/while/body/eval_jaxpr/gkei,gkej->gkij/dot_general | solution.py:38
  201.7 0.1 reshape.194
  201.8 4.6 gather_fusion
  206.4 4.5 fusion.38
  210.9 1.1 add_select_fusion.4
  212.0 1.0 add_select_fusion.5
  213.0 31.0 %fusion.37 = bf16[4,24,128,128]{3,2,1,0:T(8,128)(2,1)} fusion(s32[4,24,512]{2,1,0:T(8,128)S(1)} %add_select_fusion.5, s32[4,24,512]{2,1,0:T(8,128)S(1)} %get-tuple-element.163), kind=kOutput, calls=%fused_computation.9.clone.clone.clone.clone.clone.1.clone.1 | convolution fusion | flops 1624768512 | bytes 3538944 | tf_op jit(solution)/shard_map/while/body/eval_jaxpr/gkei,gkej->gkij/dot_general | solution.py:38
  244.1 0.1 reshape.194
  244.2 4.6 gather_fusion
  248.8 4.5 fusion.38
  253.3 1.1 add_select_fusion.4
  254.4 1.0 add_select_fusion.5
  255.4 31.0 %fusion.37 = bf16[4,24,128,128]{3,2,1,0:T(8,128)(2,1)} fusion(s32[4,24,512]{2,1,0:T(8,128)S(1)} %add_select_fusion.5, s32[4,24,512]{2,1,0:T(8,128)S(1)} %get-tuple-element.163), kind=kOutput, calls=%fused_computation.9.clone.clone.clone.clone.clone.1.clone.1 | convolution fusion | flops 1624768512 | bytes 3538944 | tf_op jit(solution)/shard_map/while/body/eval_jaxpr/gkei,gkej->gkij/dot_general | solution.py:38
  286.5 4.6 gather_fusion
  291.2 4.6 fusion.38
  295.7 1.1 add_select_fusion.4
  296.8 1.0 add_select_fusion.5
  297.8 31.0 %fusion.37 = bf16[4,24,128,128]{3,2,1,0:T(8,128)(2,1)} fusion(s32[4,24,512]{2,1,0:T(8,128)S(1)} %add_select_fusion.5, s32[4,24,512]{2,1,0:T(8,128)S(1)} %get-tuple-element.163), kind=kOutput, calls=%fused_computation.9.clone.clone.clone.clone.clone.1.clone.1 | convolution fusion | flops 1624768512 | bytes 3538944 | tf_op jit(solution)/shard_map/while/body/eval_jaxpr/gkei,gkej->gkij/dot_general | solution.py:38
  329.0 4.6 gather_fusion
  333.6 4.5 fusion.38
  338.1 1.1 add_select_fusion.4
  339.2 1.0 add_select_fusion.5
  340.2 31.0 %fusion.37 = bf16[4,24,128,128]{3,2,1,0:T(8,128)(2,1)} fusion(s32[4,24,512]{2,1,0:T(8,128)S(1)} %add_select_fusion.5, s32[4,24,512]{2,1,0:T(8,128)S(1)} %get-tuple-element.163), kind=kOutput, calls=%fused_computation.9.clone.clone.clone.clone.clone.1.clone.1 | convolution fusion | flops 1624768512 | bytes 3538944 | tf_op jit(solution)/shard_map/while/body/eval_jaxpr/gkei,gkej->gkij/dot_general | solution.py:38
  371.3 0.1 reshape.194
  371.4 4.6 gather_fusion
  376.0 4.5 fusion.38
  380.5 1.1 add_select_fusion.4
  381.6 1.0 add_select_fusion.5
  382.6 31.0 %fusion.37 = bf16[4,24,128,128]{3,2,1,0:T(8,128)(2,1)} fusion(s32[4,24,512]{2,1,0:T(8,128)S(1)} %add_select_fusion.5, s32[4,24,512]{2,1,0:T(8,128)S(1)} %get-tuple-element.163), kind=kOutput, calls=%fused_computation.9.clone.clone.clone.clone.clone.1.clone.1 | convolution fusion | flops 1624768512 | bytes 3538944 | tf_op jit(solution)/shard_map/while/body/eval_jaxpr/gkei,gkej->gkij/dot_general | solution.py:38
  413.8 4.6 gather_fusion
  418.4 4.5 fusion.38
  422.9 1.9 fusion.17
  424.9 0.7 fusion.18
  425.6 0.1 copy-done.3
  425.8 2.7 fusion.16
  428.5 11.2 %reduce-scatter.2.cloned.1.call-done = f32[4096,128]{0,1:T(8,128)} async-done(((f32[4096,256]{0,1:T(8,128)}), f32[4096,128]{0,1:T(8,128)}) %reduce-scatter.2.cloned.1.call-update) | async-done | bytes 2097168 | tf_op jit(solution)/shard_map/reduce_scatter | solution.py:52
  439.8 1.9 reduce_sum.18
  441.7 179.0 %psum.14 = f32[128]{0:T(128)S(1)} all-reduce(f32[128]{0:T(128)S(1)} %reduce_sum.18), channel_id=1, replica_groups=mesh['dom'=64,'feat'=2] {'dom'}, use_global_device_ids=true, to_apply=%region_4.5 | all-reduce | flops 128 | bytes 1024 | tf_op jit(solution)/shard_map/psum | solution.py:54
  620.7 0.4 multiply_reduce_fusion
  621.1 171.7 %psum.15 = f32[128]{0:T(128)S(1)} all-reduce(f32[128]{0:T(128)S(1)} %multiply_reduce_fusion), channel_id=1, replica_groups=mesh['dom'=64,'feat'=2] {'dom'}, use_global_device_ids=true, to_apply=%region_6.7 | all-reduce | flops 128 | bytes 1024 | tf_op jit(solution)/shard_map/psum | solution.py:57
  792.9 0.5 maximum_convert_fusion
  793.4 1.3 copy.13
  (42 shorter events, 0.5 us)
Async XLA Ops:
  6.5 418.3 %copy-start = (bf16[256,256]{1,0:T(8,128)(2,1)S(1)}, bf16[256,256]{1,0:T(8,128)(2,1)}, u32[]{:S(2)}) copy-start(bf16[256,256]{1,0:T(8,128)(2,1)} %param.19) | copy-start | bytes 393220
  34.1 11.7 %copy-start.5 = (s32[32,24]{0,1:T(8,128)S(1)}, s32[32,24]{0,1:T(8,128)}, u32[]{:S(2)}) copy-start(s32[32,24]{0,1:T(8,128)} %param.15) | copy-start | bytes 9220
  34.1 11.8 %copy-start.4 = (s32[4096]{0:T(1024)S(1)}, s32[4096]{0:T(1024)}, u32[]{:S(2)}) copy-start(s32[4096]{0:T(1024)} %param.17) | copy-start | bytes 49156
  34.1 41.2 %copy-start.1 = (bf16[4096,128]{1,0:T(8,128)(2,1)S(1)}, bf16[4096,128]{1,0:T(8,128)(2,1)}, u32[]{:S(2)}) copy-start(bf16[4096,128]{1,0:T(8,128)(2,1)} %param.12) | copy-start | bytes 3145732
  34.1 41.2 %all-to-all-start = ((bf16[64,128,128]{2,1,0:T(8,128)(2,1)}), bf16[64,128,128]{2,1,0:T(8,128)(2,1)S(1)}, u32[]{:S(2)}, u32[]{:S(2)}) async-start(bf16[64,128,128]{2,1,0:T(8,128)(2,1)} %broadcast_select_fusion), calls=%async_computation | async-start | bytes 4194304 | tf_op jit(solution)/shard_map/all_to_all | solution.py:21
  45.7 394.1 %reduce-scatter.2.cloned.1.call-start = ((), (), s32[]{:S(2)}) async-start(), calls=%async_computation.2 | async-start | bytes 6291456 | tf_op jit(solution)/shard_map/reduce_scatter | solution.py:52
  424.9 0.9 copy-start.3
  428.5 364.4 %copy-start.6 = (f32[128]{0:T(128)S(1)}, f32[128]{0:T(128)}, u32[]{:S(2)}) copy-start(f32[128]{0:T(128)} %param.21) | copy-start | bytes 1540
  428.5 364.4 %copy-start.7 = (f32[128]{0:T(128)S(1)}, f32[128]{0:T(128)}, u32[]{:S(2)}) copy-start(f32[128]{0:T(128)} %param.20) | copy-start | bytes 1540
  439.8 181.0 %copy-start.2 = (f32[4096,128]{0,1:T(8,128)S(1)}, f32[4096,128]{0,1:T(8,128)}, u32[]{:S(2)}) copy-start(f32[4096,128]{0,1:T(8,128)} %reduce-scatter.2.cloned.1.call-done) | copy-start | bytes 6291460
Sparse Core Ops, SparseCore 0:
  428.6 11.1 reduce-scatter.1
where the time goes:
time: 803 us; the launch traced here: 802 us
  blocking collectives  351 us (44%)
  matrix products  288 us (36%)
  local copies, waits for them, and re-layouts  62.6 us (8%)
  waiting for transfers between devices  40.7 us (5%)
  other arithmetic  34.1 us (4%)
  between operations  13.5 us (2%)
  starting transfers between devices  11.7 us (1%)
    dot_general x8, matrix products, one_group(): jnp.einsum('gkei,gkej->gkij', dest_hot, source_hot, preferred_element_typ...  248 us
    psum x1, blocking collectives, local(): column_sum = lax.psum(jnp.sum(pre, axis=0), 'dom')  179 us
    psum x1, blocking collectives, local(): square_sum = lax.psum(jnp.sum(centred * centred, axis=0), 'dom')  172 us
    gather x8, local copies, waits for them, and re-layouts, one_group(): gathered = sources[indices]  37.1 us
    dot_general x8, matrix products, one_group(): jnp.einsum('gkij,gkjc->gic', adjacency, gathered, preferred_element_type=...  36.2 us
    all_to_all x1, waiting for transfers between devices, local(): lax.all_to_all(outgoing, 'dom', split_axis=0, concat_axis=0, tiled=True)  29.4 us
    gather x1, local copies, waits for them, and re-layouts, local(): features[slot_rows.reshape(-1)].reshape(peer_count, slot_count, half_width)  23.3 us
  transfers between devices with their start and end apart: 2, of which 2 were waited for; matrix products, arithmetic and copies ran while one was open for 0% of the time, Pallas kernels for 0%

commit v1 on v0

v1 whole, which is shorter than its diff:
```python
import jax
import jax.numpy as jnp
from jax import lax
from jax.experimental import pallas as pl
from jax.experimental.pallas import tpu as pltpu
from jax.sharding import PartitionSpec as P

TILE = 128
PEERS_STEP = 8
EPS = 1e-05
BF16 = jnp.bfloat16
F32 = jnp.float32


def params(mib, axes=1):
    return pltpu.CompilerParams(
        dimension_semantics=("arbitrary",) * axes, vmem_limit_bytes=mib * 2**20
    )


def pick_kernel(idx_ref, own_ref, other_ref, out_ref, table):
    half = own_ref.shape[1]
    chunks = own_ref.shape[0] // TILE

    @pl.when(pl.program_id(0) == 0)
    def _():
        table[:, :half] = own_ref[...]
        table[:, half:] = other_ref[...]

    slots, peers = idx_ref.shape[1:]
    cols = idx_ref[0]
    lane = lax.broadcasted_iota(jnp.int32, (slots, TILE), 1)
    rows = []
    for p in range(peers):
        col = jnp.broadcast_to(cols[:, p : p + 1], (slots, TILE))
        low = jnp.where((col & (TILE - 1)) == lane, 1.0, 0.0).astype(BF16)
        high = (col >> 7).astype(F32).astype(BF16)
        zero = jnp.zeros_like(low)
        rows.append(
            jnp.concatenate(
                [jnp.where(high == jnp.asarray(c, BF16), low, zero) for c in range(chunks)],
                axis=1,
            )
        )
    hot = jnp.concatenate(rows, axis=0)
    picked = jnp.dot(hot, table[...], preferred_element_type=F32).astype(BF16)
    out_ref[...] = picked.reshape(out_ref.shape)


def pick_rows(idx, own, other):
    groups, slots, peers = idx.shape
    rows, half = own.shape
    return pl.pallas_call(
        pick_kernel,
        grid=(groups,),
        in_specs=[
            pl.BlockSpec((1, slots, peers), lambda g: (g, 0, 0)),
            pl.BlockSpec((rows, half), lambda g: (0, 0)),
            pl.BlockSpec((rows, half), lambda g: (0, 0)),
        ],
        out_specs=pl.BlockSpec((peers, slots, 2 * half), lambda g: (g, 0, 0)),
        out_shape=jax.ShapeDtypeStruct((groups * peers, slots, 2 * half), BF16),
        scratch_shapes=[pltpu.VMEM((rows, 2 * half), BF16)],
        compiler_params=params(40),
        name="pick_rows",
    )(idx, own, other)


def adjacency_kernel(core_ref, codes_ref, out_ref):
    per_tile, edges = codes_ref.shape[1:]
    ids = lax.broadcasted_iota(jnp.int32, (TILE, edges), 0).astype(F32).astype(BF16)
    one = jnp.ones((TILE, edges), BF16)
    zero = jnp.zeros((TILE, edges), BF16)

    def hot(values):
        spread = jnp.broadcast_to(values.astype(F32), (16, edges)).astype(BF16)
        spread = jnp.concatenate([spread] * (TILE // 16), axis=0)
        return jnp.where(spread == ids, one, zero)

    for k in range(per_tile):
        codes = codes_ref[0, k : k + 1, :]
        counts = lax.dot_general(
            hot(codes >> 7),
            hot(codes & (TILE - 1)),
            (((1,), (1,)), ((), ())),
            preferred_element_type=F32,
        )
        out_ref[0, :, k * TILE : (k + 1) * TILE] = counts.astype(BF16)


def adjacency(core, codes, tiles):
    _, per_tile, edges = codes.shape
    return pl.pallas_call(
        adjacency_kernel,
        grid_spec=pltpu.PrefetchScalarGridSpec(
            num_scalar_prefetch=1,
            grid=(tiles,),
            in_specs=[
                pl.BlockSpec(
                    (1, per_tile, edges), lambda t, core_ref: (core_ref[0] * tiles + t, 0, 0)
                )
            ],
            out_specs=pl.BlockSpec((1, TILE, per_tile * TILE), lambda t, core_ref: (t, 0, 0)),
        ),
        out_shape=jax.ShapeDtypeStruct((tiles, TILE, per_tile * TILE), BF16),
        compiler_params=params(40),
        cost_estimate=pl.CostEstimate(
            flops=2 * tiles * per_tile * TILE * TILE * edges * 2,
            transcendentals=0,
            bytes_accessed=tiles * per_tile * (TILE * TILE * 2 + edges * 4),
        ),
        name="adjacency",
    )(core, codes)


def aggregate_kernel(
    core_ref,
    tile_src_ref,
    adj_ref,
    deg_ref,
    weight_ref,
    own_ref,
    other_ref,
    mine_ref,
    sibling_ref,
    keep_ref,
    send_ref,
    sources,
    agg,
    sems,
):
    tiles, per_tile = tile_src_ref.shape
    tiles //= 2
    step = pl.program_id(0)
    core = core_ref[0]
    own_tiles = own_ref.shape[0]
    peers, slots, width = mine_ref.shape
    half = width // 2
    lo = pl.ds(0, half)
    hi = pl.ds(half, half)

    @pl.when(step == 0)
    def _():
        owned = pl.ds(0, own_tiles)
        halo = pl.ds(own_tiles, peers)
        here = pl.ds(pl.multiple_of(core * slots, slots), slots)
        there = pl.ds(pl.multiple_of((1 - core) * slots, slots), slots)
        copies = [
            pltpu.make_async_copy(own_ref, sources.at[owned, :, lo], sems.at[0]),
            pltpu.make_async_copy(other_ref, sources.at[owned, :, hi], sems.at[1]),
            pltpu.make_async_copy(mine_ref, sources.at[halo, here, :], sems.at[2]),
            pltpu.make_async_copy(
                sibling_ref.at[:, :, hi], sources.at[halo, there, lo], sems.at[3]
            ),
            pltpu.make_async_copy(
                sibling_ref.at[:, :, lo], sources.at[halo, there, hi], sems.at[4]
            ),
        ]
        for copy in copies:
            copy.start()
        for copy in copies:
            copy.wait()

    row = core * tiles + step
    total = jnp.zeros((TILE, width), F32)
    for k in range(0, per_tile, 2):
        pair = jnp.concatenate(
            [sources[tile_src_ref[row, k]], sources[tile_src_ref[row, k + 1]]], axis=0
        )
        total += jnp.dot(
            adj_ref[0, :, k * TILE : (k + 2) * TILE], pair, preferred_element_type=F32
        )
    degree = deg_ref[0].astype(F32)
    column = jnp.broadcast_to(degree, (8, TILE)).T[:, :1]
    mean_rows = (total / column).astype(BF16)
    both = jnp.concatenate([sources[row], mean_rows], axis=1)
    pre = jnp.dot(both, weight_ref[...], preferred_element_type=F32)
    keep_ref[...] = pre[:, :half]
    send_ref[...] = pre[:, half:]


def aggregate(core, tile_src, adj, degrees, weights, own, other, mine, sibling):
    tiles = adj.shape[0]
    width = mine.shape[2]
    half = width // 2
    rows = tiles * TILE
    source_tiles = own.shape[0] // TILE + mine.shape[0]
    own = own.reshape(-1, TILE, half)
    other = other.reshape(-1, TILE, half)
    anywhere = pl.BlockSpec(memory_space=pl.ANY)
    return pl.pallas_call(
        aggregate_kernel,
        grid_spec=pltpu.PrefetchScalarGridSpec(
            num_scalar_prefetch=2,
            grid=(tiles,),
            in_specs=[
                pl.BlockSpec((1,) + adj.shape[1:], lambda t, c, s: (t, 0, 0)),
                pl.BlockSpec((1, 1, TILE), lambda t, c, s: (c[0] * tiles + t, 0, 0)),
                pl.BlockSpec(weights.shape, lambda t, c, s: (0, 0)),
                anywhere,
                anywhere,
                anywhere,
                anywhere,
            ],
            out_specs=[pl.BlockSpec((TILE, half), lambda t, c, s: (t, 0))] * 2,
            scratch_shapes=[
                pltpu.VMEM((source_tiles, TILE, width), BF16),
                pltpu.VMEM((TILE, width), BF16),
                pltpu.SemaphoreType.DMA((5,)),
            ],
        ),
        out_shape=[jax.ShapeDtypeStruct((rows, half), F32)] * 2,
        compiler_params=params(40),
        name="aggregate",
    )(core, tile_src, adj, degrees, weights, own, other, mine, sibling)


def moments_kernel(keep_ref, got_ref, out_ref):
    count = keep_ref.shape[0] + got_ref.shape[0]
    keep = keep_ref[...]
    got = got_ref[...]
    total = jnp.sum(keep, axis=0, keepdims=True) + jnp.sum(got, axis=0, keepdims=True)
    mean = total / count
    spread = jnp.sum(jnp.square(keep - mean), axis=0, keepdims=True) + jnp.sum(
        jnp.square(got - mean), axis=0, keepdims=True
    )
    both = jnp.concatenate([total, spread], axis=0)
    out_ref[...] = jnp.broadcast_to(both[None], out_ref.shape)


def moments(keep, got, peers):
    return pl.pallas_call(
        moments_kernel,
        out_shape=jax.ShapeDtypeStruct((peers, 2, keep.shape[1]), F32),
        compiler_params=pltpu.CompilerParams(vmem_limit_bytes=40 * 2**20),
        name="moments",
    )(keep, got)


def normalise_kernel(core_ref, keep_ref, got_ref, parts_ref, gamma_ref, beta_ref, out_ref):
    rows = keep_ref.shape[0]
    count = float(2 * rows)
    parts = parts_ref[...]
    peers = parts.shape[0]
    totals = parts[:, 0, :]
    spreads = parts[:, 1, :]
    mean = jnp.sum(totals, axis=0, keepdims=True) / (count * peers)
    shift = totals / count - mean
    var = jnp.sum(spreads + count * shift * shift, axis=0, keepdims=True) / (count * peers)
    scale = gamma_ref[...] / jnp.sqrt(var + EPS)
    beta = beta_ref[...]
    here = pl.multiple_of(core_ref[0] * rows, rows)
    there = pl.multiple_of((1 - core_ref[0]) * rows, rows)
    out_ref[pl.ds(here, rows), :] = jnp.maximum(
        (keep_ref[...] - mean) * scale + beta, 0.0
    ).astype(BF16)
    out_ref[pl.ds(there, rows), :] = jnp.maximum(
        (got_ref[...] - mean) * scale + beta, 0.0
    ).astype(BF16)


def normalise(core, keep, got, parts, gamma, beta):
    rows, half = keep.shape
    whole = pl.BlockSpec(memory_space=pltpu.VMEM)
    return pl.pallas_call(
        normalise_kernel,
        in_specs=[pl.BlockSpec(memory_space=pltpu.SMEM)] + [whole] * 5,
        out_specs=whole,
        out_shape=jax.ShapeDtypeStruct((2 * rows, half), BF16),
        compiler_params=pltpu.CompilerParams(vmem_limit_bytes=40 * 2**20),
        name="normalise",
    )(core, keep, got, parts, gamma.reshape(1, half), beta.reshape(1, half))


def local(
    features, send_rows, send_counts, tile_src, edge_codes, degrees, w_self, w_neigh, gamma, beta
):
    rows, half = features.shape
    peers = lax.axis_size("dom")
    slots = send_rows.shape[2]
    tiles = rows // TILE // 2
    core = lax.axis_index("feat").astype(jnp.int32)
    core_arg = core.reshape(1)
    swap = [(0, 1), (1, 0)]

    other = lax.ppermute(features, "feat", swap)
    part = lax.dynamic_slice_in_dim(send_rows[0], core * (slots // 2), slots // 2, 1)
    slot_ids = jnp.arange(slots // 2, dtype=jnp.int32) + core * (slots // 2)
    idx = jnp.where(slot_ids[None, :] < send_counts[0][:, None], part, -1)
    idx = idx.reshape(peers // PEERS_STEP, PEERS_STEP, slots // 2).transpose(0, 2, 1)
    outgoing = pick_rows(idx, features, other)
    mine = lax.all_to_all(outgoing, "dom", split_axis=0, concat_axis=0, tiled=True)
    adj = adjacency(core_arg, edge_codes, tiles)
    sibling = lax.ppermute(mine, "feat", swap)

    def turned(w):
        return jnp.where(core == 0, w, jnp.roll(w, (half, half), (0, 1)))

    weights = jnp.concatenate([turned(w_self), turned(w_neigh)], axis=0)
    keep, send = aggregate(
        core_arg,
        tile_src,
        adj,
        degrees.reshape(-1, 1, TILE),
        weights,
        features,
        other,
        mine,
        sibling,
    )
    got = lax.ppermute(send, "feat", swap)
    parts = lax.all_to_all(
        moments(keep, got, peers), "dom", split_axis=0, concat_axis=0, tiled=True
    )
    return normalise(core_arg, keep, got, parts, gamma, beta)


def solution(mesh):
    return jax.shard_map(
        local,
        mesh=mesh,
        in_specs=(
            P("dom", "feat"),
            P("dom", None, None),
            P("dom", None),
            P("dom", None),
            P("dom", None, None),
            P("dom"),
            P(),
            P(),
            P("feat"),
            P("feat"),
        ),
        out_specs=P("dom", "feat"),
        check_vma=False,
    )
```

time: 803 us -> 117 us (0.15)
  blocking collectives: 351 us -> 56.4 us
  matrix products: 288 us -> 0 us
  local copies, waits for them, and re-layouts: 62.6 us -> 6.98 us
  Pallas kernels: 0 us -> 46.6 us
  waiting for transfers between devices: 40.7 us -> 2.92 us
  other arithmetic: 34.1 us -> 2.53 us
  between operations: 13.5 us -> 0.17 us
  starting transfers between devices: 11.7 us -> 0.53 us
    psum x2 -> x0, blocking collectives: 351 us -> none  [the longest x1 179 us: local(): column_sum = lax.psum(jnp.sum(pre, axis=0), 'dom')]
    dot_general x18 -> x0, matrix products: 288 us -> none  [the longest x8 248 us: one_group(): jnp.einsum('gkei,gkej->gkij', dest_hot, source_hot, preferred_element_typ...]
    gather x9 -> x0, local copies, waits for them, and re-layouts: 60.4 us -> none  [the longest x8 37.1 us: one_group(): gathered = sources[indices]]
    all_to_all x0 -> x2, blocking collectives: none -> 56.4 us  [the longest x1 41.3 us: local(): lax.all_to_all(outgoing, 'dom', split_axis=0, concat_axis=0, tiled=True)]
    pallas_call x0 -> x5, Pallas kernels: none -> 46.6 us  [the longest x1 17.8 us: aggregate(): pl.pallas_call(aggregate_kernel, grid_spec=pltpu.PrefetchScalarGridSpec(n...]
    all_to_all x1 -> x0, waiting for transfers between devices: 29.4 us -> none  [local(): lax.all_to_all(outgoing, 'dom', split_axis=0, concat_axis=0, tiled=True)]
    select_n x26 -> x1, other arithmetic: 20.1 us -> 1.08 us  [turned(): return jnp.where(core == 0, w, jnp.roll(w, (half, half), (0, 1)))]
    all_to_all x1 -> x0, starting transfers between devices: 11.6 us -> none  [local(): lax.all_to_all(outgoing, 'dom', split_axis=0, concat_axis=0, tiled=True)]
  transfers between devices with their start and end apart: 2 -> 3, of which waited for: 2 -> 2; matrix products, arithmetic and copies ran while one was open for 0% -> 3% of each run, Pallas kernels for 0% -> 14%
where the time goes in v1:
time: 117 us; the launch traced here: 116 us
  blocking collectives  56.4 us (48%)
  Pallas kernels  46.6 us (40%)
  local copies, waits for them, and re-layouts  6.98 us (6%)
  waiting for transfers between devices  2.92 us (2%)
  other arithmetic  2.53 us (2%)
    all_to_all x1, blocking collectives, local(): lax.all_to_all(outgoing, 'dom', split_axis=0, concat_axis=0, tiled=True)  41.3 us
    pallas_call x1, Pallas kernels, aggregate(): pl.pallas_call(aggregate_kernel, grid_spec=pltpu.PrefetchScalarGridSpec(n...  17.8 us
    pallas_call x1, Pallas kernels, adjacency(): pl.pallas_call(adjacency_kernel, grid_spec=pltpu.PrefetchScalarGridSpec(n...  16 us
    all_to_all x1, blocking collectives, local(): lax.all_to_all(moments(keep, got, peers), 'dom', split_axis=0, concat_axi...  15 us
    pallas_call x1, Pallas kernels, pick_rows(): pl.pallas_call(pick_kernel, grid=(groups,), in_specs=[pl.BlockSpec((1, sl...  10.8 us
    unnamed x24, local copies, waits for them, and re-layouts  6.68 us
  transfers between devices with their start and end apart: 3, of which 2 were waited for; matrix products, arithmetic and copies ran while one was open for 3% of the time, Pallas kernels for 14%

profile of v1, /device:TPU:0, one launch (start us, length us, event | category | flops | bytes accessed | tf_op | source)
XLA Modules:
  0.0 116.1 jit_solution(11658437961532904766)
XLA Ops:
  0.0 0.0 copy-start
  0.0 0.0 collective-permute-start
  0.0 0.5 broadcast.14
  0.5 1.3 %reduce.3 = s32[64]{0:T(128)S(1)} reduce(s32[1,64]{1,0:T(1,128)} %param.12, s32[]{:T(128)} %broadcast.14), dimensions={0}, to_apply=%param.12.reduce_sub_computation.3 | reduce | bytes 516 | tf_op args[2]
  1.8 0.1 lt.20
  1.9 0.0 copy-done
  1.9 0.1 dynamic-slice_bitcast_fusion
  2.0 0.1 copy.12
  2.1 0.1 select_bitcast_fusion.idx_ref
  2.2 0.6 collective-permute-done.other_ref
  2.9 0.0 copy-start.2
  2.9 1.2 %copy-done.2 = bf16[4096,128]{1,0:T(8,128)(2,1)S(1)} copy-done((bf16[4096,128]{1,0:T(8,128)(2,1)S(1)}, bf16[4096,128]{1,0:T(8,128)(2,1)}, u32[]{:S(2)}) %copy-start.2) | copy-done | bytes 1048600
  4.1 10.8 %pick_rows.1 = bf16[64,64,256]{2,1,0:T(8,128)(2,1)S(1)} custom-call(s32[8,64,8]{2,1,0:T(8,128)S(1)} %select_bitcast_fusion.idx_ref, bf16[4096,128]{1,0:T(8,128)(2,1)S(1)} %copy-done.2, bf16[4096,128]{1,0:T(8,128)(2,1)S(1)} %collective-permute-done.other_ref), custom_call_target="tpu_custom_call" | custom-call | tf_op jit(solution)/shard_map/pick_rows/pallas_call | solution.py:53
  14.9 0.0 copy-start.9
  14.9 0.0 copy-start.10
  14.9 0.0 copy-start.8
  14.9 41.3 %all_to_all.10.mine_ref = bf16[64,64,256]{2,1,0:T(8,128)(2,1)S(1)} all-to-all(bf16[64,64,256]{2,1,0:T(8,128)(2,1)S(1)} %pick_rows.1), channel_id=1, replica_groups=mesh['dom'=64,'feat'=2] {'dom'}, dimensions={0} | all-to-all | bytes 4194304 | tf_op jit(solution)/shard_map/all_to_all | solution.py:292
  56.3 0.0 collective-permute-start.1
  56.3 0.0 copy-done.9
  56.3 0.0 copy-done.10
  56.3 0.1 copy.13.tile_src_ref
  56.4 0.0 copy-start.7
  56.4 0.0 copy-done.8
  56.4 1.1 fusion.1
  57.5 0.3 copy-done.7
  57.8 0.0 copy-start.3
  57.8 0.0 copy-start.4
  57.8 16.0 %adjacency.1.adj_ref = bf16[16,128,3072]{2,1,0:T(8,128)(2,1)S(1)} custom-call(s32[1]{0:T(128)} %bitcast.core_ref, s32[32,24,512]{2,1,0:T(8,128)S(1)} %copy-done.7), custom_call_target="tpu_custom_call" | custom-call | flops 12884901888 | bytes 13369344 | tf_op jit(solution)/shard_map/adjacency/pallas_call | solution.py:93
  73.8 0.0 copy-start.1
  73.8 4.5 %copy-done.1 = bf16[16,128,3072]{2,1,0:T(8,128)(2,1)} copy-done((bf16[16,128,3072]{2,1,0:T(8,128)(2,1)}, bf16[16,128,3072]{2,1,0:T(8,128)(2,1)S(1)}, u32[]{:S(2)}) %copy-start.1) | copy-done | bytes 12582936
  78.3 0.0 collective-permute-done.1.sibling_ref
  78.3 0.0 copy-done.3
  78.4 0.0 copy-done.4
  78.4 17.8 %aggregate.1 = (f32[2048,128]{1,0:T(8,128)S(1)}, f32[2048,128]{1,0:T(8,128)S(1)}) custom-call(s32[1]{0:T(128)} %bitcast.core_ref, s32[32,24]{1,0:T(8,128)S(1)} %copy.13.tile_src_ref, bf16[16,128,3072]{2,1,0:T(8,128)(2,1)} %copy-done.1, s32[32,1,128]{2,1,0:T(1,128)S(1)} %bitcast.12, bf16[512,256]{1,0:T(8,128)(2,1)S(1)} %pad_maximum_fusion.weight_ref, ...), custom_call_target="tpu_custom_call" | custom-call | tf_op jit(solution)/shard_map/aggregate/pallas_call | solution.py:191
  96.2 0.0 copy-start.5
  96.2 0.0 copy-start.6
  96.2 0.5 collective-permute-start.2
  96.7 2.3 %collective-permute-done.2.got_ref = f32[2048,128]{1,0:T(8,128)S(1)} collective-permute-done((f32[2048,128]{1,0:T(8,128)S(1)}, f32[2048,128]{1,0:T(8,128)S(1)}, u32[]{:S(2)}, u32[]{:S(2)}) %collective-permute-start.2) | collective-permute-done | bytes 1048608 | tf_op jit(solution)/shard_map/ppermute | solution.py:311
  99.0 0.6 moments.1
  99.7 15.0 %all_to_all.11.parts_ref = f32[64,2,128]{2,1,0:T(2,128)S(1)} all-to-all(f32[64,2,128]{2,1,0:T(2,128)S(1)} %moments.1), channel_id=1, replica_groups=mesh['dom'=64,'feat'=2] {'dom'}, dimensions={0} | all-to-all | bytes 131072 | tf_op jit(solution)/shard_map/all_to_all | solution.py:312
  114.7 0.0 copy-done.5
  114.7 0.0 copy-done.6
  114.7 1.4 %normalise.1 = bf16[4096,128]{1,0:T(8,128)(2,1)} custom-call(s32[1]{0:T(128)} %bitcast.core_ref, f32[2048,128]{1,0:T(8,128)S(1)} %get-tuple-element.7.keep_ref, f32[2048,128]{1,0:T(8,128)S(1)} %collective-permute-done.2.got_ref, f32[64,2,128]{2,1,0:T(2,128)S(1)} %all_to_all.11.parts_ref, f32[1,128]{1,0:T(1,128)S(1)} %bitcast.13, f32[1,128]{1,0:T(1,128)S(1)} %bitcast.14), custom_call_target="tpu_custom_call" | custom-call | tf_op jit(solution)/shard_map/normalise/pallas_call | solution.py:265
  (6 shorter events, 0.1 us)
Async XLA Ops:
  0.0 1.9 %copy-start = (s32[1,64,128]{2,1,0:T(8,128)S(1)}, s32[1,64,128]{2,1,0:T(8,128)}, u32[]{:S(2)}) copy-start(s32[1,64,128]{2,1,0:T(8,128)} %param.11) | copy-start | bytes 98308
  0.0 2.9 %collective-permute-start = (bf16[4096,128]{1,0:T(8,128)(2,1)}, bf16[4096,128]{1,0:T(8,128)(2,1)S(1)}, u32[]{:S(2)}, u32[]{:S(2)}) collective-permute-start(bf16[4096,128]{1,0:T(8,128)(2,1)} %own_ref.1), channel_id=1, source_target_pairs={{0,1},{1,0},{2,3},{3,2},{4,5},{5,4},{6,7},{7,6},{8,9},{9,8},{10,11... | collective-permute-start | bytes 3145736 | tf_op jit(solution)/shard_map/ppermute | solution.py:286
  2.9 1.2 %copy-start.2 = (bf16[4096,128]{1,0:T(8,128)(2,1)S(1)}, bf16[4096,128]{1,0:T(8,128)(2,1)}, u32[]{:S(2)}) copy-start(bf16[4096,128]{1,0:T(8,128)(2,1)} %own_ref.1) | copy-start | bytes 3145732
  14.9 41.4 %copy-start.9 = (bf16[256,256]{1,0:T(8,128)(2,1)S(1)}, bf16[256,256]{1,0:T(8,128)(2,1)}, u32[]{:S(2)}) copy-start(bf16[256,256]{1,0:T(8,128)(2,1)} %param.16) | copy-start | bytes 393220
  14.9 41.4 %copy-start.10 = (s32[32,24]{0,1:T(8,128)S(1)}, s32[32,24]{0,1:T(8,128)}, u32[]{:S(2)}) copy-start(s32[32,24]{0,1:T(8,128)} %param.13) | copy-start | bytes 9220
  14.9 41.5 %copy-start.8 = (bf16[256,256]{1,0:T(8,128)(2,1)S(1)}, bf16[256,256]{1,0:T(8,128)(2,1)}, u32[]{:S(2)}) copy-start(bf16[256,256]{1,0:T(8,128)(2,1)} %param.17) | copy-start | bytes 393220
  56.3 22.1 %collective-permute-start.1 = (bf16[64,64,256]{2,1,0:T(8,128)(2,1)S(1)}, bf16[64,64,256]{2,1,0:T(8,128)(2,1)}, u32[]{:S(2)}, u32[]{:S(2)}) collective-permute-start(bf16[64,64,256]{2,1,0:T(8,128)(2,1)S(1)} %all_to_all.10.mine_ref), channel_id=1, source_target_pairs={{0,1},{1,0},{2,3},{3,2},{4,5},{5,4},{6,7},{7,6},{8,9},{9,8},{10,11... | collective-permute-start | bytes 6291464 | tf_op jit(solution)/shard_map/ppermute | solution.py:294
  56.4 1.5 %copy-start.7 = (s32[32,24,512]{2,1,0:T(8,128)S(1)}, s32[32,24,512]{2,1,0:T(8,128)}, u32[]{:S(2)}) copy-start(s32[32,24,512]{2,1,0:T(8,128)} %codes_ref.1) | copy-start | bytes 4718596
  57.8 20.5 %copy-start.3 = (bf16[4096,128]{1,0:T(8,128)(2,1)S(1)}, bf16[4096,128]{1,0:T(8,128)(2,1)}, u32[]{:S(2)}) copy-start(bf16[4096,128]{1,0:T(8,128)(2,1)} %own_ref.1) | copy-start | bytes 3145732
  57.8 20.5 %copy-start.4 = (s32[4096]{0:T(1024)S(1)}, s32[4096]{0:T(1024)}, u32[]{:S(2)}) copy-start(s32[4096]{0:T(1024)} %param.15) | copy-start | bytes 49156
  73.8 4.5 %copy-start.1 = (bf16[16,128,3072]{2,1,0:T(8,128)(2,1)}, bf16[16,128,3072]{2,1,0:T(8,128)(2,1)S(1)}, u32[]{:S(2)}) copy-start(bf16[16,128,3072]{2,1,0:T(8,128)(2,1)S(1)} %adjacency.1.adj_ref) | copy-start | bytes 37748740
  96.2 18.5 %copy-start.5 = (f32[128]{0:T(128)S(1)}, f32[128]{0:T(128)}, u32[]{:S(2)}) copy-start(f32[128]{0:T(128)} %param.18) | copy-start | bytes 1540
  96.2 18.5 %copy-start.6 = (f32[128]{0:T(128)S(1)}, f32[128]{0:T(128)}, u32[]{:S(2)}) copy-start(f32[128]{0:T(128)} %param.19) | copy-start | bytes 1540
  96.2 2.8 %collective-permute-start.2 = (f32[2048,128]{1,0:T(8,128)S(1)}, f32[2048,128]{1,0:T(8,128)S(1)}, u32[]{:S(2)}, u32[]{:S(2)}) collective-permute-start(f32[2048,128]{1,0:T(8,128)S(1)} %get-tuple-element.8), channel_id=1, source_target_pairs={{0,1},{1,0},{2,3},{3,2},{4,5},{5,4},{6,7},{7,6},{8,9},{9,8},{10,11... | collective-permute-start | bytes 3145736 | tf_op jit(solution)/shard_map/ppermute | solution.py:311

commit v2 on v1

--- a/solution.py
+++ b/solution.py
@@ -44,7 +44,9 @@
         )
     hot = jnp.concatenate(rows, axis=0)
     picked = jnp.dot(hot, table[...], preferred_element_type=F32).astype(BF16)
-    out_ref[...] = picked.reshape(out_ref.shape)
+    picked = picked.reshape(peers, slots, 2 * half)
+    out_ref[:, :slots, :] = picked[:, :, :half]
+    out_ref[:, slots:, :] = picked[:, :, half:]
 
 
 def pick_rows(idx, own, other):
@@ -58,8 +60,8 @@
             pl.BlockSpec((rows, half), lambda g: (0, 0)),
             pl.BlockSpec((rows, half), lambda g: (0, 0)),
         ],
-        out_specs=pl.BlockSpec((peers, slots, 2 * half), lambda g: (g, 0, 0)),
-        out_shape=jax.ShapeDtypeStruct((groups * peers, slots, 2 * half), BF16),
+        out_specs=pl.BlockSpec((peers, 2 * slots, half), lambda g: (g, 0, 0)),
+        out_shape=pltpu.HBM((groups * peers, 2 * slots, half), BF16),
         scratch_shapes=[pltpu.VMEM((rows, 2 * half), BF16)],
         compiler_params=params(40),
         name="pick_rows",
@@ -126,7 +128,6 @@
     keep_ref,
     send_ref,
     sources,
-    agg,
     sems,
 ):
     tiles, per_tile = tile_src_ref.shape
@@ -134,8 +135,9 @@
     step = pl.program_id(0)
     core = core_ref[0]
     own_tiles = own_ref.shape[0]
-    peers, slots, width = mine_ref.shape
-    half = width // 2
+    peers, slots, half = mine_ref.shape
+    slots //= 2
+    width = 2 * half
     lo = pl.ds(0, half)
     hi = pl.ds(half, half)
 
@@ -143,17 +145,24 @@
     def _():
         owned = pl.ds(0, own_tiles)
         halo = pl.ds(own_tiles, peers)
+        first = pl.ds(0, slots)
+        second = pl.ds(slots, slots)
         here = pl.ds(pl.multiple_of(core * slots, slots), slots)
         there = pl.ds(pl.multiple_of((1 - core) * slots, slots), slots)
         copies = [
             pltpu.make_async_copy(own_ref, sources.at[owned, :, lo], sems.at[0]),
             pltpu.make_async_copy(other_ref, sources.at[owned, :, hi], sems.at[1]),
-            pltpu.make_async_copy(mine_ref, sources.at[halo, here, :], sems.at[2]),
             pltpu.make_async_copy(
-                sibling_ref.at[:, :, hi], sources.at[halo, there, lo], sems.at[3]
+                mine_ref.at[:, first, :], sources.at[halo, here, lo], sems.at[2]
             ),
             pltpu.make_async_copy(
-                sibling_ref.at[:, :, lo], sources.at[halo, there, hi], sems.at[4]
+                mine_ref.at[:, second, :], sources.at[halo, here, hi], sems.at[3]
+            ),
+            pltpu.make_async_copy(
+                sibling_ref.at[:, second, :], sources.at[halo, there, lo], sems.at[4]
+            ),
+            pltpu.make_async_copy(
+                sibling_ref.at[:, first, :], sources.at[halo, there, hi], sems.at[5]
             ),
         ]
         for copy in copies:
@@ -181,8 +190,8 @@
 
 def aggregate(core, tile_src, adj, degrees, weights, own, other, mine, sibling):
     tiles = adj.shape[0]
-    width = mine.shape[2]
-    half = width // 2
+    half = mine.shape[2]
+    width = 2 * half
     rows = tiles * TILE
     source_tiles = own.shape[0] // TILE + mine.shape[0]
     own = own.reshape(-1, TILE, half)
@@ -205,8 +214,7 @@
             out_specs=[pl.BlockSpec((TILE, half), lambda t, c, s: (t, 0))] * 2,
             scratch_shapes=[
                 pltpu.VMEM((source_tiles, TILE, width), BF16),
-                pltpu.VMEM((TILE, width), BF16),
-                pltpu.SemaphoreType.DMA((5,)),
+                pltpu.SemaphoreType.DMA((6,)),
             ],
         ),
         out_shape=[jax.ShapeDtypeStruct((rows, half), F32)] * 2,
@@ -291,6 +299,7 @@
     outgoing = pick_rows(idx, features, other)
     mine = lax.all_to_all(outgoing, "dom", split_axis=0, concat_axis=0, tiled=True)
     adj = adjacency(core_arg, edge_codes, tiles)
+    mine, adj = lax.optimization_barrier((mine, adj))
     sibling = lax.ppermute(mine, "feat", swap)
 
     def turned(w):

time: 117 us -> 99.8 us (0.85)
  blocking collectives: 56.4 us -> 15 us
  waiting for transfers between devices: 2.92 us -> 15.1 us
  starting transfers between devices: 0.53 us -> 11.7 us
    all_to_all x1 -> x0, blocking collectives: 41.3 us -> none  [local(): lax.all_to_all(outgoing, 'dom', split_axis=0, concat_axis=0, tiled=True)]
    all_to_all x0 -> x1, starting transfers between devices: none -> 11.5 us  [local(): lax.all_to_all(outgoing, 'dom', split_axis=0, concat_axis=0, tiled=True)]
    all_to_all x0 -> x1, waiting for transfers between devices: none -> 7.94 us  [local(): lax.all_to_all(outgoing, 'dom', split_axis=0, concat_axis=0, tiled=True)]
    ppermute x1, waiting for transfers between devices: 0.01 us -> 4.03 us  [local(): sibling = lax.ppermute(mine, 'feat', swap)]
    unnamed x24 -> x28, local copies, waits for them, and re-layouts: 6.68 us -> 7.77 us
  transfers between devices with their start and end apart: 3 -> 4, of which waited for: 2 -> 4; matrix products, arithmetic and copies ran while one was open for 3% -> 2% of each run, Pallas kernels for 14% -> 16%
where the time goes in v2:
time: 99.8 us; the launch traced here: 99.1 us
  Pallas kernels  47.5 us (48%)
  waiting for transfers between devices  15.1 us (15%)
  blocking collectives  15 us (15%)
  starting transfers between devices  11.7 us (12%)
  local copies, waits for them, and re-layouts  8.08 us (8%)
  other arithmetic  1.51 us (2%)
    pallas_call x1, Pallas kernels, aggregate(): pl.pallas_call(aggregate_kernel, grid_spec=pltpu.PrefetchScalarGridSpec(n...  17.9 us
    pallas_call x1, Pallas kernels, adjacency(): pl.pallas_call(adjacency_kernel, grid_spec=pltpu.PrefetchScalarGridSpec(n...  16 us
    all_to_all x1, blocking collectives, local(): lax.all_to_all(moments(keep, got, peers), 'dom', split_axis=0, concat_axi...  15 us
    all_to_all x1, starting transfers between devices, local(): lax.all_to_all(outgoing, 'dom', split_axis=0, concat_axis=0, tiled=True)  11.5 us
    pallas_call x1, Pallas kernels, pick_rows(): pl.pallas_call(pick_kernel, grid=(groups,), in_specs=[pl.BlockSpec((1, sl...  11.5 us
    all_to_all x1, waiting for transfers between devices, local(): lax.all_to_all(outgoing, 'dom', split_axis=0, concat_axis=0, tiled=True)  7.94 us
    unnamed x28, local copies, waits for them, and re-layouts  7.77 us
    ppermute x1, waiting for transfers between devices, local(): sibling = lax.ppermute(mine, 'feat', swap)  4.03 us
  transfers between devices with their start and end apart: 4, of which 4 were waited for; matrix products, arithmetic and copies ran while one was open for 2% of the time, Pallas kernels for 16%

profile of v2, /device:TPU:0, one launch (start us, length us, event | category | flops | bytes accessed | tf_op | source)
XLA Modules:
  0.0 99.1 jit_solution(78917043517473262)
XLA Ops:
  0.0 0.0 copy-start
  0.0 0.0 collective-permute-start
  0.0 0.5 broadcast.14
  0.5 1.3 %reduce.3 = s32[64]{0:T(128)S(1)} reduce(s32[1,64]{1,0:T(1,128)} %param.12, s32[]{:T(128)} %broadcast.14), dimensions={0}, to_apply=%param.12.reduce_sub_computation.3 | reduce | bytes 516 | tf_op args[2]
  1.8 0.1 lt.20
  1.9 0.0 copy-done
  1.9 0.1 dynamic-slice_bitcast_fusion
  2.0 0.1 copy.12
  2.1 0.1 select_bitcast_fusion.idx_ref
  2.2 0.6 collective-permute-done.other_ref
  2.9 0.0 copy-start.2
  2.9 1.2 %copy-done.2 = bf16[4096,128]{1,0:T(8,128)(2,1)S(1)} copy-done((bf16[4096,128]{1,0:T(8,128)(2,1)S(1)}, bf16[4096,128]{1,0:T(8,128)(2,1)}, u32[]{:S(2)}) %copy-start.2) | copy-done | bytes 1048600
  4.1 0.0 copy-start.4
  4.1 11.5 %pick_rows.1 = bf16[64,128,128]{2,1,0:T(8,128)(2,1)} custom-call(s32[8,64,8]{2,1,0:T(8,128)S(1)} %select_bitcast_fusion.idx_ref, bf16[4096,128]{1,0:T(8,128)(2,1)S(1)} %copy-done.2, bf16[4096,128]{1,0:T(8,128)(2,1)S(1)} %collective-permute-done.other_ref), custom_call_target="tpu_custom_call" | custom-call | tf_op jit(solution)/shard_map/pick_rows/pallas_call | solution.py:55
  15.6 0.0 copy-done.4
  15.6 11.5 %all-to-all-start = ((bf16[64,128,128]{2,1,0:T(8,128)(2,1)}), bf16[64,128,128]{2,1,0:T(8,128)(2,1)S(1)}, u32[]{:S(2)}, u32[]{:S(2)}) async-start(bf16[64,128,128]{2,1,0:T(8,128)(2,1)} %pick_rows.1), calls=%async_computation | async-start | bytes 4194304 | tf_op jit(solution)/shard_map/all_to_all | solution.py:300
  27.1 0.0 copy-start.9
  27.2 1.4 %copy-done.9 = s32[32,24,512]{2,1,0:T(8,128)S(1)} copy-done((s32[32,24,512]{2,1,0:T(8,128)S(1)}, s32[32,24,512]{2,1,0:T(8,128)}, u32[]{:S(2)}) %copy-start.9) | copy-done | bytes 1572888
  28.6 0.0 copy-start.12
  28.6 0.0 copy-start.11
  28.6 0.0 copy-start.10
  28.6 16.0 %adjacency.1.adj_ref = bf16[16,128,3072]{2,1,0:T(8,128)(2,1)S(1)} custom-call(s32[1]{0:T(128)} %bitcast.core_ref, s32[32,24,512]{2,1,0:T(8,128)S(1)} %copy-done.9), custom_call_target="tpu_custom_call" | custom-call | flops 12884901888 | bytes 13369344 | tf_op jit(solution)/shard_map/adjacency/pallas_call | solution.py:95
  44.5 0.0 copy-start.1
  44.5 4.5 %copy-done.1 = bf16[16,128,3072]{2,1,0:T(8,128)(2,1)} copy-done((bf16[16,128,3072]{2,1,0:T(8,128)(2,1)}, bf16[16,128,3072]{2,1,0:T(8,128)(2,1)S(1)}, u32[]{:S(2)}) %copy-start.1) | copy-done | bytes 12582936
  49.1 0.0 copy-start.3
  49.1 0.0 copy-start.6
  49.1 7.9 %all-to-all-done.mine_ref = bf16[64,128,128]{2,1,0:T(8,128)(2,1)S(1)} async-done(((bf16[64,128,128]{2,1,0:T(8,128)(2,1)}), bf16[64,128,128]{2,1,0:T(8,128)(2,1)S(1)}, u32[]{:S(2)}, u32[]{:S(2)}) %all-to-all-start) | async-done | bytes 2097184 | tf_op jit(solution)/shard_map/all_to_all | solution.py:300
  57.0 0.0 collective-permute-start.1
  57.0 0.0 copy-done.12
  57.0 0.1 copy.13.tile_src_ref
  57.1 0.0 copy-done.11
  57.1 0.0 copy-start.5
  57.1 0.0 copy-done.10
  57.2 0.1 fusion.1
  57.3 4.0 %collective-permute-done.1.sibling_ref = bf16[64,128,128]{2,1,0:T(8,128)(2,1)} collective-permute-done((bf16[64,128,128]{2,1,0:T(8,128)(2,1)S(1)}, bf16[64,128,128]{2,1,0:T(8,128)(2,1)}, u32[]{:S(2)}, u32[]{:S(2)}) %collective-permute-start.1) | collective-permute-done | bytes 2097184 | tf_op jit(solution)/shard_map/ppermute | solution.py:303
  61.3 0.0 copy-done.3
  61.3 0.0 copy-done.6
  61.3 0.0 copy-done.5
  61.3 17.9 %aggregate.1 = (f32[2048,128]{1,0:T(8,128)S(1)}, f32[2048,128]{1,0:T(8,128)S(1)}) custom-call(s32[1]{0:T(128)} %bitcast.core_ref, s32[32,24]{1,0:T(8,128)S(1)} %copy.13.tile_src_ref, bf16[16,128,3072]{2,1,0:T(8,128)(2,1)} %copy-done.1, s32[32,1,128]{2,1,0:T(1,128)S(1)} %bitcast.12, bf16[512,256]{1,0:T(8,128)(2,1)S(1)} %pad_maximum_fusion.weight_ref, ...), custom_call_target="tpu_custom_call" | custom-call | tf_op jit(solution)/shard_map/aggregate/pallas_call | solution.py:200
  79.3 0.0 copy-start.7
  79.3 0.0 copy-start.8
  79.3 0.2 collective-permute-start.2
  79.5 2.5 %collective-permute-done.2.got_ref = f32[2048,128]{1,0:T(8,128)S(1)} collective-permute-done((f32[2048,128]{1,0:T(8,128)S(1)}, f32[2048,128]{1,0:T(8,128)S(1)}, u32[]{:S(2)}, u32[]{:S(2)}) %collective-permute-start.2) | collective-permute-done | bytes 1048608 | tf_op jit(solution)/shard_map/ppermute | solution.py:320
  82.0 0.6 moments.1
  82.6 15.0 %all_to_all.10.parts_ref = f32[64,2,128]{2,1,0:T(2,128)S(1)} all-to-all(f32[64,2,128]{2,1,0:T(2,128)S(1)} %moments.1), channel_id=1, replica_groups=mesh['dom'=64,'feat'=2] {'dom'}, dimensions={0} | all-to-all | bytes 131072 | tf_op jit(solution)/shard_map/all_to_all | solution.py:321
  97.7 0.0 copy-done.7
  97.7 0.0 copy-done.8
  97.7 1.4 %normalise.1 = bf16[4096,128]{1,0:T(8,128)(2,1)} custom-call(s32[1]{0:T(128)} %bitcast.core_ref, f32[2048,128]{1,0:T(8,128)S(1)} %get-tuple-element.11.keep_ref, f32[2048,128]{1,0:T(8,128)S(1)} %collective-permute-done.2.got_ref, f32[64,2,128]{2,1,0:T(2,128)S(1)} %all_to_all.10.parts_ref, f32[1,128]{1,0:T(1,128)S(1)} %bitcast.13, f32[1,128]{1,0:T(1,128)S(1)} %bitcast.14), custom_call_target="tpu_custom_call" | custom-call | tf_op jit(solution)/shard_map/normalise/pallas_call | solution.py:273
  (6 shorter events, 0.1 us)
Async XLA Ops:
  0.0 1.9 %copy-start = (s32[1,64,128]{2,1,0:T(8,128)S(1)}, s32[1,64,128]{2,1,0:T(8,128)}, u32[]{:S(2)}) copy-start(s32[1,64,128]{2,1,0:T(8,128)} %param.11) | copy-start | bytes 98308
  0.0 2.9 %collective-permute-start = (bf16[4096,128]{1,0:T(8,128)(2,1)}, bf16[4096,128]{1,0:T(8,128)(2,1)S(1)}, u32[]{:S(2)}, u32[]{:S(2)}) collective-permute-start(bf16[4096,128]{1,0:T(8,128)(2,1)} %own_ref.1), channel_id=1, source_target_pairs={{0,1},{1,0},{2,3},{3,2},{4,5},{5,4},{6,7},{7,6},{8,9},{9,8},{10,11... | collective-permute-start | bytes 3145736 | tf_op jit(solution)/shard_map/ppermute | solution.py:294
  2.9 1.2 %copy-start.2 = (bf16[4096,128]{1,0:T(8,128)(2,1)S(1)}, bf16[4096,128]{1,0:T(8,128)(2,1)}, u32[]{:S(2)}) copy-start(bf16[4096,128]{1,0:T(8,128)(2,1)} %own_ref.1) | copy-start | bytes 3145732
  4.1 11.5 %copy-start.4 = (bf16[4096,128]{1,0:T(8,128)(2,1)}, bf16[4096,128]{1,0:T(8,128)(2,1)S(1)}, u32[]{:S(2)}) copy-start(bf16[4096,128]{1,0:T(8,128)(2,1)S(1)} %collective-permute-done.other_ref) | copy-start | bytes 3145732
  15.6 41.4 %all-to-all-start = ((bf16[64,128,128]{2,1,0:T(8,128)(2,1)}), bf16[64,128,128]{2,1,0:T(8,128)(2,1)S(1)}, u32[]{:S(2)}, u32[]{:S(2)}) async-start(bf16[64,128,128]{2,1,0:T(8,128)(2,1)} %pick_rows.1), calls=%async_computation | async-start | bytes 4194304 | tf_op jit(solution)/shard_map/all_to_all | solution.py:300
  27.1 1.4 %copy-start.9 = (s32[32,24,512]{2,1,0:T(8,128)S(1)}, s32[32,24,512]{2,1,0:T(8,128)}, u32[]{:S(2)}) copy-start(s32[32,24,512]{2,1,0:T(8,128)} %codes_ref.1) | copy-start | bytes 4718596
  28.6 28.5 %copy-start.12 = (s32[32,24]{0,1:T(8,128)S(1)}, s32[32,24]{0,1:T(8,128)}, u32[]{:S(2)}) copy-start(s32[32,24]{0,1:T(8,128)} %param.13) | copy-start | bytes 9220
  28.6 28.5 %copy-start.11 = (bf16[256,256]{1,0:T(8,128)(2,1)S(1)}, bf16[256,256]{1,0:T(8,128)(2,1)}, u32[]{:S(2)}) copy-start(bf16[256,256]{1,0:T(8,128)(2,1)} %param.16) | copy-start | bytes 393220
  28.6 28.6 %copy-start.10 = (bf16[256,256]{1,0:T(8,128)(2,1)S(1)}, bf16[256,256]{1,0:T(8,128)(2,1)}, u32[]{:S(2)}) copy-start(bf16[256,256]{1,0:T(8,128)(2,1)} %param.17) | copy-start | bytes 393220
  44.5 4.5 %copy-start.1 = (bf16[16,128,3072]{2,1,0:T(8,128)(2,1)}, bf16[16,128,3072]{2,1,0:T(8,128)(2,1)S(1)}, u32[]{:S(2)}) copy-start(bf16[16,128,3072]{2,1,0:T(8,128)(2,1)S(1)} %adjacency.1.adj_ref) | copy-start | bytes 37748740
  49.1 12.2 %copy-start.3 = (bf16[4096,128]{1,0:T(8,128)(2,1)S(1)}, bf16[4096,128]{1,0:T(8,128)(2,1)}, u32[]{:S(2)}) copy-start(bf16[4096,128]{1,0:T(8,128)(2,1)} %own_ref.1) | copy-start | bytes 3145732
  49.1 12.2 %copy-start.6 = (s32[4096]{0:T(1024)S(1)}, s32[4096]{0:T(1024)}, u32[]{:S(2)}) copy-start(s32[4096]{0:T(1024)} %param.15) | copy-start | bytes 49156
  57.0 4.3 %collective-permute-start.1 = (bf16[64,128,128]{2,1,0:T(8,128)(2,1)S(1)}, bf16[64,128,128]{2,1,0:T(8,128)(2,1)}, u32[]{:S(2)}, u32[]{:S(2)}) collective-permute-start(bf16[64,128,128]{2,1,0:T(8,128)(2,1)S(1)} %all-to-all-done.mine_ref), channel_id=1, source_target_pairs={{0,1},{1,0},{2,3},{3,2},{4,5},{5,4},{6,7},{7,6},{8,9},{9,8},{10,11... | collective-permute-start | bytes 6291464 | tf_op jit(solution)/shard_map/ppermute | solution.py:303
  57.1 4.2 %copy-start.5 = (bf16[4096,128]{1,0:T(8,128)(2,1)S(1)}, bf16[4096,128]{1,0:T(8,128)(2,1)}, u32[]{:S(2)}) copy-start(bf16[4096,128]{1,0:T(8,128)(2,1)} %copy-done.4) | copy-start | bytes 3145732
  79.3 18.4 %copy-start.7 = (f32[128]{0:T(128)S(1)}, f32[128]{0:T(128)}, u32[]{:S(2)}) copy-start(f32[128]{0:T(128)} %param.18) | copy-start | bytes 1540
  79.3 18.4 %copy-start.8 = (f32[128]{0:T(128)S(1)}, f32[128]{0:T(128)}, u32[]{:S(2)}) copy-start(f32[128]{0:T(128)} %param.19) | copy-start | bytes 1540
  79.3 2.7 %collective-permute-start.2 = (f32[2048,128]{1,0:T(8,128)S(1)}, f32[2048,128]{1,0:T(8,128)S(1)}, u32[]{:S(2)}, u32[]{:S(2)}) collective-permute-start(f32[2048,128]{1,0:T(8,128)S(1)} %get-tuple-element.12), channel_id=1, source_target_pairs={{0,1},{1,0},{2,3},{3,2},{4,5},{5,4},{6,7},{7,6},{8,9},{9,8},{10,11... | collective-permute-start | bytes 3145736 | tf_op jit(solution)/shard_map/ppermute | solution.py:320

commit v3 on v1

v3 whole, which is shorter than its diff:
```python
import jax
import jax.numpy as jnp
from jax import lax
from jax.experimental import pallas as pl
from jax.experimental.pallas import tpu as pltpu
from jax.sharding import PartitionSpec as P

TILE = 128
PEERS_STEP = 8
TILES_STEP = 4
LOAD_PARTS = 4
EPS = 1e-05
BF16 = jnp.bfloat16
F32 = jnp.float32
F8 = jnp.float8_e4m3fn


def params(mib, axes=1):
    return pltpu.CompilerParams(
        dimension_semantics=("arbitrary",) * axes, vmem_limit_bytes=mib * 2**20
    )


def in_hbm(array):
    return pltpu.with_memory_space_constraint(array, pltpu.HBM)


def pick_kernel(rows_ref, counts_ref, own_ref, out_ref, rows, counts, loaded, table, lines, sems):
    step = pl.program_id(0)
    peers, slots, half = out_ref.shape

    @pl.when(step == 0)
    def _():
        part = own_ref.shape[0] // LOAD_PARTS
        copies = [
            pltpu.make_async_copy(
                own_ref.at[pl.ds(q * part, part)], loaded.at[pl.ds(q * part, part)], sems.at[q]
            )
            for q in range(LOAD_PARTS)
        ]
        row_copy = pltpu.make_async_copy(rows_ref, rows, sems.at[LOAD_PARTS])
        count_copy = pltpu.make_async_copy(counts_ref, counts, sems.at[LOAD_PARTS + 1])
        for copy in copies:
            copy.start()
        row_copy.start()
        count_copy.start()
        for q, copy in enumerate(copies):
            copy.wait()
            table[q * part : (q + 1) * part, :] = loaded[q * part : (q + 1) * part, :].astype(F32)
        row_copy.wait()
        count_copy.wait()

    for p in range(peers):
        for s in range(slots):
            at = p * slots + s
            lines[at : at + 1, :] = table[pl.ds(rows[0, step * peers + p, s], 1), :]
    slot = lax.broadcasted_iota(jnp.int32, (slots, half), 0)
    for p in range(peers):
        live = slot < counts[0, step * peers + p]
        block = lines[p * slots : (p + 1) * slots, :]
        out_ref[p] = jnp.where(live, block, 0.0).astype(BF16)


def pick_rows(send_rows, send_counts, own):
    _, peers, slots = send_rows.shape
    rows, half = own.shape
    hbm = pl.BlockSpec(memory_space=pltpu.HBM)
    return pl.pallas_call(
        pick_kernel,
        grid=(peers // PEERS_STEP,),
        in_specs=[hbm, hbm, hbm],
        out_specs=pl.BlockSpec((PEERS_STEP, slots, half), lambda g: (g, 0, 0)),
        out_shape=pltpu.HBM((peers, slots, half), BF16),
        scratch_shapes=[
            pltpu.SMEM(send_rows.shape, jnp.int32),
            pltpu.SMEM(send_counts.shape, jnp.int32),
            pltpu.VMEM((rows, half), BF16),
            pltpu.VMEM((rows, half), F32),
            pltpu.VMEM((PEERS_STEP * slots, half), F32),
            pltpu.SemaphoreType.DMA((LOAD_PARTS + 2,)),
        ],
        compiler_params=params(16),
        name="pick_rows",
    )(in_hbm(send_rows), in_hbm(send_counts), in_hbm(own))


def adjacency_kernel(core_ref, codes_ref, out_ref):
    per_tile, edges = codes_ref.shape[1:]
    ids = lax.broadcasted_iota(jnp.int32, (TILE, edges), 0).astype(F32).astype(BF16)
    one = jnp.ones((TILE, edges), BF16)
    zero = jnp.zeros((TILE, edges), BF16)

    def hot(values):
        spread = jnp.broadcast_to(values.astype(F32), (16, edges)).astype(BF16)
        spread = jnp.concatenate([spread] * (TILE // 16), axis=0)
        return jnp.where(spread == ids, one, zero).astype(F8)

    for k in range(per_tile):
        codes = codes_ref[0, k : k + 1, :]
        counts = lax.dot_general(
            hot(codes >> 7),
            hot(codes & (TILE - 1)),
            (((1,), (1,)), ((), ())),
            preferred_element_type=F32,
        )
        out_ref[0, :, k * TILE : (k + 1) * TILE] = counts.astype(BF16)


def adjacency(core, codes, tiles):
    _, per_tile, edges = codes.shape
    return pl.pallas_call(
        adjacency_kernel,
        grid_spec=pltpu.PrefetchScalarGridSpec(
            num_scalar_prefetch=1,
            grid=(tiles,),
            in_specs=[
                pl.BlockSpec(
                    (1, per_tile, edges), lambda t, core_ref: (core_ref[0] * tiles + t, 0, 0)
                )
            ],
            out_specs=pl.BlockSpec((1, TILE, per_tile * TILE), lambda t, core_ref: (t, 0, 0)),
        ),
        out_shape=pltpu.HBM((tiles, TILE, per_tile * TILE), BF16),
        compiler_params=params(16),
        cost_estimate=pl.CostEstimate(
            flops=2 * tiles * per_tile * TILE * TILE * edges * 2,
            transcendentals=0,
            bytes_accessed=tiles * per_tile * (TILE * TILE * 2 + edges * 4),
        ),
        name="adjacency",
    )(core, in_hbm(codes))


def aggregate_kernel(
    core_ref,
    tile_src_ref,
    adj_ref,
    deg_ref,
    weight_ref,
    own_ref,
    other_ref,
    mine_ref,
    sibling_ref,
    keep_ref,
    send_ref,
    keep_stats_ref,
    send_stats_ref,
    near,
    far,
    sems,
):
    per_tile = tile_src_ref.shape[1]
    step = pl.program_id(0)
    steps = pl.num_programs(0)
    core = core_ref[0]
    own_tiles, _, half = own_ref.shape
    peers = mine_ref.shape[0]

    @pl.when(step == 0)
    def _():
        owned = pl.ds(0, own_tiles)
        halo = pl.ds(own_tiles, peers)
        copies = [
            pltpu.make_async_copy(own_ref, near.at[owned], sems.at[0]),
            pltpu.make_async_copy(other_ref, far.at[owned], sems.at[1]),
            pltpu.make_async_copy(mine_ref, near.at[halo], sems.at[2]),
            pltpu.make_async_copy(sibling_ref, far.at[halo], sems.at[3]),
        ]
        for copy in copies:
            copy.start()
        for copy in copies:
            copy.wait()

    def source(number):
        return jnp.concatenate([near[number], far[number]], axis=1)

    first = core * (own_tiles // 2) + step * TILES_STEP
    inputs = []
    for q in range(TILES_STEP):
        row = first + q
        total = jnp.zeros((TILE, 2 * half), F32)
        for k in range(0, per_tile, 2):
            pair = jnp.concatenate(
                [source(tile_src_ref[row, k]), source(tile_src_ref[row, k + 1])], axis=0
            )
            total += jnp.dot(
                adj_ref[q, :, k * TILE : (k + 2) * TILE], pair, preferred_element_type=F32
            )
        degree = jnp.broadcast_to(deg_ref[q].astype(F32), (8, TILE)).T[:, :1]
        inputs.append(jnp.concatenate([source(row), (total / degree).astype(BF16)], axis=1))
    pre = jnp.dot(
        jnp.concatenate(inputs, axis=0), weight_ref[...], preferred_element_type=F32
    )
    rows = TILES_STEP * TILE
    here = pl.ds(pl.multiple_of(step * rows, rows), rows)
    keep_ref[here, :] = pre[:, :half]
    send_ref[here, :] = pre[:, half:]

    @pl.when(step == steps - 1)
    def _():
        for values_ref, stats_ref in ((keep_ref, keep_stats_ref), (send_ref, send_stats_ref)):
            values = values_ref[...]
            sums = jnp.sum(values, axis=0, keepdims=True)
            centred = values - sums / values.shape[0]
            stats_ref[0:1, :] = sums
            stats_ref[1:2, :] = jnp.sum(centred * centred, axis=0, keepdims=True)


def aggregate(core, tile_src, adj, degrees, weights, own, other, mine, sibling):
    tiles = adj.shape[0]
    half = mine.shape[2]
    rows = tiles * TILE
    steps = tiles // TILES_STEP
    own = own.reshape(-1, TILE, half)
    other = other.reshape(-1, TILE, half)
    source_tiles = own.shape[0] + mine.shape[0]
    anywhere = pl.BlockSpec(memory_space=pl.ANY)
    vmem = pl.BlockSpec(memory_space=pltpu.VMEM)
    return pl.pallas_call(
        aggregate_kernel,
        grid_spec=pltpu.PrefetchScalarGridSpec(
            num_scalar_prefetch=2,
            grid=(steps,),
            in_specs=[
                pl.BlockSpec((TILES_STEP,) + adj.shape[1:], lambda t, c, s: (t, 0, 0)),
                pl.BlockSpec((TILES_STEP, 1, TILE), lambda t, c, s: (c[0] * steps + t, 0, 0)),
                vmem,
                anywhere,
                anywhere,
                anywhere,
                anywhere,
            ],
            out_specs=[vmem] * 4,
            scratch_shapes=[
                pltpu.VMEM((source_tiles, TILE, half), BF16),
                pltpu.VMEM((source_tiles, TILE, half), BF16),
                pltpu.SemaphoreType.DMA((4,)),
            ],
        ),
        out_shape=[jax.ShapeDtypeStruct((rows, half), F32)] * 2
        + [jax.ShapeDtypeStruct((2, half), F32)] * 2,
        compiler_params=params(32),
        name="aggregate",
    )(core, tile_src, in_hbm(adj), degrees, weights, own, other, mine, sibling)


def normalise_kernel(core_ref, keep_ref, got_ref, parts_ref, gamma_ref, beta_ref, out_ref):
    rows = keep_ref.shape[0]
    parts = parts_ref[...]
    members = 2.0 * parts.shape[0]
    sums = jnp.concatenate([parts[:, 0, :], parts[:, 2, :]], axis=0)
    spreads = jnp.concatenate([parts[:, 1, :], parts[:, 3, :]], axis=0)
    mean = jnp.sum(sums, axis=0, keepdims=True) / (rows * members)
    shift = sums / rows - mean
    var = jnp.sum(spreads + rows * (shift * shift), axis=0, keepdims=True) / (rows * members)
    scale = gamma_ref[...] / jnp.sqrt(var + EPS)
    beta = beta_ref[...]
    here = pl.multiple_of(core_ref[0] * rows, rows)
    there = pl.multiple_of((1 - core_ref[0]) * rows, rows)
    out_ref[pl.ds(here, rows), :] = jnp.maximum(
        (keep_ref[...] - mean) * scale + beta, 0.0
    ).astype(BF16)
    out_ref[pl.ds(there, rows), :] = jnp.maximum(
        (got_ref[...] - mean) * scale + beta, 0.0
    ).astype(BF16)


def normalise(core, keep, got, parts, gamma, beta):
    rows, half = keep.shape
    whole = pl.BlockSpec(memory_space=pltpu.VMEM)
    return pl.pallas_call(
        normalise_kernel,
        in_specs=[pl.BlockSpec(memory_space=pltpu.SMEM)] + [whole] * 5,
        out_specs=whole,
        out_shape=jax.ShapeDtypeStruct((2 * rows, half), BF16),
        compiler_params=pltpu.CompilerParams(vmem_limit_bytes=32 * 2**20),
        name="normalise",
    )(core, keep, got, parts, gamma.reshape(1, half), beta.reshape(1, half))


def local(
    features, send_rows, send_counts, tile_src, edge_codes, degrees, w_self, w_neigh, gamma, beta
):
    rows, half = features.shape
    peers = lax.axis_size("dom")
    tiles = rows // TILE // 2
    core = lax.axis_index("feat").astype(jnp.int32)
    core_arg = core.reshape(1)
    swap = [(0, 1), (1, 0)]

    outgoing = pick_rows(send_rows, send_counts, features)
    mine = lax.all_to_all(outgoing, "dom", split_axis=0, concat_axis=0, tiled=True)
    other = lax.ppermute(features, "feat", swap)
    adj = adjacency(core_arg, edge_codes, tiles)

    def turned(w):
        return jnp.where(core == 0, w, jnp.roll(w, (half, half), (0, 1)))

    weights = jnp.concatenate([turned(w_self), turned(w_neigh)], axis=0)
    mine, adj, other, weights = lax.optimization_barrier((mine, adj, other, weights))
    sibling = lax.ppermute(mine, "feat", swap)
    keep, send, keep_stats, send_stats = aggregate(
        core_arg,
        tile_src,
        adj,
        degrees.reshape(-1, 1, TILE),
        weights,
        features,
        other,
        mine,
        sibling,
    )
    got_stats = lax.ppermute(send_stats, "feat", swap)
    got = lax.ppermute(send, "feat", swap)
    stats = jnp.concatenate([keep_stats, got_stats], axis=0)
    stats = jnp.broadcast_to(stats[None], (peers,) + stats.shape)
    parts = lax.all_to_all(stats, "dom", split_axis=0, concat_axis=0, tiled=True)
    return normalise(core_arg, keep, got, parts, gamma, beta)


def solution(mesh):
    return jax.shard_map(
        local,
        mesh=mesh,
        in_specs=(
            P("dom", "feat"),
            P("dom", None, None),
            P("dom", None),
            P("dom", None),
            P("dom", None, None),
            P("dom"),
            P(),
            P(),
            P("feat"),
            P("feat"),
        ),
        out_specs=P("dom", "feat"),
        check_vma=False,
    )
```

time: 117 us -> 88.8 us (0.76)
  blocking collectives: 56.4 us -> 16.7 us
  waiting for transfers between devices: 2.92 us -> 21.3 us
  starting transfers between devices: 0.53 us -> 12.2 us
  Pallas kernels: 46.6 us -> 36.8 us
  local copies, waits for them, and re-layouts: 6.98 us -> 0.15 us
  other arithmetic: 2.53 us -> 0.11 us
    all_to_all x2 -> x1, blocking collectives: 56.4 us -> 16.7 us  [local(): lax.all_to_all(stats, 'dom', split_axis=0, concat_axis=0, tiled=True)]
    all_to_all x0 -> x1, waiting for transfers between devices: none -> 14.9 us  [local(): lax.all_to_all(outgoing, 'dom', split_axis=0, concat_axis=0, tiled=True)]
    all_to_all x0 -> x1, starting transfers between devices: none -> 11.6 us  [local(): lax.all_to_all(outgoing, 'dom', split_axis=0, concat_axis=0, tiled=True)]
    unnamed x24 -> x15, local copies, waits for them, and re-layouts: 6.68 us -> 0.11 us
    pallas_call x1, Pallas kernels: 17.8 us -> 11.4 us  [aggregate(): pl.pallas_call(aggregate_kernel, grid_spec=pltpu.PrefetchScalarGridSpec(n...]
    ppermute x1, waiting for transfers between devices: 0.01 us -> 4.21 us  [local(): sibling = lax.ppermute(mine, 'feat', swap)]
    pallas_call x2 -> x1, Pallas kernels: 11.4 us -> 9.07 us  [pick_rows(): pl.pallas_call(pick_kernel, grid=(peers // PEERS_STEP,), in_specs=[hbm, h...]
    ppermute x1, waiting for transfers between devices: 2.29 us -> 0.01 us  [local(): got = lax.ppermute(send, 'feat', swap)]
  transfers between devices with their start and end apart: 3 -> 5, of which waited for: 2 -> 3; matrix products, arithmetic and copies ran while one was open for 3% -> 0% of each run, Pallas kernels for 14% -> 27%
where the time goes in v3:
time: 88.8 us; the launch traced here: 87.5 us
  Pallas kernels  36.8 us (41%)
  waiting for transfers between devices  21.3 us (24%)
  blocking collectives  16.7 us (19%)
  starting transfers between devices  12.2 us (14%)
    all_to_all x1, blocking collectives, local(): lax.all_to_all(stats, 'dom', split_axis=0, concat_axis=0, tiled=True)  16.7 us
    pallas_call x1, Pallas kernels, adjacency(): pl.pallas_call(adjacency_kernel, grid_spec=pltpu.PrefetchScalarGridSpec(n...  15 us
    all_to_all x1, waiting for transfers between devices, local(): lax.all_to_all(outgoing, 'dom', split_axis=0, concat_axis=0, tiled=True)  14.9 us
    all_to_all x1, starting transfers between devices, local(): lax.all_to_all(outgoing, 'dom', split_axis=0, concat_axis=0, tiled=True)  11.6 us
    pallas_call x1, Pallas kernels, aggregate(): pl.pallas_call(aggregate_kernel, grid_spec=pltpu.PrefetchScalarGridSpec(n...  11.4 us
    pallas_call x1, Pallas kernels, pick_rows(): pl.pallas_call(pick_kernel, grid=(peers // PEERS_STEP,), in_specs=[hbm, h...  9.07 us
    ppermute x1, waiting for transfers between devices, local(): sibling = lax.ppermute(mine, 'feat', swap)  4.21 us
    ppermute x1, waiting for transfers between devices, local(): got_stats = lax.ppermute(send_stats, 'feat', swap)  2.15 us
  transfers between devices with their start and end apart: 5, of which 3 were waited for; matrix products, arithmetic and copies ran while one was open for 0% of the time, Pallas kernels for 27%

profile of v3, /device:TPU:0, one launch (start us, length us, event | category | flops | bytes accessed | tf_op | source)
XLA Modules:
  0.0 87.5 jit_solution(3363918325043382042)
XLA Ops:
  0.0 0.0 collective-permute-start
  0.0 9.1 %pick_rows.1 = bf16[64,128,128]{2,1,0:T(8,128)(2,1)} custom-call(s32[1,64,128]{2,1,0:T(8,128)} %rows_ref.1, s32[1,64]{1,0:T(1,128)} %counts_ref.1, bf16[4096,128]{1,0:T(8,128)(2,1)} %own_ref.1), custom_call_target="tpu_custom_call" | custom-call | tf_op jit(solution)/shard_map/pick_rows/pallas_call | solution.py:68
  9.1 0.0 copy-start.5
  9.1 0.0 copy-start.4
  9.1 11.6 %all-to-all-start = ((bf16[64,128,128]{2,1,0:T(8,128)(2,1)}), bf16[64,128,128]{2,1,0:T(8,128)(2,1)S(1)}, u32[]{:S(2)}, u32[]{:S(2)}) async-start(bf16[64,128,128]{2,1,0:T(8,128)(2,1)} %pick_rows.1), calls=%async_computation | async-start | bytes 4194304 | tf_op jit(solution)/shard_map/all_to_all | solution.py:292
  20.8 0.0 copy-done.5
  20.8 0.0 copy-done.4
  20.8 0.1 fusion.1
  20.9 0.0 copy-start.6
  21.0 0.0 copy-start
  21.0 0.0 copy-start.1
  21.0 15.0 %adjacency.1.adj_ref = bf16[16,128,3072]{2,1,0:T(8,128)(2,1)} custom-call(s32[1]{0:T(128)} %bitcast.core_ref, s32[32,24,512]{2,1,0:T(8,128)} %codes_ref.1), custom_call_target="tpu_custom_call" | custom-call | flops 12884901888 | bytes 13369344 | tf_op jit(solution)/shard_map/adjacency/pallas_call | solution.py:111
  35.9 0.0 collective-permute-done
  35.9 14.9 %all-to-all-done.mine_ref = bf16[64,128,128]{2,1,0:T(8,128)(2,1)S(1)} async-done(((bf16[64,128,128]{2,1,0:T(8,128)(2,1)}), bf16[64,128,128]{2,1,0:T(8,128)(2,1)S(1)}, u32[]{:S(2)}, u32[]{:S(2)}) %all-to-all-start) | async-done | bytes 2097184 | tf_op jit(solution)/shard_map/all_to_all | solution.py:292
  50.9 0.0 collective-permute-start.1
  50.9 0.0 copy-done.6
  50.9 0.1 copy.11.tile_src_ref
  51.0 4.2 %collective-permute-done.1.sibling_ref = bf16[64,128,128]{2,1,0:T(8,128)(2,1)} collective-permute-done((bf16[64,128,128]{2,1,0:T(8,128)(2,1)S(1)}, bf16[64,128,128]{2,1,0:T(8,128)(2,1)}, u32[]{:S(2)}, u32[]{:S(2)}) %collective-permute-start.1) | collective-permute-done | bytes 2097184 | tf_op jit(solution)/shard_map/ppermute | solution.py:301
  55.2 0.0 copy-done
  55.2 0.0 copy-done.1
  55.2 0.0 copy-start.2
  55.2 0.0 copy-start.3
  55.2 11.4 %aggregate.1 = (f32[2048,128]{1,0:T(8,128)S(1)}, f32[2048,128]{1,0:T(8,128)S(1)}, f32[2,128]{1,0:T(2,128)S(1)}, f32[2,128]{1,0:T(2,128)S(1)}) custom-call(s32[1]{0:T(128)} %bitcast.core_ref, s32[32,24]{1,0:T(8,128)S(1)} %copy.11.tile_src_ref, bf16[16,128,3072]{2,1,0:T(8,128)(2,1)} %adjacency.1.adj_ref, s32[32,1,128]{2,1,0:T(1,128)S(1)} %bitcast.7, ...), custom_call_target="tpu_custom_call" | custom-call | tf_op jit(solution)/shard_map/aggregate/pallas_call | solution.py:219
  66.6 0.2 collective-permute-start.2
  66.8 0.4 collective-permute-start.3
  67.2 2.1 %collective-permute-done.3 = f32[2,128]{1,0:T(2,128)S(1)} collective-permute-done((f32[2,128]{1,0:T(2,128)S(1)}, f32[2,128]{1,0:T(2,128)S(1)}, u32[]{:S(2)}, u32[]{:S(2)}) %collective-permute-start.3) | collective-permute-done | bytes 1056 | tf_op jit(solution)/shard_map/ppermute | solution.py:313
  69.3 16.7 %all_to_all.10.parts_ref = f32[64,4,128]{2,1,0:T(4,128)S(1)} all-to-all(f32[64,4,128]{2,1,0:T(4,128)S(1)} %broadcast_in_dim.2), channel_id=1, replica_groups=mesh['dom'=64,'feat'=2] {'dom'}, dimensions={0} | all-to-all | bytes 262144 | tf_op jit(solution)/shard_map/all_to_all | solution.py:317
  86.1 0.0 collective-permute-done.2.got_ref
  86.1 0.0 copy-done.2
  86.1 0.0 copy-done.3
  86.1 1.4 %normalise.1 = bf16[4096,128]{1,0:T(8,128)(2,1)} custom-call(s32[1]{0:T(128)} %bitcast.core_ref, f32[2048,128]{1,0:T(8,128)S(1)} %get-tuple-element.17.keep_ref, f32[2048,128]{1,0:T(8,128)S(1)} %collective-permute-done.2.got_ref, f32[64,4,128]{2,1,0:T(4,128)S(1)} %all_to_all.10.parts_ref, f32[1,128]{1,0:T(1,128)S(1)} %bitcast.8, f32[1,128]{1,0:T(1,128)S(1)} %bitcast.9), custom_call_target="tpu_custom_call" | custom-call | tf_op jit(solution)/shard_map/normalise/pallas_call | solution.py:271
  (7 shorter events, 0.1 us)
Async XLA Ops:
  0.0 35.9 %collective-permute-start = (bf16[4096,128]{1,0:T(8,128)(2,1)}, bf16[4096,128]{1,0:T(8,128)(2,1)}, u32[]{:S(2)}, u32[]{:S(2)}) collective-permute-start(bf16[4096,128]{1,0:T(8,128)(2,1)} %own_ref.1), channel_id=1, source_target_pairs={{0,1},{1,0},{2,3},{3,2},{4,5},{5,4},{6,7},{7,6},{8,9},{9,8},{10,11... | collective-permute-start | bytes 3145736 | tf_op jit(solution)/shard_map/ppermute | solution.py:293
  9.1 11.7 %copy-start.5 = (bf16[256,256]{1,0:T(8,128)(2,1)S(1)}, bf16[256,256]{1,0:T(8,128)(2,1)}, u32[]{:S(2)}) copy-start(bf16[256,256]{1,0:T(8,128)(2,1)} %param.16) | copy-start | bytes 393220
  9.1 11.7 %copy-start.4 = (bf16[256,256]{1,0:T(8,128)(2,1)S(1)}, bf16[256,256]{1,0:T(8,128)(2,1)}, u32[]{:S(2)}) copy-start(bf16[256,256]{1,0:T(8,128)(2,1)} %param.17) | copy-start | bytes 393220
  9.1 41.8 %all-to-all-start = ((bf16[64,128,128]{2,1,0:T(8,128)(2,1)}), bf16[64,128,128]{2,1,0:T(8,128)(2,1)S(1)}, u32[]{:S(2)}, u32[]{:S(2)}) async-start(bf16[64,128,128]{2,1,0:T(8,128)(2,1)} %pick_rows.1), calls=%async_computation | async-start | bytes 4194304 | tf_op jit(solution)/shard_map/all_to_all | solution.py:292
  20.9 29.9 %copy-start.6 = (s32[32,24]{0,1:T(8,128)S(1)}, s32[32,24]{0,1:T(8,128)}, u32[]{:S(2)}) copy-start(s32[32,24]{0,1:T(8,128)} %param.13) | copy-start | bytes 9220
  21.0 34.2 %copy-start = (bf16[4096,128]{1,0:T(8,128)(2,1)S(1)}, bf16[4096,128]{1,0:T(8,128)(2,1)}, u32[]{:S(2)}) copy-start(bf16[4096,128]{1,0:T(8,128)(2,1)} %own_ref.1) | copy-start | bytes 3145732
  21.0 34.2 %copy-start.1 = (s32[4096]{0:T(1024)S(1)}, s32[4096]{0:T(1024)}, u32[]{:S(2)}) copy-start(s32[4096]{0:T(1024)} %param.15) | copy-start | bytes 49156
  50.9 4.3 %collective-permute-start.1 = (bf16[64,128,128]{2,1,0:T(8,128)(2,1)S(1)}, bf16[64,128,128]{2,1,0:T(8,128)(2,1)}, u32[]{:S(2)}, u32[]{:S(2)}) collective-permute-start(bf16[64,128,128]{2,1,0:T(8,128)(2,1)S(1)} %all-to-all-done.mine_ref), channel_id=1, source_target_pairs={{0,1},{1,0},{2,3},{3,2},{4,5},{5,4},{6,7},{7,6},{8,9},{9,8},{10,11... | collective-permute-start | bytes 6291464 | tf_op jit(solution)/shard_map/ppermute | solution.py:301
  55.2 30.9 %copy-start.2 = (f32[128]{0:T(128)S(1)}, f32[128]{0:T(128)}, u32[]{:S(2)}) copy-start(f32[128]{0:T(128)} %param.18) | copy-start | bytes 1540
  55.2 30.9 %copy-start.3 = (f32[128]{0:T(128)S(1)}, f32[128]{0:T(128)}, u32[]{:S(2)}) copy-start(f32[128]{0:T(128)} %param.19) | copy-start | bytes 1540
  66.6 19.5 %collective-permute-start.2 = (f32[2048,128]{1,0:T(8,128)S(1)}, f32[2048,128]{1,0:T(8,128)S(1)}, u32[]{:S(2)}, u32[]{:S(2)}) collective-permute-start(f32[2048,128]{1,0:T(8,128)S(1)} %get-tuple-element.18), channel_id=1, source_target_pairs={{0,1},{1,0},{2,3},{3,2},{4,5},{5,4},{6,7},{7,6},{8,9},{9,8},{10,11... | collective-permute-start | bytes 3145736 | tf_op jit(solution)/shard_map/ppermute | solution.py:314
  66.8 2.5 %collective-permute-start.3 = (f32[2,128]{1,0:T(2,128)S(1)}, f32[2,128]{1,0:T(2,128)S(1)}, u32[]{:S(2)}, u32[]{:S(2)}) collective-permute-start(f32[2,128]{1,0:T(2,128)S(1)} %get-tuple-element.20), channel_id=1, source_target_pairs={{0,1},{1,0},{2,3},{3,2},{4,5},{5,4},{6,7},{7,6},{8,9},{9,8},{10,11... | collective-permute-start | bytes 3080 | tf_op jit(solution)/shard_map/ppermute | solution.py:313

commit v4 on v3

v4 whole, which is shorter than its diff:
```python
import jax
import jax.numpy as jnp
from jax import lax
from jax.experimental import pallas as pl
from jax.experimental.pallas import tpu as pltpu
from jax.sharding import PartitionSpec as P

TILE = 128
PEERS_STEP = 4
TILES_STEP = 4
PAIR = 2
LOAD_PARTS = 4
EPS = 1e-05
BF16 = jnp.bfloat16
F32 = jnp.float32
F8 = jnp.float8_e4m3fn


def params(mib, axes=1):
    return pltpu.CompilerParams(
        dimension_semantics=("arbitrary",) * axes, vmem_limit_bytes=mib * 2**20
    )


def in_hbm(array):
    return pltpu.with_memory_space_constraint(array, pltpu.HBM)


def pick_kernel(rows_ref, counts_ref, own_ref, out_ref, rows, counts, loaded, table, lines, sems):
    peers, slots, half = out_ref.shape
    part = own_ref.shape[0] // LOAD_PARTS
    row_copy = pltpu.make_async_copy(rows_ref, rows, sems.at[LOAD_PARTS])
    count_copy = pltpu.make_async_copy(counts_ref, counts, sems.at[LOAD_PARTS + 1])
    copies = [
        pltpu.make_async_copy(
            own_ref.at[pl.ds(q * part, part)], loaded.at[pl.ds(q * part, part)], sems.at[q]
        )
        for q in range(LOAD_PARTS)
    ]
    row_copy.start()
    count_copy.start()
    for copy in copies:
        copy.start()
    for q, copy in enumerate(copies):
        copy.wait()
        table[q * part : (q + 1) * part, :] = loaded[q * part : (q + 1) * part, :].astype(F32)
    row_copy.wait()
    count_copy.wait()
    slot = lax.broadcasted_iota(jnp.int32, (slots, half), 0)

    def group(g, carry):
        for p in range(PEERS_STEP):
            for s in range(slots):
                at = p * slots + s
                lines[at : at + 1, :] = table[pl.ds(rows[0, g * PEERS_STEP + p, s], 1), :]
        for p in range(PEERS_STEP):
            peer = g * PEERS_STEP + p
            block = lines[p * slots : (p + 1) * slots, :]
            out_ref[peer] = jnp.where(slot < counts[0, peer], block, 0.0).astype(BF16)
        return carry

    lax.fori_loop(0, peers // PEERS_STEP, group, 0)


def pick_rows(send_rows, send_counts, own):
    _, peers, slots = send_rows.shape
    rows, half = own.shape
    hbm = pl.BlockSpec(memory_space=pltpu.HBM)
    return pl.pallas_call(
        pick_kernel,
        in_specs=[hbm, hbm, hbm],
        out_specs=pl.BlockSpec(memory_space=pltpu.VMEM),
        out_shape=jax.ShapeDtypeStruct((peers, slots, half), BF16),
        scratch_shapes=[
            pltpu.SMEM(send_rows.shape, jnp.int32),
            pltpu.SMEM(send_counts.shape, jnp.int32),
            pltpu.VMEM((rows, half), BF16),
            pltpu.VMEM((rows, half), F32),
            pltpu.VMEM((PEERS_STEP * slots, half), F32),
            pltpu.SemaphoreType.DMA((LOAD_PARTS + 2,)),
        ],
        compiler_params=pltpu.CompilerParams(vmem_limit_bytes=10 * 2**20),
        name="pick_rows",
    )(in_hbm(send_rows), in_hbm(send_counts), in_hbm(own))


def adjacency_kernel(core_ref, codes_ref, out_ref):
    per_tile, edges = codes_ref.shape[1:]
    ids = lax.broadcasted_iota(jnp.int32, (TILE, edges), 0).astype(F32).astype(BF16)
    one = jnp.ones((TILE, edges), BF16)
    zero = jnp.zeros((TILE, edges), BF16)

    def hot(values):
        spread = jnp.broadcast_to(values.astype(F32), (16, edges)).astype(BF16)
        spread = jnp.concatenate([spread] * (TILE // 16), axis=0)
        return jnp.where(spread == ids, one, zero).astype(F8)

    for q in range(PAIR):
        for k in range(per_tile):
            codes = codes_ref[q, k : k + 1, :]
            counts = lax.dot_general(
                hot(codes >> 7),
                hot(codes & (TILE - 1)),
                (((1,), (1,)), ((), ())),
                preferred_element_type=F32,
            )
            out_ref[q, :, k * TILE : (k + 1) * TILE] = counts.astype(BF16)


def adjacency(core, codes, tiles):
    _, per_tile, edges = codes.shape
    steps = tiles // PAIR
    return pl.pallas_call(
        adjacency_kernel,
        grid_spec=pltpu.PrefetchScalarGridSpec(
            num_scalar_prefetch=1,
            grid=(steps,),
            in_specs=[
                pl.BlockSpec(
                    (PAIR, per_tile, edges), lambda t, core_ref: (core_ref[0] * steps + t, 0, 0)
                )
            ],
            out_specs=pl.BlockSpec((PAIR, TILE, per_tile * TILE), lambda t, core_ref: (t, 0, 0)),
        ),
        out_shape=pltpu.HBM((tiles, TILE, per_tile * TILE), BF16),
        compiler_params=params(12),
        cost_estimate=pl.CostEstimate(
            flops=2 * tiles * per_tile * TILE * TILE * edges * 2,
            transcendentals=0,
            bytes_accessed=tiles * per_tile * (TILE * TILE * 2 + edges * 4),
        ),
        name="adjacency",
    )(core, in_hbm(codes))


def stage_kernel(own_ref, mine_ref, adj_ref, near_ref, early_ref, sems):
    own_tiles = own_ref.shape[0]
    copies = [
        pltpu.make_async_copy(own_ref, near_ref.at[pl.ds(0, own_tiles)], sems.at[0]),
        pltpu.make_async_copy(
            mine_ref, near_ref.at[pl.ds(own_tiles, mine_ref.shape[0])], sems.at[1]
        ),
    ]
    for t in range(early_ref.shape[0]):
        copies.append(pltpu.make_async_copy(adj_ref.at[t], early_ref.at[t], sems.at[2 + t]))
    for copy in copies:
        copy.start()
    for copy in copies:
        copy.wait()


def stage(own, mine, adj):
    early = adj.shape[0] // 2
    source_tiles = own.shape[0] + mine.shape[0]
    return pl.pallas_call(
        stage_kernel,
        in_specs=[
            pl.BlockSpec(memory_space=pl.ANY),
            pl.BlockSpec(memory_space=pl.ANY),
            pl.BlockSpec(memory_space=pltpu.HBM),
        ],
        out_specs=[pl.BlockSpec(memory_space=pltpu.VMEM)] * 2,
        out_shape=[
            jax.ShapeDtypeStruct((source_tiles,) + own.shape[1:], BF16),
            jax.ShapeDtypeStruct((early,) + adj.shape[1:], BF16),
        ],
        scratch_shapes=[pltpu.SemaphoreType.DMA((2 + early,))],
        compiler_params=pltpu.CompilerParams(vmem_limit_bytes=2 * 2**20),
        name="stage",
    )(own, mine, in_hbm(adj))


def aggregate_kernel(
    core_ref,
    tile_src_ref,
    adj_ref,
    deg_ref,
    weight_ref,
    other_ref,
    sibling_ref,
    near,
    early,
    keep_ref,
    send_ref,
    keep_stats_ref,
    send_stats_ref,
    far,
    late,
    sems,
):
    per_tile = tile_src_ref.shape[1]
    own_tiles, _, half = other_ref.shape
    peers = sibling_ref.shape[0]
    tiles = adj_ref.shape[0]
    ahead = early.shape[0]
    core = core_ref[0]

    def late_copy(t):
        return pltpu.make_async_copy(adj_ref.at[ahead + t], late.at[t], sems.at[2 + t])

    copies = [
        pltpu.make_async_copy(other_ref, far.at[pl.ds(0, own_tiles)], sems.at[0]),
        pltpu.make_async_copy(sibling_ref, far.at[pl.ds(own_tiles, peers)], sems.at[1]),
    ]
    for copy in copies:
        copy.start()
    for t in range(tiles - ahead):
        late_copy(t).start()
    for copy in copies:
        copy.wait()

    def source(number):
        return jnp.concatenate([near[number], far[number]], axis=1)

    def block(counts, base, at):
        inputs = []
        for q in range(TILES_STEP):
            row = core * tiles + base + at + q
            total = jnp.zeros((TILE, 2 * half), F32)
            for k in range(0, per_tile, 2):
                pair = jnp.concatenate(
                    [source(tile_src_ref[row, k]), source(tile_src_ref[row, k + 1])], axis=0
                )
                total += jnp.dot(
                    counts[at + q, :, k * TILE : (k + 2) * TILE],
                    pair,
                    preferred_element_type=F32,
                )
            degree = jnp.broadcast_to(deg_ref[row].astype(F32), (8, TILE)).T[:, :1]
            inputs.append(jnp.concatenate([source(row), (total / degree).astype(BF16)], axis=1))
        pre = jnp.dot(
            jnp.concatenate(inputs, axis=0), weight_ref[...], preferred_element_type=F32
        )
        rows = TILES_STEP * TILE
        here = pl.ds(pl.multiple_of((base + at) * TILE, rows), rows)
        keep_ref[here, :] = pre[:, :half]
        send_ref[here, :] = pre[:, half:]

    def early_step(step, carry):
        block(early, 0, step * TILES_STEP)
        return carry

    def late_step(step, carry):
        for q in range(TILES_STEP):
            late_copy(step * TILES_STEP + q).wait()
        block(late, ahead, step * TILES_STEP)
        return carry

    lax.fori_loop(0, ahead // TILES_STEP, early_step, 0)
    lax.fori_loop(0, (tiles - ahead) // TILES_STEP, late_step, 0)
    for values_ref, stats_ref in ((keep_ref, keep_stats_ref), (send_ref, send_stats_ref)):
        values = values_ref[...]
        sums = jnp.sum(values, axis=0, keepdims=True)
        centred = values - sums / values.shape[0]
        stats_ref[0:1, :] = sums
        stats_ref[1:2, :] = jnp.sum(centred * centred, axis=0, keepdims=True)


def aggregate(core, tile_src, adj, degrees, weights, other, sibling, near, early):
    tiles = adj.shape[0]
    late = tiles - early.shape[0]
    half = sibling.shape[2]
    rows = tiles * TILE
    smem = pl.BlockSpec(memory_space=pltpu.SMEM)
    vmem = pl.BlockSpec(memory_space=pltpu.VMEM)
    anywhere = pl.BlockSpec(memory_space=pl.ANY)
    hbm = pl.BlockSpec(memory_space=pltpu.HBM)
    return pl.pallas_call(
        aggregate_kernel,
        in_specs=[smem, smem, hbm, vmem, vmem, anywhere, anywhere, vmem, vmem],
        out_specs=[vmem] * 4,
        out_shape=[jax.ShapeDtypeStruct((rows, half), F32)] * 2
        + [jax.ShapeDtypeStruct((2, half), F32)] * 2,
        scratch_shapes=[
            pltpu.VMEM(near.shape, BF16),
            pltpu.VMEM((late,) + adj.shape[1:], BF16),
            pltpu.SemaphoreType.DMA((2 + late,)),
        ],
        compiler_params=pltpu.CompilerParams(vmem_limit_bytes=20 * 2**20),
        name="aggregate",
    )(core, tile_src, in_hbm(adj), degrees, weights, other, sibling, near, early)


def normalise_kernel(core_ref, keep_ref, got_ref, parts_ref, gamma_ref, beta_ref, out_ref):
    rows = keep_ref.shape[0]
    parts = parts_ref[...]
    members = 2.0 * parts.shape[0]
    sums = jnp.concatenate([parts[:, 0, :], parts[:, 2, :]], axis=0)
    spreads = jnp.concatenate([parts[:, 1, :], parts[:, 3, :]], axis=0)
    mean = jnp.sum(sums, axis=0, keepdims=True) / (rows * members)
    shift = sums / rows - mean
    var = jnp.sum(spreads + rows * (shift * shift), axis=0, keepdims=True) / (rows * members)
    scale = gamma_ref[...] / jnp.sqrt(var + EPS)
    beta = beta_ref[...]
    here = pl.multiple_of(core_ref[0] * rows, rows)
    there = pl.multiple_of((1 - core_ref[0]) * rows, rows)
    out_ref[pl.ds(here, rows), :] = jnp.maximum(
        (keep_ref[...] - mean) * scale + beta, 0.0
    ).astype(BF16)
    out_ref[pl.ds(there, rows), :] = jnp.maximum(
        (got_ref[...] - mean) * scale + beta, 0.0
    ).astype(BF16)


def normalise(core, keep, got, parts, gamma, beta):
    rows, half = keep.shape
    whole = pl.BlockSpec(memory_space=pltpu.VMEM)
    return pl.pallas_call(
        normalise_kernel,
        in_specs=[pl.BlockSpec(memory_space=pltpu.SMEM)] + [whole] * 5,
        out_specs=whole,
        out_shape=jax.ShapeDtypeStruct((2 * rows, half), BF16),
        compiler_params=pltpu.CompilerParams(vmem_limit_bytes=8 * 2**20),
        name="normalise",
    )(core, keep, got, parts, gamma.reshape(1, half), beta.reshape(1, half))


def local(
    features, send_rows, send_counts, tile_src, edge_codes, degrees, w_self, w_neigh, gamma, beta
):
    rows, half = features.shape
    peers = lax.axis_size("dom")
    tiles = rows // TILE // 2
    core = lax.axis_index("feat").astype(jnp.int32)
    core_arg = core.reshape(1)
    swap = [(0, 1), (1, 0)]

    outgoing = pick_rows(send_rows, send_counts, features)
    mine = lax.all_to_all(outgoing, "dom", split_axis=0, concat_axis=0, tiled=True)
    other = lax.ppermute(features, "feat", swap)
    adj = adjacency(core_arg, edge_codes, tiles)

    def turned(w):
        return jnp.where(core == 0, w, jnp.roll(w, (half, half), (0, 1)))

    weights = jnp.concatenate([turned(w_self), turned(w_neigh)], axis=0)
    mine, adj, other, weights = lax.optimization_barrier((mine, adj, other, weights))
    sibling = lax.ppermute(mine, "feat", swap)
    other = other.reshape(-1, TILE, half)
    near, early = stage(features.reshape(-1, TILE, half), mine, adj)
    keep, send, keep_stats, send_stats = aggregate(
        core_arg,
        tile_src,
        adj,
        degrees.reshape(-1, 1, TILE),
        weights,
        other,
        sibling,
        near,
        early,
    )
    got_stats = lax.ppermute(send_stats, "feat", swap)
    got = lax.ppermute(send, "feat", swap)
    stats = jnp.concatenate([keep_stats, got_stats], axis=0)
    stats = jnp.broadcast_to(stats[None], (peers,) + stats.shape)
    parts = lax.all_to_all(stats, "dom", split_axis=0, concat_axis=0, tiled=True)
    return normalise(core_arg, keep, got, parts, gamma, beta)


def solution(mesh):
    return jax.shard_map(
        local,
        mesh=mesh,
        in_specs=(
            P("dom", "feat"),
            P("dom", None, None),
            P("dom", None),
            P("dom", None),
            P("dom", None, None),
            P("dom"),
            P(),
            P(),
            P("feat"),
            P("feat"),
        ),
        out_specs=P("dom", "feat"),
        check_vma=False,
    )
```

time: 88.8 us -> 85.3 us (0.961); the launches traced: 87.5 us -> 85 us
  Pallas kernels: 36.8 us -> 34.4 us
  waiting for transfers between devices: 21.3 us -> 19.9 us
  local copies, waits for them, and re-layouts: 0.15 us -> 1.48 us
    ppermute x1, waiting for transfers between devices: 4.21 us -> 1.11 us  [local(): sibling = lax.ppermute(mine, 'feat', swap)]
    all_to_all x1, waiting for transfers between devices: 14.9 us -> 16.7 us  [local(): lax.all_to_all(outgoing, 'dom', split_axis=0, concat_axis=0, tiled=True)]
    pallas_call x1, Pallas kernels: 15 us -> 13.3 us  [adjacency(): pl.pallas_call(adjacency_kernel, grid_spec=pltpu.PrefetchScalarGridSpec(n...]
    unnamed x15 -> x17, local copies, waits for them, and re-layouts: 0.11 us -> 1.44 us
    pallas_call x2 -> x3, Pallas kernels: 20.4 us -> 19.7 us  [the longest x1 8.41 us: aggregate(): pl.pallas_call(aggregate_kernel, in_specs=[smem, smem, hbm, vmem, vmem, a...]
  transfers between devices with their start and end apart: 5 -> 5, of which waited for: 3 -> 3; matrix products, arithmetic and copies ran while one was open for 0% -> 0% of each run, Pallas kernels for 27% -> 29%
where the time goes in v4:
time: 85.3 us; the launch traced here: 85 us
  Pallas kernels  34.4 us (40%)
  waiting for transfers between devices  19.9 us (23%)
  blocking collectives  16.7 us (20%)
  starting transfers between devices  12.2 us (14%)
  local copies, waits for them, and re-layouts  1.48 us (2%)
    all_to_all x1, blocking collectives, local(): lax.all_to_all(stats, 'dom', split_axis=0, concat_axis=0, tiled=True)  16.7 us
    all_to_all x1, waiting for transfers between devices, local(): lax.all_to_all(outgoing, 'dom', split_axis=0, concat_axis=0, tiled=True)  16.7 us
    pallas_call x1, Pallas kernels, adjacency(): pl.pallas_call(adjacency_kernel, grid_spec=pltpu.PrefetchScalarGridSpec(n...  13.3 us
    all_to_all x1, starting transfers between devices, local(): lax.all_to_all(outgoing, 'dom', split_axis=0, concat_axis=0, tiled=True)  11.6 us
    pallas_call x1, Pallas kernels, aggregate(): pl.pallas_call(aggregate_kernel, in_specs=[smem, smem, hbm, vmem, vmem, a...  8.41 us
    pallas_call x1, Pallas kernels, pick_rows(): pl.pallas_call(pick_kernel, in_specs=[hbm, hbm, hbm], out_specs=pl.BlockS...  8.2 us
    pallas_call x1, Pallas kernels, stage(): pl.pallas_call(stage_kernel, in_specs=[pl.BlockSpec(memory_space=pl.ANY),...  3.09 us
    ppermute x1, waiting for transfers between devices, local(): got_stats = lax.ppermute(send_stats, 'feat', swap)  2.15 us
  transfers between devices with their start and end apart: 5, of which 3 were waited for; matrix products, arithmetic and copies ran while one was open for 0% of the time, Pallas kernels for 29%

profile of v4, /device:TPU:0, one launch (start us, length us, event | category | flops | bytes accessed | tf_op | source)
XLA Modules:
  0.0 85.0 jit_solution(10631587889472158207)
XLA Ops:
  0.0 0.0 collective-permute-start
  0.0 8.2 %pick_rows.1 = bf16[64,128,128]{2,1,0:T(8,128)(2,1)S(1)} custom-call(s32[1,64,128]{2,1,0:T(8,128)} %rows_ref.1, s32[1,64]{1,0:T(1,128)} %counts_ref.1, bf16[4096,128]{1,0:T(8,128)(2,1)} %own_ref.1), custom_call_target="tpu_custom_call" | custom-call | tf_op jit(solution)/shard_map/pick_rows/pallas_call | solution.py:69
  8.2 0.0 copy-start
  8.2 1.3 %copy-done = bf16[64,128,128]{2,1,0:T(8,128)(2,1)} copy-done((bf16[64,128,128]{2,1,0:T(8,128)(2,1)}, bf16[64,128,128]{2,1,0:T(8,128)(2,1)S(1)}, u32[]{:S(2)}) %copy-start) | copy-done | bytes 2097176
  9.6 0.0 copy-start.6
  9.6 0.0 copy-start.5
  9.6 11.6 %all-to-all-start = ((bf16[64,128,128]{2,1,0:T(8,128)(2,1)}), bf16[64,128,128]{2,1,0:T(8,128)(2,1)S(1)}, u32[]{:S(2)}, u32[]{:S(2)}) async-start(bf16[64,128,128]{2,1,0:T(8,128)(2,1)} %copy-done), calls=%async_computation | async-start | bytes 4194304 | tf_op jit(solution)/shard_map/all_to_all | solution.py:329
  21.2 0.0 copy-done.6
  21.2 0.0 copy-done.5
  21.3 0.1 fusion.1
  21.4 0.0 copy-start.7
  21.4 0.0 copy-start.1
  21.4 13.3 %adjacency.1.adj_ref = bf16[16,128,3072]{2,1,0:T(8,128)(2,1)} custom-call(s32[1]{0:T(128)} %bitcast.core_ref, s32[32,24,512]{2,1,0:T(8,128)} %codes_ref.1), custom_call_target="tpu_custom_call" | custom-call | flops 12884901888 | bytes 13369344 | tf_op jit(solution)/shard_map/adjacency/pallas_call | solution.py:113
  34.7 0.0 collective-permute-done
  34.7 16.7 %all-to-all-done.mine_ref = bf16[64,128,128]{2,1,0:T(8,128)(2,1)S(1)} async-done(((bf16[64,128,128]{2,1,0:T(8,128)(2,1)}), bf16[64,128,128]{2,1,0:T(8,128)(2,1)S(1)}, u32[]{:S(2)}, u32[]{:S(2)}) %all-to-all-start) | async-done | bytes 2097184 | tf_op jit(solution)/shard_map/all_to_all | solution.py:329
  51.3 0.0 collective-permute-start.1
  51.3 0.0 copy-done.7
  51.3 0.1 copy.11.tile_src_ref
  51.4 0.0 copy-done.1
  51.4 0.0 copy-start.2
  51.4 3.1 %stage.1 = (bf16[96,128,128]{2,1,0:T(8,128)(2,1)S(1)}, bf16[8,128,3072]{2,1,0:T(8,128)(2,1)S(1)}) custom-call(bf16[32,128,128]{2,1,0:T(8,128)(2,1)S(1)} %bitcast.6, bf16[64,128,128]{2,1,0:T(8,128)(2,1)S(1)} %all-to-all-done.mine_ref, bf16[16,128,3072]{2,1,0:T(8,128)(2,1)} %adjacency.1.adj_ref), custom_call_target="tpu_custom_call" | custom-call | tf_op jit(solution)/shard_map/stage/pallas_call | solution.py:155
  54.5 1.1 %collective-permute-done.1.sibling_ref = bf16[64,128,128]{2,1,0:T(8,128)(2,1)} collective-permute-done((bf16[64,128,128]{2,1,0:T(8,128)(2,1)S(1)}, bf16[64,128,128]{2,1,0:T(8,128)(2,1)}, u32[]{:S(2)}, u32[]{:S(2)}) %collective-permute-start.1) | collective-permute-done | bytes 2097184 | tf_op jit(solution)/shard_map/ppermute | solution.py:338
  55.6 0.0 copy-done.2
  55.6 0.0 copy-start.3
  55.6 0.0 copy-start.4
  55.6 8.4 %aggregate.1 = (f32[2048,128]{1,0:T(8,128)S(1)}, f32[2048,128]{1,0:T(8,128)S(1)}, f32[2,128]{1,0:T(2,128)S(1)}, f32[2,128]{1,0:T(2,128)S(1)}) custom-call(s32[1]{0:T(128)} %bitcast.core_ref, s32[32,24]{1,0:T(8,128)S(1)} %copy.11.tile_src_ref, bf16[16,128,3072]{2,1,0:T(8,128)(2,1)} %adjacency.1.adj_ref, s32[32,1,128]{2,1,0:T(1,128)S(1)} %bitcast.7, ...), custom_call_target="tpu_custom_call" | custom-call | tf_op jit(solution)/shard_map/aggregate/pallas_call | solution.py:268
  64.0 0.2 collective-permute-start.2
  64.2 0.4 collective-permute-start.3
  64.6 2.1 %collective-permute-done.3 = f32[2,128]{1,0:T(2,128)S(1)} collective-permute-done((f32[2,128]{1,0:T(2,128)S(1)}, f32[2,128]{1,0:T(2,128)S(1)}, u32[]{:S(2)}, u32[]{:S(2)}) %collective-permute-start.3) | collective-permute-done | bytes 1056 | tf_op jit(solution)/shard_map/ppermute | solution.py:352
  66.8 16.7 %all_to_all.10.parts_ref = f32[64,4,128]{2,1,0:T(4,128)S(1)} all-to-all(f32[64,4,128]{2,1,0:T(4,128)S(1)} %broadcast_in_dim.2), channel_id=1, replica_groups=mesh['dom'=64,'feat'=2] {'dom'}, dimensions={0} | all-to-all | bytes 262144 | tf_op jit(solution)/shard_map/all_to_all | solution.py:356
  83.5 0.0 collective-permute-done.2.got_ref
  83.5 0.0 copy-done.3
  83.5 0.0 copy-done.4
  83.5 1.4 %normalise.1 = bf16[4096,128]{1,0:T(8,128)(2,1)} custom-call(s32[1]{0:T(128)} %bitcast.core_ref, f32[2048,128]{1,0:T(8,128)S(1)} %get-tuple-element.21.keep_ref, f32[2048,128]{1,0:T(8,128)S(1)} %collective-permute-done.2.got_ref, f32[64,4,128]{2,1,0:T(4,128)S(1)} %all_to_all.10.parts_ref, f32[1,128]{1,0:T(1,128)S(1)} %bitcast.8, f32[1,128]{1,0:T(1,128)S(1)} %bitcast.9), custom_call_target="tpu_custom_call" | custom-call | tf_op jit(solution)/shard_map/normalise/pallas_call | solution.py:308
  (7 shorter events, 0.1 us)
Async XLA Ops:
  0.0 34.7 %collective-permute-start = (bf16[4096,128]{1,0:T(8,128)(2,1)}, bf16[4096,128]{1,0:T(8,128)(2,1)}, u32[]{:S(2)}, u32[]{:S(2)}) collective-permute-start(bf16[4096,128]{1,0:T(8,128)(2,1)} %own_ref.1), channel_id=1, source_target_pairs={{0,1},{1,0},{2,3},{3,2},{4,5},{5,4},{6,7},{7,6},{8,9},{9,8},{10,11... | collective-permute-start | bytes 3145736 | tf_op jit(solution)/shard_map/ppermute | solution.py:330
  8.2 1.3 %copy-start = (bf16[64,128,128]{2,1,0:T(8,128)(2,1)}, bf16[64,128,128]{2,1,0:T(8,128)(2,1)S(1)}, u32[]{:S(2)}) copy-start(bf16[64,128,128]{2,1,0:T(8,128)(2,1)S(1)} %pick_rows.1) | copy-start | bytes 6291460
  9.6 11.6 %copy-start.6 = (bf16[256,256]{1,0:T(8,128)(2,1)S(1)}, bf16[256,256]{1,0:T(8,128)(2,1)}, u32[]{:S(2)}) copy-start(bf16[256,256]{1,0:T(8,128)(2,1)} %param.16) | copy-start | bytes 393220
  9.6 11.7 %copy-start.5 = (bf16[256,256]{1,0:T(8,128)(2,1)S(1)}, bf16[256,256]{1,0:T(8,128)(2,1)}, u32[]{:S(2)}) copy-start(bf16[256,256]{1,0:T(8,128)(2,1)} %param.17) | copy-start | bytes 393220
  9.6 41.8 %all-to-all-start = ((bf16[64,128,128]{2,1,0:T(8,128)(2,1)}), bf16[64,128,128]{2,1,0:T(8,128)(2,1)S(1)}, u32[]{:S(2)}, u32[]{:S(2)}) async-start(bf16[64,128,128]{2,1,0:T(8,128)(2,1)} %copy-done), calls=%async_computation | async-start | bytes 4194304 | tf_op jit(solution)/shard_map/all_to_all | solution.py:329
  21.4 29.9 %copy-start.7 = (s32[32,24]{0,1:T(8,128)S(1)}, s32[32,24]{0,1:T(8,128)}, u32[]{:S(2)}) copy-start(s32[32,24]{0,1:T(8,128)} %param.13) | copy-start | bytes 9220
  21.4 30.0 %copy-start.1 = (bf16[4096,128]{1,0:T(8,128)(2,1)S(1)}, bf16[4096,128]{1,0:T(8,128)(2,1)}, u32[]{:S(2)}) copy-start(bf16[4096,128]{1,0:T(8,128)(2,1)} %own_ref.1) | copy-start | bytes 3145732
  51.3 4.3 %collective-permute-start.1 = (bf16[64,128,128]{2,1,0:T(8,128)(2,1)S(1)}, bf16[64,128,128]{2,1,0:T(8,128)(2,1)}, u32[]{:S(2)}, u32[]{:S(2)}) collective-permute-start(bf16[64,128,128]{2,1,0:T(8,128)(2,1)S(1)} %all-to-all-done.mine_ref), channel_id=1, source_target_pairs={{0,1},{1,0},{2,3},{3,2},{4,5},{5,4},{6,7},{7,6},{8,9},{9,8},{10,11... | collective-permute-start | bytes 6291464 | tf_op jit(solution)/shard_map/ppermute | solution.py:338
  51.4 4.2 %copy-start.2 = (s32[4096]{0:T(1024)S(1)}, s32[4096]{0:T(1024)}, u32[]{:S(2)}) copy-start(s32[4096]{0:T(1024)} %param.15) | copy-start | bytes 49156
  55.6 27.9 %copy-start.3 = (f32[128]{0:T(128)S(1)}, f32[128]{0:T(128)}, u32[]{:S(2)}) copy-start(f32[128]{0:T(128)} %param.18) | copy-start | bytes 1540
  55.6 27.9 %copy-start.4 = (f32[128]{0:T(128)S(1)}, f32[128]{0:T(128)}, u32[]{:S(2)}) copy-start(f32[128]{0:T(128)} %param.19) | copy-start | bytes 1540
  64.0 19.5 %collective-permute-start.2 = (f32[2048,128]{1,0:T(8,128)S(1)}, f32[2048,128]{1,0:T(8,128)S(1)}, u32[]{:S(2)}, u32[]{:S(2)}) collective-permute-start(f32[2048,128]{1,0:T(8,128)S(1)} %get-tuple-element.22), channel_id=1, source_target_pairs={{0,1},{1,0},{2,3},{3,2},{4,5},{5,4},{6,7},{7,6},{8,9},{9,8},{10,11... | collective-permute-start | bytes 3145736 | tf_op jit(solution)/shard_map/ppermute | solution.py:353
  64.2 2.5 %collective-permute-start.3 = (f32[2,128]{1,0:T(2,128)S(1)}, f32[2,128]{1,0:T(2,128)S(1)}, u32[]{:S(2)}, u32[]{:S(2)}) collective-permute-start(f32[2,128]{1,0:T(2,128)S(1)} %get-tuple-element.24), channel_id=1, source_target_pairs={{0,1},{1,0},{2,3},{3,2},{4,5},{5,4},{6,7},{7,6},{8,9},{9,8},{10,11... | collective-permute-start | bytes 3080 | tf_op jit(solution)/shard_map/ppermute | solution.py:352

commit v5 on v4

--- a/solution.py
+++ b/solution.py
@@ -7,6 +7,7 @@
 
 TILE = 128
 PEERS_STEP = 4
+RING = 4
 TILES_STEP = 4
 PAIR = 2
 LOAD_PARTS = 4
@@ -26,40 +27,65 @@
     return pltpu.with_memory_space_constraint(array, pltpu.HBM)
 
 
-def pick_kernel(rows_ref, counts_ref, own_ref, out_ref, rows, counts, loaded, table, lines, sems):
+def pick_kernel(rows_ref, counts_ref, own_ref, out_ref, *scratch):
+    ring = scratch[:RING]
+    counts, loaded, table, lines, done, own_sems, ring_sems, count_sem, out_sems = scratch[RING:]
     peers, slots, half = out_ref.shape
     part = own_ref.shape[0] // LOAD_PARTS
-    row_copy = pltpu.make_async_copy(rows_ref, rows, sems.at[LOAD_PARTS])
-    count_copy = pltpu.make_async_copy(counts_ref, counts, sems.at[LOAD_PARTS + 1])
-    copies = [
+    rounds = peers // (PEERS_STEP * RING)
+
+    def row_copy(g, b):
+        wanted = rows_ref.at[0, pl.ds(g * PEERS_STEP, PEERS_STEP)]
+        return pltpu.make_async_copy(wanted, ring[b], ring_sems.at[b])
+
+    def out_copy(g):
+        at = pl.ds(g * PEERS_STEP, PEERS_STEP)
+        return pltpu.make_async_copy(done.at[at], out_ref.at[at], out_sems.at[g])
+
+    count_copy = pltpu.make_async_copy(counts_ref, counts, count_sem)
+    own_copies = [
         pltpu.make_async_copy(
-            own_ref.at[pl.ds(q * part, part)], loaded.at[pl.ds(q * part, part)], sems.at[q]
+            own_ref.at[pl.ds(q * part, part)], loaded.at[pl.ds(q * part, part)], own_sems.at[q]
         )
         for q in range(LOAD_PARTS)
     ]
-    row_copy.start()
+    for b in range(RING):
+        row_copy(b, b).start()
     count_copy.start()
-    for copy in copies:
+    for copy in own_copies:
         copy.start()
-    for q, copy in enumerate(copies):
+    for q, copy in enumerate(own_copies):
         copy.wait()
         table[q * part : (q + 1) * part, :] = loaded[q * part : (q + 1) * part, :].astype(F32)
-    row_copy.wait()
     count_copy.wait()
     slot = lax.broadcasted_iota(jnp.int32, (slots, half), 0)
 
-    def group(g, carry):
-        for p in range(PEERS_STEP):
-            for s in range(slots):
-                at = p * slots + s
-                lines[at : at + 1, :] = table[pl.ds(rows[0, g * PEERS_STEP + p, s], 1), :]
-        for p in range(PEERS_STEP):
-            peer = g * PEERS_STEP + p
-            block = lines[p * slots : (p + 1) * slots, :]
-            out_ref[peer] = jnp.where(slot < counts[0, peer], block, 0.0).astype(BF16)
+    def one_round(i, carry):
+        for b in range(RING):
+            g = i * RING + b
+            row_copy(g, b).wait()
+            for p in range(PEERS_STEP):
+                for s in range(slots):
+                    at = p * slots + s
+                    lines[at : at + 1, :] = table[pl.ds(ring[b][p, s], 1), :]
+
+            @pl.when(i < rounds - 1)
+            def _():
+                row_copy(g + RING, b).start()
+
+            for p in range(PEERS_STEP):
+                peer = g * PEERS_STEP + p
+                block = lines[p * slots : (p + 1) * slots, :]
+                done[peer] = jnp.where(slot < counts[0, peer], block, 0.0).astype(BF16)
+            out_copy(g).start()
         return carry
 
-    lax.fori_loop(0, peers // PEERS_STEP, group, 0)
+    def finish(g, carry):
+        out_copy(g).wait()
+        return carry
+
+    lax.fori_loop(0, rounds, one_round, 0)
+    lax.fori_loop(0, peers // PEERS_STEP, finish, 0)
 
 
 def pick_rows(send_rows, send_counts, own):
@@ -69,17 +95,21 @@
     return pl.pallas_call(
         pick_kernel,
         in_specs=[hbm, hbm, hbm],
-        out_specs=pl.BlockSpec(memory_space=pltpu.VMEM),
-        out_shape=jax.ShapeDtypeStruct((peers, slots, half), BF16),
-        scratch_shapes=[
-            pltpu.SMEM(send_rows.shape, jnp.int32),
+        out_specs=hbm,
+        out_shape=pltpu.HBM((peers, slots, half), BF16),
+        scratch_shapes=[pltpu.SMEM((PEERS_STEP, slots), jnp.int32)] * RING
+        + [
             pltpu.SMEM(send_counts.shape, jnp.int32),
             pltpu.VMEM((rows, half), BF16),
             pltpu.VMEM((rows, half), F32),
             pltpu.VMEM((PEERS_STEP * slots, half), F32),
-            pltpu.SemaphoreType.DMA((LOAD_PARTS + 2,)),
+            pltpu.VMEM((peers, slots, half), BF16),
+            pltpu.SemaphoreType.DMA((LOAD_PARTS,)),
+            pltpu.SemaphoreType.DMA((RING,)),
+            pltpu.SemaphoreType.DMA,
+            pltpu.SemaphoreType.DMA((peers // PEERS_STEP,)),
         ],
-        compiler_params=pltpu.CompilerParams(vmem_limit_bytes=10 * 2**20),
+        compiler_params=pltpu.CompilerParams(vmem_limit_bytes=12 * 2**20),
         name="pick_rows",
     )(in_hbm(send_rows), in_hbm(send_counts), in_hbm(own))
 
@@ -350,6 +380,7 @@
         early,
     )
     got_stats = lax.ppermute(send_stats, "feat", swap)
+    got_stats, send = lax.optimization_barrier((got_stats, send))
     got = lax.ppermute(send, "feat", swap)
     stats = jnp.concatenate([keep_stats, got_stats], axis=0)
     stats = jnp.broadcast_to(stats[None], (peers,) + stats.shape)

time: 85.3 us -> 81.6 us (0.957)
  local copies, waits for them, and re-layouts: 1.48 us -> 0.15 us
  waiting for transfers between devices: 19.9 us -> 18.8 us
  Pallas kernels: 34.4 us -> 33.4 us
    unnamed x17 -> x15, local copies, waits for them, and re-layouts: 1.44 us -> 0.11 us
    pallas_call x1, Pallas kernels: 8.2 us -> 7.03 us  [pick_rows(): pl.pallas_call(pick_kernel, in_specs=[hbm, hbm, hbm], out_specs=hbm, out_...]
    ppermute x1, waiting for transfers between devices: 2.15 us -> 1 us  [local(): got_stats = lax.ppermute(send_stats, 'feat', swap)]
where the time goes in v5:
time: 81.6 us; the launch traced here: 81.3 us
  Pallas kernels  33.4 us (41%)
  waiting for transfers between devices  18.8 us (23%)
  blocking collectives  16.7 us (20%)
  starting transfers between devices  12.1 us (15%)
    all_to_all x1, blocking collectives, local(): lax.all_to_all(stats, 'dom', split_axis=0, concat_axis=0, tiled=True)  16.7 us
    all_to_all x1, waiting for transfers between devices, local(): lax.all_to_all(outgoing, 'dom', split_axis=0, concat_axis=0, tiled=True)  16.6 us
    pallas_call x1, Pallas kernels, adjacency(): pl.pallas_call(adjacency_kernel, grid_spec=pltpu.PrefetchScalarGridSpec(n...  13.3 us
    all_to_all x1, starting transfers between devices, local(): lax.all_to_all(outgoing, 'dom', split_axis=0, concat_axis=0, tiled=True)  11.6 us
    pallas_call x1, Pallas kernels, aggregate(): pl.pallas_call(aggregate_kernel, in_specs=[smem, smem, hbm, vmem, vmem, a...  8.56 us
    pallas_call x1, Pallas kernels, pick_rows(): pl.pallas_call(pick_kernel, in_specs=[hbm, hbm, hbm], out_specs=hbm, out_...  7.03 us
    pallas_call x1, Pallas kernels, stage(): pl.pallas_call(stage_kernel, in_specs=[pl.BlockSpec(memory_space=pl.ANY),...  3.09 us
  transfers between devices with their start and end apart: 5, of which 3 were waited for; matrix products, arithmetic and copies ran while one was open for 0% of the time, Pallas kernels for 29%

profile of v5, /device:TPU:0, one launch (start us, length us, event | category | flops | bytes accessed | tf_op | source)
XLA Modules:
  0.0 81.3 jit_solution(2935383226674938055)
XLA Ops:
  0.0 0.0 collective-permute-start
  0.0 7.0 %pick_rows.1 = bf16[64,128,128]{2,1,0:T(8,128)(2,1)} custom-call(s32[1,64,128]{2,1,0:T(8,128)} %rows_ref.1, s32[1,64]{1,0:T(1,128)} %counts_ref.1, bf16[4096,128]{1,0:T(8,128)(2,1)} %own_ref.1), custom_call_target="tpu_custom_call" | custom-call | tf_op jit(solution)/shard_map/pick_rows/pallas_call | solution.py:95
  7.0 0.0 copy-start.5
  7.1 0.0 copy-start.4
  7.1 11.6 %all-to-all-start = ((bf16[64,128,128]{2,1,0:T(8,128)(2,1)}), bf16[64,128,128]{2,1,0:T(8,128)(2,1)S(1)}, u32[]{:S(2)}, u32[]{:S(2)}) async-start(bf16[64,128,128]{2,1,0:T(8,128)(2,1)} %pick_rows.1), calls=%async_computation | async-start | bytes 4194304 | tf_op jit(solution)/shard_map/all_to_all | solution.py:359
  18.7 0.0 copy-done.5
  18.8 0.0 copy-done.4
  18.8 0.1 fusion.1
  18.9 0.0 copy-start.6
  18.9 0.0 copy-start
  18.9 13.3 %adjacency.1.adj_ref = bf16[16,128,3072]{2,1,0:T(8,128)(2,1)} custom-call(s32[1]{0:T(128)} %bitcast.core_ref, s32[32,24,512]{2,1,0:T(8,128)} %codes_ref.1), custom_call_target="tpu_custom_call" | custom-call | flops 12884901888 | bytes 13369344 | tf_op jit(solution)/shard_map/adjacency/pallas_call | solution.py:143
  32.2 0.0 collective-permute-done
  32.2 16.6 %all-to-all-done.mine_ref = bf16[64,128,128]{2,1,0:T(8,128)(2,1)S(1)} async-done(((bf16[64,128,128]{2,1,0:T(8,128)(2,1)}), bf16[64,128,128]{2,1,0:T(8,128)(2,1)S(1)}, u32[]{:S(2)}, u32[]{:S(2)}) %all-to-all-start) | async-done | bytes 2097184 | tf_op jit(solution)/shard_map/all_to_all | solution.py:359
  48.8 0.0 collective-permute-start.1
  48.8 0.0 copy-done.6
  48.8 0.1 copy.11.tile_src_ref
  48.9 0.0 copy-done
  48.9 0.0 copy-start.1
  48.9 3.1 %stage.1 = (bf16[96,128,128]{2,1,0:T(8,128)(2,1)S(1)}, bf16[8,128,3072]{2,1,0:T(8,128)(2,1)S(1)}) custom-call(bf16[32,128,128]{2,1,0:T(8,128)(2,1)S(1)} %bitcast.6, bf16[64,128,128]{2,1,0:T(8,128)(2,1)S(1)} %all-to-all-done.mine_ref, bf16[16,128,3072]{2,1,0:T(8,128)(2,1)} %adjacency.1.adj_ref), custom_call_target="tpu_custom_call" | custom-call | tf_op jit(solution)/shard_map/stage/pallas_call | solution.py:185
  52.0 1.1 %collective-permute-done.1.sibling_ref = bf16[64,128,128]{2,1,0:T(8,128)(2,1)} collective-permute-done((bf16[64,128,128]{2,1,0:T(8,128)(2,1)S(1)}, bf16[64,128,128]{2,1,0:T(8,128)(2,1)}, u32[]{:S(2)}, u32[]{:S(2)}) %collective-permute-start.1) | collective-permute-done | bytes 2097184 | tf_op jit(solution)/shard_map/ppermute | solution.py:368
  53.1 0.0 copy-done.1
  53.1 0.0 copy-start.2
  53.1 0.0 copy-start.3
  53.1 8.6 %aggregate.1 = (f32[2048,128]{1,0:T(8,128)S(1)}, f32[2048,128]{1,0:T(8,128)S(1)}, f32[2,128]{1,0:T(2,128)S(1)}, f32[2,128]{1,0:T(2,128)S(1)}) custom-call(s32[1]{0:T(128)} %bitcast.core_ref, s32[32,24]{1,0:T(8,128)S(1)} %copy.11.tile_src_ref, bf16[16,128,3072]{2,1,0:T(8,128)(2,1)} %adjacency.1.adj_ref, s32[32,1,128]{2,1,0:T(1,128)S(1)} %bitcast.7, ...), custom_call_target="tpu_custom_call" | custom-call | tf_op jit(solution)/shard_map/aggregate/pallas_call | solution.py:298
  61.7 0.2 collective-permute-start.2
  61.9 1.0 %collective-permute-done.2 = f32[2,128]{1,0:T(2,128)S(1)} collective-permute-done((f32[2,128]{1,0:T(2,128)S(1)}, f32[2,128]{1,0:T(2,128)S(1)}, u32[]{:S(2)}, u32[]{:S(2)}) %collective-permute-start.2) | collective-permute-done | bytes 1056 | tf_op jit(solution)/shard_map/ppermute | solution.py:382
  62.9 0.2 collective-permute-start.3
  63.2 16.7 %all_to_all.10.parts_ref = f32[64,4,128]{2,1,0:T(4,128)S(1)} all-to-all(f32[64,4,128]{2,1,0:T(4,128)S(1)} %broadcast_in_dim.2), channel_id=1, replica_groups=mesh['dom'=64,'feat'=2] {'dom'}, dimensions={0} | all-to-all | bytes 262144 | tf_op jit(solution)/shard_map/all_to_all | solution.py:387
  79.9 0.0 collective-permute-done.3.got_ref
  79.9 0.0 copy-done.2
  79.9 0.0 copy-done.3
  79.9 1.4 %normalise.1 = bf16[4096,128]{1,0:T(8,128)(2,1)} custom-call(s32[1]{0:T(128)} %bitcast.core_ref, f32[2048,128]{1,0:T(8,128)S(1)} %get-tuple-element.23.keep_ref, f32[2048,128]{1,0:T(8,128)S(1)} %collective-permute-done.3.got_ref, f32[64,4,128]{2,1,0:T(4,128)S(1)} %all_to_all.10.parts_ref, f32[1,128]{1,0:T(1,128)S(1)} %bitcast.8, f32[1,128]{1,0:T(1,128)S(1)} %bitcast.9), custom_call_target="tpu_custom_call" | custom-call | tf_op jit(solution)/shard_map/normalise/pallas_call | solution.py:338
  (7 shorter events, 0.1 us)
Async XLA Ops:
  0.0 32.2 %collective-permute-start = (bf16[4096,128]{1,0:T(8,128)(2,1)}, bf16[4096,128]{1,0:T(8,128)(2,1)}, u32[]{:S(2)}, u32[]{:S(2)}) collective-permute-start(bf16[4096,128]{1,0:T(8,128)(2,1)} %own_ref.1), channel_id=1, source_target_pairs={{0,1},{1,0},{2,3},{3,2},{4,5},{5,4},{6,7},{7,6},{8,9},{9,8},{10,11... | collective-permute-start | bytes 3145736 | tf_op jit(solution)/shard_map/ppermute | solution.py:360
  7.0 11.7 %copy-start.5 = (bf16[256,256]{1,0:T(8,128)(2,1)S(1)}, bf16[256,256]{1,0:T(8,128)(2,1)}, u32[]{:S(2)}) copy-start(bf16[256,256]{1,0:T(8,128)(2,1)} %param.16) | copy-start | bytes 393220
  7.1 11.7 %copy-start.4 = (bf16[256,256]{1,0:T(8,128)(2,1)S(1)}, bf16[256,256]{1,0:T(8,128)(2,1)}, u32[]{:S(2)}) copy-start(bf16[256,256]{1,0:T(8,128)(2,1)} %param.17) | copy-start | bytes 393220
  7.1 41.8 %all-to-all-start = ((bf16[64,128,128]{2,1,0:T(8,128)(2,1)}), bf16[64,128,128]{2,1,0:T(8,128)(2,1)S(1)}, u32[]{:S(2)}, u32[]{:S(2)}) async-start(bf16[64,128,128]{2,1,0:T(8,128)(2,1)} %pick_rows.1), calls=%async_computation | async-start | bytes 4194304 | tf_op jit(solution)/shard_map/all_to_all | solution.py:359
  18.9 29.9 %copy-start.6 = (s32[32,24]{0,1:T(8,128)S(1)}, s32[32,24]{0,1:T(8,128)}, u32[]{:S(2)}) copy-start(s32[32,24]{0,1:T(8,128)} %param.13) | copy-start | bytes 9220
  18.9 30.0 %copy-start = (bf16[4096,128]{1,0:T(8,128)(2,1)S(1)}, bf16[4096,128]{1,0:T(8,128)(2,1)}, u32[]{:S(2)}) copy-start(bf16[4096,128]{1,0:T(8,128)(2,1)} %own_ref.1) | copy-start | bytes 3145732
  48.8 4.3 %collective-permute-start.1 = (bf16[64,128,128]{2,1,0:T(8,128)(2,1)S(1)}, bf16[64,128,128]{2,1,0:T(8,128)(2,1)}, u32[]{:S(2)}, u32[]{:S(2)}) collective-permute-start(bf16[64,128,128]{2,1,0:T(8,128)(2,1)S(1)} %all-to-all-done.mine_ref), channel_id=1, source_target_pairs={{0,1},{1,0},{2,3},{3,2},{4,5},{5,4},{6,7},{7,6},{8,9},{9,8},{10,11... | collective-permute-start | bytes 6291464 | tf_op jit(solution)/shard_map/ppermute | solution.py:368
  48.9 4.2 %copy-start.1 = (s32[4096]{0:T(1024)S(1)}, s32[4096]{0:T(1024)}, u32[]{:S(2)}) copy-start(s32[4096]{0:T(1024)} %param.15) | copy-start | bytes 49156
  53.1 26.7 %copy-start.2 = (f32[128]{0:T(128)S(1)}, f32[128]{0:T(128)}, u32[]{:S(2)}) copy-start(f32[128]{0:T(128)} %param.18) | copy-start | bytes 1540
  53.1 26.7 %copy-start.3 = (f32[128]{0:T(128)S(1)}, f32[128]{0:T(128)}, u32[]{:S(2)}) copy-start(f32[128]{0:T(128)} %param.19) | copy-start | bytes 1540
  61.7 1.2 %collective-permute-start.2 = (f32[2,128]{1,0:T(2,128)S(1)}, f32[2,128]{1,0:T(2,128)S(1)}, u32[]{:S(2)}, u32[]{:S(2)}) collective-permute-start(f32[2,128]{1,0:T(2,128)S(1)} %get-tuple-element.24), channel_id=1, source_target_pairs={{0,1},{1,0},{2,3},{3,2},{4,5},{5,4},{6,7},{7,6},{8,9},{9,8},{10,11... | collective-permute-start | bytes 3080 | tf_op jit(solution)/shard_map/ppermute | solution.py:382
  62.9 16.9 %collective-permute-start.3 = (f32[2048,128]{1,0:T(8,128)S(1)}, f32[2048,128]{1,0:T(8,128)S(1)}, u32[]{:S(2)}, u32[]{:S(2)}) collective-permute-start(f32[2048,128]{1,0:T(8,128)S(1)} %get-tuple-element.26), channel_id=1, source_target_pairs={{0,1},{1,0},{2,3},{3,2},{4,5},{5,4},{6,7},{7,6},{8,9},{9,8},{10,11... | collective-permute-start | bytes 3145736 | tf_op jit(solution)/shard_map/ppermute | solution.py:384

commit v6 on v5

--- a/solution.py
+++ b/solution.py
@@ -25,6 +25,10 @@
 
 def in_hbm(array):
     return pltpu.with_memory_space_constraint(array, pltpu.HBM)
+
+
+def in_vmem(array):
+    return pltpu.with_memory_space_constraint(array, pltpu.VMEM)
 
 
 def pick_kernel(rows_ref, counts_ref, own_ref, out_ref, *scratch):
@@ -163,41 +167,33 @@
     )(core, in_hbm(codes))
 
 
-def stage_kernel(own_ref, mine_ref, adj_ref, near_ref, early_ref, sems):
-    own_tiles = own_ref.shape[0]
+def stage_kernel(adj_ref, staged_ref, sems):
     copies = [
-        pltpu.make_async_copy(own_ref, near_ref.at[pl.ds(0, own_tiles)], sems.at[0]),
-        pltpu.make_async_copy(
-            mine_ref, near_ref.at[pl.ds(own_tiles, mine_ref.shape[0])], sems.at[1]
-        ),
+        pltpu.make_async_copy(adj_ref.at[t], staged_ref.at[t], sems.at[t])
+        for t in range(adj_ref.shape[0])
     ]
-    for t in range(early_ref.shape[0]):
-        copies.append(pltpu.make_async_copy(adj_ref.at[t], early_ref.at[t], sems.at[2 + t]))
     for copy in copies:
         copy.start()
     for copy in copies:
         copy.wait()
 
 
-def stage(own, mine, adj):
-    early = adj.shape[0] // 2
-    source_tiles = own.shape[0] + mine.shape[0]
-    return pl.pallas_call(
-        stage_kernel,
+def stage(adj, after):
+    def kernel(adj_ref, after_ref, staged_ref, sems):
+        stage_kernel(adj_ref, staged_ref, sems)
+
+    return pl.pallas_call(
+        kernel,
         in_specs=[
+            pl.BlockSpec(memory_space=pltpu.HBM),
             pl.BlockSpec(memory_space=pl.ANY),
-            pl.BlockSpec(memory_space=pl.ANY),
-            pl.BlockSpec(memory_space=pltpu.HBM),
         ],
-        out_specs=[pl.BlockSpec(memory_space=pltpu.VMEM)] * 2,
-        out_shape=[
-            jax.ShapeDtypeStruct((source_tiles,) + own.shape[1:], BF16),
-            jax.ShapeDtypeStruct((early,) + adj.shape[1:], BF16),
-        ],
-        scratch_shapes=[pltpu.SemaphoreType.DMA((2 + early,))],
+        out_specs=pl.BlockSpec(memory_space=pltpu.VMEM),
+        out_shape=jax.ShapeDtypeStruct(adj.shape, adj.dtype),
+        scratch_shapes=[pltpu.SemaphoreType.DMA((adj.shape[0],))],
         compiler_params=pltpu.CompilerParams(vmem_limit_bytes=2 * 2**20),
         name="stage",
-    )(own, mine, in_hbm(adj))
+    )(in_hbm(adj), after)
 
 
 def aggregate_kernel(
@@ -206,78 +202,54 @@
     adj_ref,
     deg_ref,
     weight_ref,
+    own_ref,
     other_ref,
+    mine_ref,
     sibling_ref,
-    near,
-    early,
     keep_ref,
     send_ref,
     keep_stats_ref,
     send_stats_ref,
-    far,
-    late,
-    sems,
 ):
     per_tile = tile_src_ref.shape[1]
     own_tiles, _, half = other_ref.shape
-    peers = sibling_ref.shape[0]
     tiles = adj_ref.shape[0]
-    ahead = early.shape[0]
     core = core_ref[0]
 
-    def late_copy(t):
-        return pltpu.make_async_copy(adj_ref.at[ahead + t], late.at[t], sems.at[2 + t])
-
-    copies = [
-        pltpu.make_async_copy(other_ref, far.at[pl.ds(0, own_tiles)], sems.at[0]),
-        pltpu.make_async_copy(sibling_ref, far.at[pl.ds(own_tiles, peers)], sems.at[1]),
-    ]
-    for copy in copies:
-        copy.start()
-    for t in range(tiles - ahead):
-        late_copy(t).start()
-    for copy in copies:
-        copy.wait()
-
     def source(number):
-        return jnp.concatenate([near[number], far[number]], axis=1)
-
-    def block(counts, base, at):
+        owned = jnp.minimum(number, own_tiles - 1)
+        halo = jnp.maximum(number - own_tiles, 0)
+        is_own = number < own_tiles
+        near = jnp.where(is_own, own_ref[owned], mine_ref[halo])
+        far = jnp.where(is_own, other_ref[owned], sibling_ref[halo])
+        return jnp.concatenate([near, far], axis=1)
+
+    def block(step, carry):
         inputs = []
         for q in range(TILES_STEP):
-            row = core * tiles + base + at + q
+            at = step * TILES_STEP + q
+            row = core * tiles + at
             total = jnp.zeros((TILE, 2 * half), F32)
             for k in range(0, per_tile, 2):
                 pair = jnp.concatenate(
                     [source(tile_src_ref[row, k]), source(tile_src_ref[row, k + 1])], axis=0
                 )
                 total += jnp.dot(
-                    counts[at + q, :, k * TILE : (k + 2) * TILE],
-                    pair,
-                    preferred_element_type=F32,
+                    adj_ref[at, :, k * TILE : (k + 2) * TILE], pair, preferred_element_type=F32
                 )
             degree = jnp.broadcast_to(deg_ref[row].astype(F32), (8, TILE)).T[:, :1]
-            inputs.append(jnp.concatenate([source(row), (total / degree).astype(BF16)], axis=1))
+            self_rows = jnp.concatenate([own_ref[row], other_ref[row]], axis=1)
+            inputs.append(jnp.concatenate([self_rows, (total / degree).astype(BF16)], axis=1))
         pre = jnp.dot(
             jnp.concatenate(inputs, axis=0), weight_ref[...], preferred_element_type=F32
         )
         rows = TILES_STEP * TILE
-        here = pl.ds(pl.multiple_of((base + at) * TILE, rows), rows)
+        here = pl.ds(pl.multiple_of(step * rows, rows), rows)
         keep_ref[here, :] = pre[:, :half]
         send_ref[here, :] = pre[:, half:]
-
-    def early_step(step, carry):
-        block(early, 0, step * TILES_STEP)
         return carry
 
-    def late_step(step, carry):
-        for q in range(TILES_STEP):
-            late_copy(step * TILES_STEP + q).wait()
-        block(late, ahead, step * TILES_STEP)
-        return carry
-
-    lax.fori_loop(0, ahead // TILES_STEP, early_step, 0)
-    lax.fori_loop(0, (tiles - ahead) // TILES_STEP, late_step, 0)
+    lax.fori_loop(0, tiles // TILES_STEP, block, 0)
     for values_ref, stats_ref in ((keep_ref, keep_stats_ref), (send_ref, send_stats_ref)):
         values = values_ref[...]
         sums = jnp.sum(values, axis=0, keepdims=True)
@@ -286,29 +258,20 @@
         stats_ref[1:2, :] = jnp.sum(centred * centred, axis=0, keepdims=True)
 
 
-def aggregate(core, tile_src, adj, degrees, weights, other, sibling, near, early):
-    tiles = adj.shape[0]
-    late = tiles - early.shape[0]
+def aggregate(core, tile_src, adj, degrees, weights, own, other, mine, sibling):
     half = sibling.shape[2]
-    rows = tiles * TILE
+    rows = adj.shape[0] * TILE
     smem = pl.BlockSpec(memory_space=pltpu.SMEM)
     vmem = pl.BlockSpec(memory_space=pltpu.VMEM)
-    anywhere = pl.BlockSpec(memory_space=pl.ANY)
-    hbm = pl.BlockSpec(memory_space=pltpu.HBM)
     return pl.pallas_call(
         aggregate_kernel,
-        in_specs=[smem, smem, hbm, vmem, vmem, anywhere, anywhere, vmem, vmem],
+        in_specs=[smem, smem] + [vmem] * 7,
         out_specs=[vmem] * 4,
         out_shape=[jax.ShapeDtypeStruct((rows, half), F32)] * 2
         + [jax.ShapeDtypeStruct((2, half), F32)] * 2,
-        scratch_shapes=[
-            pltpu.VMEM(near.shape, BF16),
-            pltpu.VMEM((late,) + adj.shape[1:], BF16),
-            pltpu.SemaphoreType.DMA((2 + late,)),
-        ],
-        compiler_params=pltpu.CompilerParams(vmem_limit_bytes=20 * 2**20),
+        compiler_params=pltpu.CompilerParams(vmem_limit_bytes=8 * 2**20),
         name="aggregate",
-    )(core, tile_src, in_hbm(adj), degrees, weights, other, sibling, near, early)
+    )(core, tile_src, adj, degrees, weights, own, other, mine, in_vmem(sibling))
 
 
 def normalise_kernel(core_ref, keep_ref, got_ref, parts_ref, gamma_ref, beta_ref, out_ref):
@@ -367,17 +330,16 @@
     mine, adj, other, weights = lax.optimization_barrier((mine, adj, other, weights))
     sibling = lax.ppermute(mine, "feat", swap)
     other = other.reshape(-1, TILE, half)
-    near, early = stage(features.reshape(-1, TILE, half), mine, adj)
     keep, send, keep_stats, send_stats = aggregate(
         core_arg,
         tile_src,
-        adj,
+        stage(adj, mine),
         degrees.reshape(-1, 1, TILE),
         weights,
+        features.reshape(-1, TILE, half),
         other,
+        mine,
         sibling,
-        near,
-        early,
     )
     got_stats = lax.ppermute(send_stats, "feat", swap)
     got_stats, send = lax.optimization_barrier((got_stats, send))

time: 81.6 us -> 84.6 us (1.037)
  Pallas kernels: 33.4 us -> 37 us
  waiting for transfers between devices: 18.8 us -> 17.6 us
    pallas_call x2, Pallas kernels: 11.6 us -> 15.3 us  [the longest x1 10.5 us: aggregate(): pl.pallas_call(aggregate_kernel, in_specs=[smem, smem] + [vmem] * 7, out_...]
    ppermute x1, waiting for transfers between devices: 1.11 us -> 0.01 us  [local(): sibling = lax.ppermute(mine, 'feat', swap)]
  transfers between devices with their start and end apart: 5 -> 5, of which waited for: 3 -> 2; matrix products, arithmetic and copies ran while one was open for 0% -> 0% of each run, Pallas kernels for 29% -> 30%
where the time goes in v6:
time: 84.6 us; the launch traced here: 84.3 us
  Pallas kernels  37 us (44%)
  waiting for transfers between devices  17.6 us (21%)
  blocking collectives  16.7 us (20%)
  starting transfers between devices  12.5 us (15%)
    all_to_all x1, waiting for transfers between devices, local(): lax.all_to_all(outgoing, 'dom', split_axis=0, concat_axis=0, tiled=True)  16.7 us
    all_to_all x1, blocking collectives, local(): lax.all_to_all(stats, 'dom', split_axis=0, concat_axis=0, tiled=True)  16.7 us
    pallas_call x1, Pallas kernels, adjacency(): pl.pallas_call(adjacency_kernel, grid_spec=pltpu.PrefetchScalarGridSpec(n...  13.2 us
    all_to_all x1, starting transfers between devices, local(): lax.all_to_all(outgoing, 'dom', split_axis=0, concat_axis=0, tiled=True)  11.6 us
    pallas_call x1, Pallas kernels, aggregate(): pl.pallas_call(aggregate_kernel, in_specs=[smem, smem] + [vmem] * 7, out_...  10.5 us
    pallas_call x1, Pallas kernels, pick_rows(): pl.pallas_call(pick_kernel, in_specs=[hbm, hbm, hbm], out_specs=hbm, out_...  7.04 us
    pallas_call x1, Pallas kernels, stage(): pl.pallas_call(kernel, in_specs=[pl.BlockSpec(memory_space=pltpu.HBM), pl...  4.81 us
  transfers between devices with their start and end apart: 5, of which 2 were waited for; matrix products, arithmetic and copies ran while one was open for 0% of the time, Pallas kernels for 30%

profile of v6, /device:TPU:0, one launch (start us, length us, event | category | flops | bytes accessed | tf_op | source)
XLA Modules:
  0.0 84.3 jit_solution(5587622025677696594)
XLA Ops:
  0.0 0.0 collective-permute-start
  0.0 7.0 %pick_rows.1 = bf16[64,128,128]{2,1,0:T(8,128)(2,1)} custom-call(s32[1,64,128]{2,1,0:T(8,128)} %rows_ref.1, s32[1,64]{1,0:T(1,128)} %counts_ref.1, bf16[4096,128]{1,0:T(8,128)(2,1)} %own_ref.1), custom_call_target="tpu_custom_call" | custom-call | tf_op jit(solution)/shard_map/pick_rows/pallas_call | solution.py:99
  7.0 0.0 copy-start.4
  7.1 0.0 copy-start.5
  7.1 11.6 %all-to-all-start = ((bf16[64,128,128]{2,1,0:T(8,128)(2,1)}), bf16[64,128,128]{2,1,0:T(8,128)(2,1)S(1)}, u32[]{:S(2)}, u32[]{:S(2)}) async-start(bf16[64,128,128]{2,1,0:T(8,128)(2,1)} %pick_rows.1), calls=%async_computation | async-start | bytes 4194304 | tf_op jit(solution)/shard_map/all_to_all | solution.py:322
  18.7 0.0 copy-done.4
  18.8 0.0 copy-done.5
  18.8 0.1 fusion.1
  18.9 0.0 copy-start.6
  18.9 13.2 %adjacency.1.adj_ref = bf16[16,128,3072]{2,1,0:T(8,128)(2,1)} custom-call(s32[1]{0:T(128)} %bitcast.core_ref, s32[32,24,512]{2,1,0:T(8,128)} %codes_ref.1), custom_call_target="tpu_custom_call" | custom-call | flops 12884901888 | bytes 13369344 | tf_op jit(solution)/shard_map/adjacency/pallas_call | solution.py:147
  32.1 0.0 collective-permute-done
  32.1 16.7 %all-to-all-done.after_ref.mine_ref = bf16[64,128,128]{2,1,0:T(8,128)(2,1)S(1)} async-done(((bf16[64,128,128]{2,1,0:T(8,128)(2,1)}), bf16[64,128,128]{2,1,0:T(8,128)(2,1)S(1)}, u32[]{:S(2)}, u32[]{:S(2)}) %all-to-all-start) | async-done | bytes 2097184 | tf_op jit(solution)/shard_map/all_to_all | solution.py:322
  48.8 0.0 collective-permute-start.1
  48.8 0.0 copy-done.6
  48.9 0.1 copy.11.tile_src_ref
  48.9 0.0 copy-start
  48.9 0.0 copy-start.1
  48.9 4.8 %stage.1.adj_ref = bf16[16,128,3072]{2,1,0:T(8,128)(2,1)S(1)} custom-call(bf16[16,128,3072]{2,1,0:T(8,128)(2,1)} %adjacency.1.adj_ref, bf16[64,128,128]{2,1,0:T(8,128)(2,1)S(1)} %all-to-all-done.after_ref.mine_ref), custom_call_target="tpu_custom_call" | custom-call | tf_op jit(solution)/shard_map/stage/pallas_call | solution.py:185
  53.7 0.0 collective-permute-done.1.sibling_ref
  53.8 0.1 copy-done
  53.8 0.0 copy-done.1
  53.8 0.0 copy-start.2
  53.8 0.0 copy-start.3
  53.8 10.5 %aggregate.1 = (f32[2048,128]{1,0:T(8,128)S(1)}, f32[2048,128]{1,0:T(8,128)S(1)}, f32[2,128]{1,0:T(2,128)S(1)}, f32[2,128]{1,0:T(2,128)S(1)}) custom-call(s32[1]{0:T(128)} %bitcast.core_ref, s32[32,24]{1,0:T(8,128)S(1)} %copy.11.tile_src_ref, bf16[16,128,3072]{2,1,0:T(8,128)(2,1)S(1)} %stage.1.adj_ref, s32[32,1,128]{2,1,0:T(1,128)S(1)} %bitcast.8, ...), custom_call_target="tpu_custom_call" | custom-call | tf_op jit(solution)/shard_map/aggregate/pallas_call | solution.py:266
  64.3 0.6 collective-permute-start.2
  64.9 0.8 collective-permute-done.2
  65.8 0.3 collective-permute-start.3
  66.1 16.7 %all_to_all.10.parts_ref = f32[64,4,128]{2,1,0:T(4,128)S(1)} all-to-all(f32[64,4,128]{2,1,0:T(4,128)S(1)} %broadcast_in_dim.2), channel_id=1, replica_groups=mesh['dom'=64,'feat'=2] {'dom'}, dimensions={0} | all-to-all | bytes 262144 | tf_op jit(solution)/shard_map/all_to_all | solution.py:349
  82.8 0.0 collective-permute-done.3.got_ref
  82.8 0.0 copy-done.2
  82.8 0.0 copy-done.3
  82.8 1.4 %normalise.1 = bf16[4096,128]{1,0:T(8,128)(2,1)} custom-call(s32[1]{0:T(128)} %bitcast.core_ref, f32[2048,128]{1,0:T(8,128)S(1)} %get-tuple-element.19.keep_ref, f32[2048,128]{1,0:T(8,128)S(1)} %collective-permute-done.3.got_ref, f32[64,4,128]{2,1,0:T(4,128)S(1)} %all_to_all.10.parts_ref, f32[1,128]{1,0:T(1,128)S(1)} %bitcast.9, f32[1,128]{1,0:T(1,128)S(1)} %bitcast.10), custom_call_target="tpu_custom_call" | custom-call | tf_op jit(solution)/shard_map/normalise/pallas_call | solution.py:301
  (7 shorter events, 0.1 us)
Async XLA Ops:
  0.0 32.1 %collective-permute-start = (bf16[4096,128]{1,0:T(8,128)(2,1)}, bf16[4096,128]{1,0:T(8,128)(2,1)S(1)}, u32[]{:S(2)}, u32[]{:S(2)}) collective-permute-start(bf16[4096,128]{1,0:T(8,128)(2,1)} %own_ref.1), channel_id=1, source_target_pairs={{0,1},{1,0},{2,3},{3,2},{4,5},{5,4},{6,7},{7,6},{8,9},{9,8},{10,11... | collective-permute-start | bytes 3145736 | tf_op jit(solution)/shard_map/ppermute | solution.py:323
  7.0 11.7 %copy-start.4 = (bf16[256,256]{1,0:T(8,128)(2,1)S(1)}, bf16[256,256]{1,0:T(8,128)(2,1)}, u32[]{:S(2)}) copy-start(bf16[256,256]{1,0:T(8,128)(2,1)} %param.17) | copy-start | bytes 393220
  7.1 11.7 %copy-start.5 = (bf16[256,256]{1,0:T(8,128)(2,1)S(1)}, bf16[256,256]{1,0:T(8,128)(2,1)}, u32[]{:S(2)}) copy-start(bf16[256,256]{1,0:T(8,128)(2,1)} %param.16) | copy-start | bytes 393220
  7.1 41.8 %all-to-all-start = ((bf16[64,128,128]{2,1,0:T(8,128)(2,1)}), bf16[64,128,128]{2,1,0:T(8,128)(2,1)S(1)}, u32[]{:S(2)}, u32[]{:S(2)}) async-start(bf16[64,128,128]{2,1,0:T(8,128)(2,1)} %pick_rows.1), calls=%async_computation | async-start | bytes 4194304 | tf_op jit(solution)/shard_map/all_to_all | solution.py:322
  18.9 29.9 %copy-start.6 = (s32[32,24]{0,1:T(8,128)S(1)}, s32[32,24]{0,1:T(8,128)}, u32[]{:S(2)}) copy-start(s32[32,24]{0,1:T(8,128)} %param.13) | copy-start | bytes 9220
  48.8 4.9 %collective-permute-start.1 = (bf16[64,128,128]{2,1,0:T(8,128)(2,1)S(1)}, bf16[64,128,128]{2,1,0:T(8,128)(2,1)}, u32[]{:S(2)}, u32[]{:S(2)}) collective-permute-start(bf16[64,128,128]{2,1,0:T(8,128)(2,1)S(1)} %all-to-all-done.after_ref.mine_ref), channel_id=1, source_target_pairs={{0,1},{1,0},{2,3},{3,2},{4,5},{5,4},{6,7},{7,6},{8,9},{9,8},{10,11... | collective-permute-start | bytes 6291464 | tf_op jit(solution)/shard_map/ppermute | solution.py:331
  48.9 4.9 %copy-start = (bf16[4096,128]{1,0:T(8,128)(2,1)S(1)}, bf16[4096,128]{1,0:T(8,128)(2,1)}, u32[]{:S(2)}) copy-start(bf16[4096,128]{1,0:T(8,128)(2,1)} %own_ref.1) | copy-start | bytes 3145732
  48.9 4.9 %copy-start.1 = (s32[4096]{0:T(1024)S(1)}, s32[4096]{0:T(1024)}, u32[]{:S(2)}) copy-start(s32[4096]{0:T(1024)} %param.15) | copy-start | bytes 49156
  53.8 29.0 %copy-start.2 = (f32[128]{0:T(128)S(1)}, f32[128]{0:T(128)}, u32[]{:S(2)}) copy-start(f32[128]{0:T(128)} %param.18) | copy-start | bytes 1540
  53.8 29.0 %copy-start.3 = (f32[128]{0:T(128)S(1)}, f32[128]{0:T(128)}, u32[]{:S(2)}) copy-start(f32[128]{0:T(128)} %param.19) | copy-start | bytes 1540
  64.3 1.4 %collective-permute-start.2 = (f32[2,128]{1,0:T(2,128)S(1)}, f32[2,128]{1,0:T(2,128)S(1)}, u32[]{:S(2)}, u32[]{:S(2)}) collective-permute-start(f32[2,128]{1,0:T(2,128)S(1)} %get-tuple-element.20), channel_id=1, source_target_pairs={{0,1},{1,0},{2,3},{3,2},{4,5},{5,4},{6,7},{7,6},{8,9},{9,8},{10,11... | collective-permute-start | bytes 3080 | tf_op jit(solution)/shard_map/ppermute | solution.py:344
  65.8 17.1 %collective-permute-start.3 = (f32[2048,128]{1,0:T(8,128)S(1)}, f32[2048,128]{1,0:T(8,128)S(1)}, u32[]{:S(2)}, u32[]{:S(2)}) collective-permute-start(f32[2048,128]{1,0:T(8,128)S(1)} %get-tuple-element.22), channel_id=1, source_target_pairs={{0,1},{1,0},{2,3},{3,2},{4,5},{5,4},{6,7},{7,6},{8,9},{9,8},{10,11... | collective-permute-start | bytes 3145736 | tf_op jit(solution)/shard_map/ppermute | solution.py:346

commit v7 on v5

--- a/solution.py
+++ b/solution.py
@@ -234,15 +234,15 @@
     ]
     for copy in copies:
         copy.start()
+    for copy in copies:
+        copy.wait()
     for t in range(tiles - ahead):
         late_copy(t).start()
-    for copy in copies:
-        copy.wait()
 
     def source(number):
         return jnp.concatenate([near[number], far[number]], axis=1)
 
-    def block(counts, base, at):
+    def block(counts, base, at, sums):
         inputs = []
         for q in range(TILES_STEP):
             row = core * tiles + base + at + q
@@ -265,24 +265,25 @@
         here = pl.ds(pl.multiple_of((base + at) * TILE, rows), rows)
         keep_ref[here, :] = pre[:, :half]
         send_ref[here, :] = pre[:, half:]
-
-    def early_step(step, carry):
-        block(early, 0, step * TILES_STEP)
-        return carry
-
-    def late_step(step, carry):
+        return sums + jnp.sum(pre, axis=0, keepdims=True)
+
+    def early_step(step, sums):
+        return block(early, 0, step * TILES_STEP, sums)
+
+    def late_step(step, sums):
         for q in range(TILES_STEP):
             late_copy(step * TILES_STEP + q).wait()
-        block(late, ahead, step * TILES_STEP)
-        return carry
-
-    lax.fori_loop(0, ahead // TILES_STEP, early_step, 0)
-    lax.fori_loop(0, (tiles - ahead) // TILES_STEP, late_step, 0)
-    for values_ref, stats_ref in ((keep_ref, keep_stats_ref), (send_ref, send_stats_ref)):
-        values = values_ref[...]
-        sums = jnp.sum(values, axis=0, keepdims=True)
-        centred = values - sums / values.shape[0]
-        stats_ref[0:1, :] = sums
+        return block(late, ahead, step * TILES_STEP, sums)
+
+    sums = jnp.zeros((1, 2 * half), F32)
+    sums = lax.fori_loop(0, ahead // TILES_STEP, early_step, sums)
+    sums = lax.fori_loop(0, (tiles - ahead) // TILES_STEP, late_step, sums)
+    for values_ref, stats_ref, total in (
+        (keep_ref, keep_stats_ref, sums[:, :half]),
+        (send_ref, send_stats_ref, sums[:, half:]),
+    ):
+        centred = values_ref[...] - total / values_ref.shape[0]
+        stats_ref[0:1, :] = total
         stats_ref[1:2, :] = jnp.sum(centred * centred, axis=0, keepdims=True)
 
 
@@ -306,7 +307,7 @@
             pltpu.VMEM((late,) + adj.shape[1:], BF16),
             pltpu.SemaphoreType.DMA((2 + late,)),
         ],
-        compiler_params=pltpu.CompilerParams(vmem_limit_bytes=20 * 2**20),
+        compiler_params=pltpu.CompilerParams(vmem_limit_bytes=12 * 2**20),
         name="aggregate",
     )(core, tile_src, in_hbm(adj), degrees, weights, other, sibling, near, early)
 
@@ -367,7 +368,7 @@
     mine, adj, other, weights = lax.optimization_barrier((mine, adj, other, weights))
     sibling = lax.ppermute(mine, "feat", swap)
     other = other.reshape(-1, TILE, half)
-    near, early = stage(features.reshape(-1, TILE, half), mine, adj)
+    near, early = stage(features.reshape(-1, TILE, half), in_hbm(mine), adj)
     keep, send, keep_stats, send_stats = aggregate(
         core_arg,
         tile_src,

time: 81.6 us -> 79.9 us (0.979)
  waiting for transfers between devices: 18.8 us -> 17.2 us
  Pallas kernels: 33.4 us -> 32 us
  local copies, waits for them, and re-layouts: 0.15 us -> 1.13 us
    pallas_call x1, Pallas kernels: 8.56 us -> 6.68 us  [aggregate(): pl.pallas_call(aggregate_kernel, in_specs=[smem, smem, hbm, vmem, vmem, a...]
    all_to_all x1, waiting for transfers between devices: 16.6 us -> 15.5 us  [local(): lax.all_to_all(outgoing, 'dom', split_axis=0, concat_axis=0, tiled=True)]
    unnamed x15 -> x19, local copies, waits for them, and re-layouts: 0.11 us -> 1.08 us
  transfers between devices with their start and end apart: 5 -> 5, of which waited for: 3 -> 3; matrix products, arithmetic and copies ran while one was open for 0% -> 0% of each run, Pallas kernels for 29% -> 30%
where the time goes in v7:
time: 79.9 us; the launch traced here: 79.6 us
  Pallas kernels  32 us (40%)
  waiting for transfers between devices  17.2 us (22%)
  blocking collectives  16.7 us (21%)
  starting transfers between devices  12.3 us (15%)
  local copies, waits for them, and re-layouts  1.13 us (1%)
    all_to_all x1, blocking collectives, local(): lax.all_to_all(stats, 'dom', split_axis=0, concat_axis=0, tiled=True)  16.7 us
    all_to_all x1, waiting for transfers between devices, local(): lax.all_to_all(outgoing, 'dom', split_axis=0, concat_axis=0, tiled=True)  15.5 us
    pallas_call x1, Pallas kernels, adjacency(): pl.pallas_call(adjacency_kernel, grid_spec=pltpu.PrefetchScalarGridSpec(n...  13.3 us
    all_to_all x1, starting transfers between devices, local(): lax.all_to_all(outgoing, 'dom', split_axis=0, concat_axis=0, tiled=True)  11.9 us
    pallas_call x1, Pallas kernels, pick_rows(): pl.pallas_call(pick_kernel, in_specs=[hbm, hbm, hbm], out_specs=hbm, out_...  7.02 us
    pallas_call x1, Pallas kernels, aggregate(): pl.pallas_call(aggregate_kernel, in_specs=[smem, smem, hbm, vmem, vmem, a...  6.68 us
    pallas_call x1, Pallas kernels, stage(): pl.pallas_call(stage_kernel, in_specs=[pl.BlockSpec(memory_space=pl.ANY),...  3.62 us
  transfers between devices with their start and end apart: 5, of which 3 were waited for; matrix products, arithmetic and copies ran while one was open for 0% of the time, Pallas kernels for 30%

profile of v7, /device:TPU:0, one launch (start us, length us, event | category | flops | bytes accessed | tf_op | source)
XLA Modules:
  0.0 79.6 jit_solution(15847924001454496236)
XLA Ops:
  0.0 0.0 collective-permute-start
  0.0 7.0 %pick_rows.1 = bf16[64,128,128]{2,1,0:T(8,128)(2,1)} custom-call(s32[1,64,128]{2,1,0:T(8,128)} %rows_ref.1, s32[1,64]{1,0:T(1,128)} %counts_ref.1, bf16[4096,128]{1,0:T(8,128)(2,1)} %own_ref.1), custom_call_target="tpu_custom_call" | custom-call | tf_op jit(solution)/shard_map/pick_rows/pallas_call | solution.py:95
  7.0 0.0 copy-start.7
  7.0 0.0 copy-start.6
  7.1 11.9 %all-to-all-start = ((bf16[64,128,128]{2,1,0:T(8,128)(2,1)}), bf16[64,128,128]{2,1,0:T(8,128)(2,1)}, u32[]{:S(2)}, u32[]{:S(2)}) async-start(bf16[64,128,128]{2,1,0:T(8,128)(2,1)} %pick_rows.1), calls=%async_computation | async-start | bytes 4194304 | tf_op jit(solution)/shard_map/all_to_all | solution.py:360
  19.0 0.0 copy-done.7
  19.0 0.0 copy-done.6
  19.1 0.1 fusion.1
  19.2 0.0 copy-start.8
  19.2 0.0 copy-start
  19.2 13.3 %adjacency.1.adj_ref = bf16[16,128,3072]{2,1,0:T(8,128)(2,1)} custom-call(s32[1]{0:T(128)} %bitcast.core_ref, s32[32,24,512]{2,1,0:T(8,128)} %codes_ref.1), custom_call_target="tpu_custom_call" | custom-call | flops 12884901888 | bytes 13369344 | tf_op jit(solution)/shard_map/adjacency/pallas_call | solution.py:143
  32.4 0.0 collective-permute-done
  32.5 0.0 copy-start.1
  32.5 1.0 %copy-done.1 = bf16[4096,128]{1,0:T(8,128)(2,1)} copy-done((bf16[4096,128]{1,0:T(8,128)(2,1)}, bf16[4096,128]{1,0:T(8,128)(2,1)S(1)}, u32[]{:S(2)}) %copy-start.1) | copy-done | bytes 1048600
  33.4 15.5 %all-to-all-done.mine_ref = bf16[64,128,128]{2,1,0:T(8,128)(2,1)} async-done(((bf16[64,128,128]{2,1,0:T(8,128)(2,1)}), bf16[64,128,128]{2,1,0:T(8,128)(2,1)}, u32[]{:S(2)}, u32[]{:S(2)}) %all-to-all-start) | async-done | bytes 2097184 | tf_op jit(solution)/shard_map/all_to_all | solution.py:360
  48.9 0.0 collective-permute-start.1
  48.9 0.0 copy-done.8
  48.9 0.1 copy.11.tile_src_ref
  49.0 0.0 copy-done
  49.0 0.0 copy-start.2
  49.0 0.0 copy-start.3
  49.0 3.6 %stage.1 = (bf16[96,128,128]{2,1,0:T(8,128)(2,1)S(1)}, bf16[8,128,3072]{2,1,0:T(8,128)(2,1)S(1)}) custom-call(bf16[32,128,128]{2,1,0:T(8,128)(2,1)S(1)} %bitcast.6, bf16[64,128,128]{2,1,0:T(8,128)(2,1)} %all-to-all-done.mine_ref, bf16[16,128,3072]{2,1,0:T(8,128)(2,1)} %adjacency.1.adj_ref), custom_call_target="tpu_custom_call" | custom-call | tf_op jit(solution)/shard_map/stage/pallas_call | solution.py:185
  52.7 0.7 collective-permute-done.1.sibling_ref
  53.3 0.0 copy-done.2
  53.3 0.0 copy-done.3
  53.3 0.0 copy-start.4
  53.3 0.0 copy-start.5
  53.3 6.7 %aggregate.1 = (f32[2048,128]{1,0:T(8,128)S(1)}, f32[2048,128]{1,0:T(8,128)S(1)}, f32[2,128]{1,0:T(2,128)S(1)}, f32[2,128]{1,0:T(2,128)S(1)}) custom-call(s32[1]{0:T(128)} %bitcast.core_ref, s32[32,24]{1,0:T(8,128)S(1)} %copy.11.tile_src_ref, bf16[16,128,3072]{2,1,0:T(8,128)(2,1)} %adjacency.1.adj_ref, s32[32,1,128]{2,1,0:T(1,128)S(1)} %bitcast.8, ...), custom_call_target="tpu_custom_call" | custom-call | tf_op jit(solution)/shard_map/aggregate/pallas_call | solution.py:299
  60.0 0.2 collective-permute-start.2
  60.2 1.0 %collective-permute-done.2 = f32[2,128]{1,0:T(2,128)S(1)} collective-permute-done((f32[2,128]{1,0:T(2,128)S(1)}, f32[2,128]{1,0:T(2,128)S(1)}, u32[]{:S(2)}, u32[]{:S(2)}) %collective-permute-start.2) | collective-permute-done | bytes 1056 | tf_op jit(solution)/shard_map/ppermute | solution.py:383
  61.2 0.2 collective-permute-start.3
  61.5 16.7 %all_to_all.10.parts_ref = f32[64,4,128]{2,1,0:T(4,128)S(1)} all-to-all(f32[64,4,128]{2,1,0:T(4,128)S(1)} %broadcast_in_dim.2), channel_id=1, replica_groups=mesh['dom'=64,'feat'=2] {'dom'}, dimensions={0} | all-to-all | bytes 262144 | tf_op jit(solution)/shard_map/all_to_all | solution.py:388
  78.2 0.0 collective-permute-done.3.got_ref
  78.2 0.0 copy-done.4
  78.2 0.0 copy-done.5
  78.2 1.4 %normalise.1 = bf16[4096,128]{1,0:T(8,128)(2,1)} custom-call(s32[1]{0:T(128)} %bitcast.core_ref, f32[2048,128]{1,0:T(8,128)S(1)} %get-tuple-element.23.keep_ref, f32[2048,128]{1,0:T(8,128)S(1)} %collective-permute-done.3.got_ref, f32[64,4,128]{2,1,0:T(4,128)S(1)} %all_to_all.10.parts_ref, f32[1,128]{1,0:T(1,128)S(1)} %bitcast.9, f32[1,128]{1,0:T(1,128)S(1)} %bitcast.10), custom_call_target="tpu_custom_call" | custom-call | tf_op jit(solution)/shard_map/normalise/pallas_call | solution.py:339
  (7 shorter events, 0.1 us)
Async XLA Ops:
  0.0 32.5 %collective-permute-start = (bf16[4096,128]{1,0:T(8,128)(2,1)}, bf16[4096,128]{1,0:T(8,128)(2,1)S(1)}, u32[]{:S(2)}, u32[]{:S(2)}) collective-permute-start(bf16[4096,128]{1,0:T(8,128)(2,1)} %own_ref.1), channel_id=1, source_target_pairs={{0,1},{1,0},{2,3},{3,2},{4,5},{5,4},{6,7},{7,6},{8,9},{9,8},{10,11... | collective-permute-start | bytes 3145736 | tf_op jit(solution)/shard_map/ppermute | solution.py:361
  7.0 11.9 %copy-start.7 = (bf16[256,256]{1,0:T(8,128)(2,1)S(1)}, bf16[256,256]{1,0:T(8,128)(2,1)}, u32[]{:S(2)}) copy-start(bf16[256,256]{1,0:T(8,128)(2,1)} %param.16) | copy-start | bytes 393220
  7.0 12.0 %copy-start.6 = (bf16[256,256]{1,0:T(8,128)(2,1)S(1)}, bf16[256,256]{1,0:T(8,128)(2,1)}, u32[]{:S(2)}) copy-start(bf16[256,256]{1,0:T(8,128)(2,1)} %param.17) | copy-start | bytes 393220
  7.1 41.9 %all-to-all-start = ((bf16[64,128,128]{2,1,0:T(8,128)(2,1)}), bf16[64,128,128]{2,1,0:T(8,128)(2,1)}, u32[]{:S(2)}, u32[]{:S(2)}) async-start(bf16[64,128,128]{2,1,0:T(8,128)(2,1)} %pick_rows.1), calls=%async_computation | async-start | bytes 4194304 | tf_op jit(solution)/shard_map/all_to_all | solution.py:360
  19.2 29.8 %copy-start.8 = (s32[32,24]{0,1:T(8,128)S(1)}, s32[32,24]{0,1:T(8,128)}, u32[]{:S(2)}) copy-start(s32[32,24]{0,1:T(8,128)} %param.13) | copy-start | bytes 9220
  19.2 29.9 %copy-start = (bf16[4096,128]{1,0:T(8,128)(2,1)S(1)}, bf16[4096,128]{1,0:T(8,128)(2,1)}, u32[]{:S(2)}) copy-start(bf16[4096,128]{1,0:T(8,128)(2,1)} %own_ref.1) | copy-start | bytes 3145732
  32.5 1.0 %copy-start.1 = (bf16[4096,128]{1,0:T(8,128)(2,1)}, bf16[4096,128]{1,0:T(8,128)(2,1)S(1)}, u32[]{:S(2)}) copy-start(bf16[4096,128]{1,0:T(8,128)(2,1)S(1)} %collective-permute-done) | copy-start | bytes 3145732
  48.9 4.4 %collective-permute-start.1 = (bf16[64,128,128]{2,1,0:T(8,128)(2,1)}, bf16[64,128,128]{2,1,0:T(8,128)(2,1)S(1)}, u32[]{:S(2)}, u32[]{:S(2)}) collective-permute-start(bf16[64,128,128]{2,1,0:T(8,128)(2,1)} %all-to-all-done.mine_ref), channel_id=1, source_target_pairs={{0,1},{1,0},{2,3},{3,2},{4,5},{5,4},{6,7},{7,6},{8,9},{9,8},{10,11... | collective-permute-start | bytes 6291464 | tf_op jit(solution)/shard_map/ppermute | solution.py:369
  49.0 4.3 %copy-start.2 = (bf16[4096,128]{1,0:T(8,128)(2,1)S(1)}, bf16[4096,128]{1,0:T(8,128)(2,1)}, u32[]{:S(2)}) copy-start(bf16[4096,128]{1,0:T(8,128)(2,1)} %copy-done.1) | copy-start | bytes 3145732
  49.0 4.3 %copy-start.3 = (s32[4096]{0:T(1024)S(1)}, s32[4096]{0:T(1024)}, u32[]{:S(2)}) copy-start(s32[4096]{0:T(1024)} %param.15) | copy-start | bytes 49156
  53.3 24.9 %copy-start.4 = (f32[128]{0:T(128)S(1)}, f32[128]{0:T(128)}, u32[]{:S(2)}) copy-start(f32[128]{0:T(128)} %param.18) | copy-start | bytes 1540
  53.3 24.9 %copy-start.5 = (f32[128]{0:T(128)S(1)}, f32[128]{0:T(128)}, u32[]{:S(2)}) copy-start(f32[128]{0:T(128)} %param.19) | copy-start | bytes 1540
  60.0 1.2 %collective-permute-start.2 = (f32[2,128]{1,0:T(2,128)S(1)}, f32[2,128]{1,0:T(2,128)S(1)}, u32[]{:S(2)}, u32[]{:S(2)}) collective-permute-start(f32[2,128]{1,0:T(2,128)S(1)} %get-tuple-element.24), channel_id=1, source_target_pairs={{0,1},{1,0},{2,3},{3,2},{4,5},{5,4},{6,7},{7,6},{8,9},{9,8},{10,11... | collective-permute-start | bytes 3080 | tf_op jit(solution)/shard_map/ppermute | solution.py:383
  61.2 16.9 %collective-permute-start.3 = (f32[2048,128]{1,0:T(8,128)S(1)}, f32[2048,128]{1,0:T(8,128)S(1)}, u32[]{:S(2)}, u32[]{:S(2)}) collective-permute-start(f32[2048,128]{1,0:T(8,128)S(1)} %get-tuple-element.26), channel_id=1, source_target_pairs={{0,1},{1,0},{2,3},{3,2},{4,5},{5,4},{6,7},{7,6},{8,9},{9,8},{10,11... | collective-permute-start | bytes 3145736 | tf_op jit(solution)/shard_map/ppermute | solution.py:385

commit v8 on v7

--- a/solution.py
+++ b/solution.py
@@ -10,6 +10,7 @@
 RING = 4
 TILES_STEP = 4
 PAIR = 2
+OUT_PARTS = 4
 LOAD_PARTS = 4
 EPS = 1e-05
 BF16 = jnp.bfloat16
@@ -312,25 +313,32 @@
     )(core, tile_src, in_hbm(adj), degrees, weights, other, sibling, near, early)
 
 
-def normalise_kernel(core_ref, keep_ref, got_ref, parts_ref, gamma_ref, beta_ref, out_ref):
+def normalise_kernel(
+    core_ref, keep_ref, got_ref, parts_ref, gamma_ref, beta_ref, out_ref, done, sems
+):
     rows = keep_ref.shape[0]
+    count = 2.0 * rows
     parts = parts_ref[...]
-    members = 2.0 * parts.shape[0]
-    sums = jnp.concatenate([parts[:, 0, :], parts[:, 2, :]], axis=0)
-    spreads = jnp.concatenate([parts[:, 1, :], parts[:, 3, :]], axis=0)
-    mean = jnp.sum(sums, axis=0, keepdims=True) / (rows * members)
-    shift = sums / rows - mean
-    var = jnp.sum(spreads + rows * (shift * shift), axis=0, keepdims=True) / (rows * members)
+    members = parts.shape[0]
+    sums = parts[:, 0, :]
+    mean = jnp.sum(sums, axis=0, keepdims=True) / (count * members)
+    shift = sums / count - mean
+    spreads = parts[:, 1, :] + count * (shift * shift)
+    var = jnp.sum(spreads, axis=0, keepdims=True) / (count * members)
     scale = gamma_ref[...] / jnp.sqrt(var + EPS)
     beta = beta_ref[...]
-    here = pl.multiple_of(core_ref[0] * rows, rows)
-    there = pl.multiple_of((1 - core_ref[0]) * rows, rows)
-    out_ref[pl.ds(here, rows), :] = jnp.maximum(
-        (keep_ref[...] - mean) * scale + beta, 0.0
-    ).astype(BF16)
-    out_ref[pl.ds(there, rows), :] = jnp.maximum(
-        (got_ref[...] - mean) * scale + beta, 0.0
-    ).astype(BF16)
+    size = rows // OUT_PARTS
+    copies = []
+    for values_ref, core in ((keep_ref, core_ref[0]), (got_ref, 1 - core_ref[0])):
+        for q in range(OUT_PARTS):
+            n = len(copies)
+            values = (values_ref[q * size : (q + 1) * size, :] - mean) * scale + beta
+            done[n] = jnp.maximum(values, 0.0).astype(BF16)
+            at = pl.ds(pl.multiple_of(core * rows + q * size, size), size)
+            copies.append(pltpu.make_async_copy(done.at[n], out_ref.at[at, :], sems.at[n]))
+            copies[n].start()
+    for copy in copies:
+        copy.wait()
 
 
 def normalise(core, keep, got, parts, gamma, beta):
@@ -339,8 +347,12 @@
     return pl.pallas_call(
         normalise_kernel,
         in_specs=[pl.BlockSpec(memory_space=pltpu.SMEM)] + [whole] * 5,
-        out_specs=whole,
+        out_specs=pl.BlockSpec(memory_space=pltpu.HBM),
         out_shape=jax.ShapeDtypeStruct((2 * rows, half), BF16),
+        scratch_shapes=[
+            pltpu.VMEM((2 * OUT_PARTS, rows // OUT_PARTS, half), BF16),
+            pltpu.SemaphoreType.DMA((2 * OUT_PARTS,)),
+        ],
         compiler_params=pltpu.CompilerParams(vmem_limit_bytes=8 * 2**20),
         name="normalise",
     )(core, keep, got, parts, gamma.reshape(1, half), beta.reshape(1, half))
@@ -358,8 +370,9 @@
 
     outgoing = pick_rows(send_rows, send_counts, features)
     mine = lax.all_to_all(outgoing, "dom", split_axis=0, concat_axis=0, tiled=True)
-    other = lax.ppermute(features, "feat", swap)
     adj = adjacency(core_arg, edge_codes, tiles)
+    late_features, adj = lax.optimization_barrier((features, adj))
+    other = lax.ppermute(late_features, "feat", swap)
 
     def turned(w):
         return jnp.where(core == 0, w, jnp.roll(w, (half, half), (0, 1)))
@@ -383,7 +396,10 @@
     got_stats = lax.ppermute(send_stats, "feat", swap)
     got_stats, send = lax.optimization_barrier((got_stats, send))
     got = lax.ppermute(send, "feat", swap)
-    stats = jnp.concatenate([keep_stats, got_stats], axis=0)
+    apart = keep_stats[0:1] - got_stats[0:1]
+    both = keep_stats + got_stats
+    spread = both[1:2] + apart * apart / (2.0 * keep.shape[0])
+    stats = jnp.concatenate([both[0:1], spread], axis=0)
     stats = jnp.broadcast_to(stats[None], (peers,) + stats.shape)
     parts = lax.all_to_all(stats, "dom", split_axis=0, concat_axis=0, tiled=True)
     return normalise(core_arg, keep, got, parts, gamma, beta)

time: 79.9 us -> 77.1 us (0.965)
  blocking collectives: 16.7 us -> 14.8 us
    all_to_all x1, waiting for transfers between devices: 15.5 us -> 12.5 us  [local(): lax.all_to_all(outgoing, 'dom', split_axis=0, concat_axis=0, tiled=True)]
    ppermute x1, waiting for transfers between devices: 0.01 us -> 2.46 us  [local(): other = lax.ppermute(late_features, 'feat', swap)]
    all_to_all x1, blocking collectives: 16.7 us -> 14.8 us  [local(): lax.all_to_all(stats, 'dom', split_axis=0, concat_axis=0, tiled=True)]
  transfers between devices with their start and end apart: 5 -> 5, of which waited for: 3 -> 4; matrix products, arithmetic and copies ran while one was open for 0% -> 0% of each run, Pallas kernels for 30% -> 22%
where the time goes in v8:
time: 77.1 us; the launch traced here: 76.8 us
  Pallas kernels  31.8 us (41%)
  waiting for transfers between devices  16.6 us (22%)
  blocking collectives  14.8 us (19%)
  starting transfers between devices  12.2 us (16%)
  local copies, waits for them, and re-layouts  1.12 us (1%)
    all_to_all x1, blocking collectives, local(): lax.all_to_all(stats, 'dom', split_axis=0, concat_axis=0, tiled=True)  14.8 us
    pallas_call x1, Pallas kernels, adjacency(): pl.pallas_call(adjacency_kernel, grid_spec=pltpu.PrefetchScalarGridSpec(n...  13.3 us
    all_to_all x1, waiting for transfers between devices, local(): lax.all_to_all(outgoing, 'dom', split_axis=0, concat_axis=0, tiled=True)  12.5 us
    all_to_all x1, starting transfers between devices, local(): lax.all_to_all(outgoing, 'dom', split_axis=0, concat_axis=0, tiled=True)  11.8 us
    pallas_call x1, Pallas kernels, pick_rows(): pl.pallas_call(pick_kernel, in_specs=[hbm, hbm, hbm], out_specs=hbm, out_...  7.04 us
    pallas_call x1, Pallas kernels, aggregate(): pl.pallas_call(aggregate_kernel, in_specs=[smem, smem, hbm, vmem, vmem, a...  6.67 us
    pallas_call x1, Pallas kernels, stage(): pl.pallas_call(stage_kernel, in_specs=[pl.BlockSpec(memory_space=pl.ANY),...  3.62 us
    ppermute x1, waiting for transfers between devices, local(): other = lax.ppermute(late_features, 'feat', swap)  2.46 us
  transfers between devices with their start and end apart: 5, of which 4 were waited for; matrix products, arithmetic and copies ran while one was open for 0% of the time, Pallas kernels for 22%

profile of v8, /device:TPU:0, one launch (start us, length us, event | category | flops | bytes accessed | tf_op | source)
XLA Modules:
  0.0 76.8 jit_solution(5989884715746573680)
XLA Ops:
  0.0 7.0 %pick_rows.1 = bf16[64,128,128]{2,1,0:T(8,128)(2,1)} custom-call(s32[1,64,128]{2,1,0:T(8,128)} %rows_ref.1, s32[1,64]{1,0:T(1,128)} %counts_ref.1, bf16[4096,128]{1,0:T(8,128)(2,1)} %own_ref.1), custom_call_target="tpu_custom_call" | custom-call | tf_op jit(solution)/shard_map/pick_rows/pallas_call | solution.py:96
  7.0 11.8 %all-to-all-start = ((bf16[64,128,128]{2,1,0:T(8,128)(2,1)}), bf16[64,128,128]{2,1,0:T(8,128)(2,1)}, u32[]{:S(2)}, u32[]{:S(2)}) async-start(bf16[64,128,128]{2,1,0:T(8,128)(2,1)} %pick_rows.1), calls=%async_computation | async-start | bytes 4194304 | tf_op jit(solution)/shard_map/all_to_all | solution.py:372
  18.8 0.0 copy-start
  18.8 0.0 copy-start.7
  18.9 0.0 copy-start.6
  18.9 13.3 %adjacency.1.adj_ref = bf16[16,128,3072]{2,1,0:T(8,128)(2,1)} custom-call(s32[1]{0:T(128)} %bitcast.core_ref, s32[32,24,512]{2,1,0:T(8,128)} %codes_ref.1), custom_call_target="tpu_custom_call" | custom-call | flops 12884901888 | bytes 13369344 | tf_op jit(solution)/shard_map/adjacency/pallas_call | solution.py:144
  32.1 0.0 copy-done
  32.1 0.0 copy-start.8
  32.1 0.0 collective-permute-start
  32.2 0.0 copy-done.7
  32.2 0.0 copy-done.6
  32.3 0.1 fusion.1
  32.4 2.5 %collective-permute-done = bf16[4096,128]{1,0:T(8,128)(2,1)S(1)} collective-permute-done((bf16[4096,128]{1,0:T(8,128)(2,1)S(1)}, bf16[4096,128]{1,0:T(8,128)(2,1)S(1)}, u32[]{:S(2)}, u32[]{:S(2)}) %collective-permute-start) | collective-permute-done | bytes 1048608 | tf_op jit(solution)/shard_map/ppermute | solution.py:375
  34.8 0.0 copy-start.1
  34.8 1.0 %copy-done.1 = bf16[4096,128]{1,0:T(8,128)(2,1)} copy-done((bf16[4096,128]{1,0:T(8,128)(2,1)}, bf16[4096,128]{1,0:T(8,128)(2,1)S(1)}, u32[]{:S(2)}) %copy-start.1) | copy-done | bytes 1048600
  35.8 12.5 %all-to-all-done.mine_ref = bf16[64,128,128]{2,1,0:T(8,128)(2,1)} async-done(((bf16[64,128,128]{2,1,0:T(8,128)(2,1)}), bf16[64,128,128]{2,1,0:T(8,128)(2,1)}, u32[]{:S(2)}, u32[]{:S(2)}) %all-to-all-start) | async-done | bytes 2097184 | tf_op jit(solution)/shard_map/all_to_all | solution.py:372
  48.3 0.0 collective-permute-start.1
  48.3 0.0 copy-done.8
  48.3 0.1 copy.11.tile_src_ref
  48.3 0.0 copy-start.2
  48.4 0.0 copy-start.3
  48.4 3.6 %stage.1 = (bf16[96,128,128]{2,1,0:T(8,128)(2,1)S(1)}, bf16[8,128,3072]{2,1,0:T(8,128)(2,1)S(1)}) custom-call(bf16[32,128,128]{2,1,0:T(8,128)(2,1)S(1)} %bitcast.6, bf16[64,128,128]{2,1,0:T(8,128)(2,1)} %all-to-all-done.mine_ref, bf16[16,128,3072]{2,1,0:T(8,128)(2,1)} %adjacency.1.adj_ref), custom_call_target="tpu_custom_call" | custom-call | tf_op jit(solution)/shard_map/stage/pallas_call | solution.py:186
  52.0 0.7 collective-permute-done.1.sibling_ref
  52.6 0.0 copy-done.2
  52.6 0.0 copy-done.3
  52.6 0.0 copy-start.4
  52.6 0.0 copy-start.5
  52.7 6.7 %aggregate.1 = (f32[2048,128]{1,0:T(8,128)S(1)}, f32[2048,128]{1,0:T(8,128)S(1)}, f32[2,128]{1,0:T(2,128)S(1)}, f32[2,128]{1,0:T(2,128)S(1)}) custom-call(s32[1]{0:T(128)} %bitcast.core_ref, s32[32,24]{1,0:T(8,128)S(1)} %copy.11.tile_src_ref, bf16[16,128,3072]{2,1,0:T(8,128)(2,1)} %adjacency.1.adj_ref, s32[32,1,128]{2,1,0:T(1,128)S(1)} %bitcast.8, ...), custom_call_target="tpu_custom_call" | custom-call | tf_op jit(solution)/shard_map/aggregate/pallas_call | solution.py:300
  59.3 0.2 collective-permute-start.2
  59.5 1.0 %collective-permute-done.2 = f32[2,128]{1,0:T(2,128)S(1)} collective-permute-done((f32[2,128]{1,0:T(2,128)S(1)}, f32[2,128]{1,0:T(2,128)S(1)}, u32[]{:S(2)}, u32[]{:S(2)}) %collective-permute-start.2) | collective-permute-done | bytes 1056 | tf_op jit(solution)/shard_map/ppermute | solution.py:396
  60.6 0.2 collective-permute-start.3
  60.8 14.8 %all_to_all.10.parts_ref = f32[64,2,128]{2,1,0:T(2,128)S(1)} all-to-all(f32[64,2,128]{2,1,0:T(2,128)S(1)} %broadcast_in_dim.2), channel_id=1, replica_groups=mesh['dom'=64,'feat'=2] {'dom'}, dimensions={0} | all-to-all | bytes 131072 | tf_op jit(solution)/shard_map/all_to_all | solution.py:404
  75.6 0.0 collective-permute-done.3.got_ref
  75.6 0.0 copy-done.4
  75.6 0.0 copy-done.5
  75.6 1.2 %normalise.1 = bf16[4096,128]{1,0:T(8,128)(2,1)} custom-call(s32[1]{0:T(128)} %bitcast.core_ref, f32[2048,128]{1,0:T(8,128)S(1)} %get-tuple-element.27.keep_ref, f32[2048,128]{1,0:T(8,128)S(1)} %collective-permute-done.3.got_ref, f32[64,2,128]{2,1,0:T(2,128)S(1)} %all_to_all.10.parts_ref, f32[1,128]{1,0:T(1,128)S(1)} %bitcast.9, f32[1,128]{1,0:T(1,128)S(1)} %bitcast.10), custom_call_target="tpu_custom_call" | custom-call | tf_op jit(solution)/shard_map/normalise/pallas_call | solution.py:347
  (9 shorter events, 0.1 us)
Async XLA Ops:
  7.0 41.2 %all-to-all-start = ((bf16[64,128,128]{2,1,0:T(8,128)(2,1)}), bf16[64,128,128]{2,1,0:T(8,128)(2,1)}, u32[]{:S(2)}, u32[]{:S(2)}) async-start(bf16[64,128,128]{2,1,0:T(8,128)(2,1)} %pick_rows.1), calls=%async_computation | async-start | bytes 4194304 | tf_op jit(solution)/shard_map/all_to_all | solution.py:372
  18.8 13.3 %copy-start = (bf16[4096,128]{1,0:T(8,128)(2,1)S(1)}, bf16[4096,128]{1,0:T(8,128)(2,1)}, u32[]{:S(2)}) copy-start(bf16[4096,128]{1,0:T(8,128)(2,1)} %own_ref.1) | copy-start | bytes 3145732
  18.8 13.3 %copy-start.7 = (bf16[256,256]{1,0:T(8,128)(2,1)S(1)}, bf16[256,256]{1,0:T(8,128)(2,1)}, u32[]{:S(2)}) copy-start(bf16[256,256]{1,0:T(8,128)(2,1)} %param.16) | copy-start | bytes 393220
  18.9 13.4 %copy-start.6 = (bf16[256,256]{1,0:T(8,128)(2,1)S(1)}, bf16[256,256]{1,0:T(8,128)(2,1)}, u32[]{:S(2)}) copy-start(bf16[256,256]{1,0:T(8,128)(2,1)} %param.17) | copy-start | bytes 393220
  32.1 16.1 %copy-start.8 = (s32[32,24]{0,1:T(8,128)S(1)}, s32[32,24]{0,1:T(8,128)}, u32[]{:S(2)}) copy-start(s32[32,24]{0,1:T(8,128)} %param.13) | copy-start | bytes 9220
  32.1 2.7 %collective-permute-start = (bf16[4096,128]{1,0:T(8,128)(2,1)S(1)}, bf16[4096,128]{1,0:T(8,128)(2,1)S(1)}, u32[]{:S(2)}, u32[]{:S(2)}) collective-permute-start(bf16[4096,128]{1,0:T(8,128)(2,1)S(1)} %copy-done), channel_id=1, source_target_pairs={{0,1},{1,0},{2,3},{3,2},{4,5},{5,4},{6,7},{7,6},{8,9},{9,8},{10,11... | collective-permute-start | bytes 3145736 | tf_op jit(solution)/shard_map/ppermute | solution.py:375
  34.8 1.0 %copy-start.1 = (bf16[4096,128]{1,0:T(8,128)(2,1)}, bf16[4096,128]{1,0:T(8,128)(2,1)S(1)}, u32[]{:S(2)}) copy-start(bf16[4096,128]{1,0:T(8,128)(2,1)S(1)} %collective-permute-done) | copy-start | bytes 3145732
  48.3 4.4 %collective-permute-start.1 = (bf16[64,128,128]{2,1,0:T(8,128)(2,1)}, bf16[64,128,128]{2,1,0:T(8,128)(2,1)S(1)}, u32[]{:S(2)}, u32[]{:S(2)}) collective-permute-start(bf16[64,128,128]{2,1,0:T(8,128)(2,1)} %all-to-all-done.mine_ref), channel_id=1, source_target_pairs={{0,1},{1,0},{2,3},{3,2},{4,5},{5,4},{6,7},{7,6},{8,9},{9,8},{10,11... | collective-permute-start | bytes 6291464 | tf_op jit(solution)/shard_map/ppermute | solution.py:382
  48.3 4.3 %copy-start.2 = (bf16[4096,128]{1,0:T(8,128)(2,1)S(1)}, bf16[4096,128]{1,0:T(8,128)(2,1)}, u32[]{:S(2)}) copy-start(bf16[4096,128]{1,0:T(8,128)(2,1)} %copy-done.1) | copy-start | bytes 3145732
  48.4 4.3 %copy-start.3 = (s32[4096]{0:T(1024)S(1)}, s32[4096]{0:T(1024)}, u32[]{:S(2)}) copy-start(s32[4096]{0:T(1024)} %param.15) | copy-start | bytes 49156
  52.6 23.0 %copy-start.4 = (f32[128]{0:T(128)S(1)}, f32[128]{0:T(128)}, u32[]{:S(2)}) copy-start(f32[128]{0:T(128)} %param.18) | copy-start | bytes 1540
  52.6 23.0 %copy-start.5 = (f32[128]{0:T(128)S(1)}, f32[128]{0:T(128)}, u32[]{:S(2)}) copy-start(f32[128]{0:T(128)} %param.19) | copy-start | bytes 1540
  59.3 1.2 %collective-permute-start.2 = (f32[2,128]{1,0:T(2,128)S(1)}, f32[2,128]{1,0:T(2,128)S(1)}, u32[]{:S(2)}, u32[]{:S(2)}) collective-permute-start(f32[2,128]{1,0:T(2,128)S(1)} %get-tuple-element.28), channel_id=1, source_target_pairs={{0,1},{1,0},{2,3},{3,2},{4,5},{5,4},{6,7},{7,6},{8,9},{9,8},{10,11... | collective-permute-start | bytes 3080 | tf_op jit(solution)/shard_map/ppermute | solution.py:396
  60.6 15.1 %collective-permute-start.3 = (f32[2048,128]{1,0:T(8,128)S(1)}, f32[2048,128]{1,0:T(8,128)S(1)}, u32[]{:S(2)}, u32[]{:S(2)}) collective-permute-start(f32[2048,128]{1,0:T(8,128)S(1)} %get-tuple-element.30), channel_id=1, source_target_pairs={{0,1},{1,0},{2,3},{3,2},{4,5},{5,4},{6,7},{7,6},{8,9},{9,8},{10,11... | collective-permute-start | bytes 3145736 | tf_op jit(solution)/shard_map/ppermute | solution.py:398

commit v9 on v8

--- a/solution.py
+++ b/solution.py
@@ -213,8 +213,7 @@
     early,
     keep_ref,
     send_ref,
-    keep_stats_ref,
-    send_stats_ref,
+    stats_ref,
     far,
     late,
     sems,
@@ -279,13 +278,13 @@
     sums = jnp.zeros((1, 2 * half), F32)
     sums = lax.fori_loop(0, ahead // TILES_STEP, early_step, sums)
     sums = lax.fori_loop(0, (tiles - ahead) // TILES_STEP, late_step, sums)
-    for values_ref, stats_ref, total in (
-        (keep_ref, keep_stats_ref, sums[:, :half]),
-        (send_ref, send_stats_ref, sums[:, half:]),
+    for values_ref, owner, total in (
+        (keep_ref, core, sums[:, :half]),
+        (send_ref, 1 - core, sums[:, half:]),
     ):
         centred = values_ref[...] - total / values_ref.shape[0]
-        stats_ref[0:1, :] = total
-        stats_ref[1:2, :] = jnp.sum(centred * centred, axis=0, keepdims=True)
+        spread = jnp.sum(centred * centred, axis=0, keepdims=True)
+        stats_ref[owner] = jnp.concatenate([total, spread], axis=0)
 
 
 def aggregate(core, tile_src, adj, degrees, weights, other, sibling, near, early):
@@ -300,9 +299,9 @@
     return pl.pallas_call(
         aggregate_kernel,
         in_specs=[smem, smem, hbm, vmem, vmem, anywhere, anywhere, vmem, vmem],
-        out_specs=[vmem] * 4,
+        out_specs=[vmem] * 3,
         out_shape=[jax.ShapeDtypeStruct((rows, half), F32)] * 2
-        + [jax.ShapeDtypeStruct((2, half), F32)] * 2,
+        + [jax.ShapeDtypeStruct((2, 2, half), F32)],
         scratch_shapes=[
             pltpu.VMEM(near.shape, BF16),
             pltpu.VMEM((late,) + adj.shape[1:], BF16),
@@ -317,7 +316,7 @@
     core_ref, keep_ref, got_ref, parts_ref, gamma_ref, beta_ref, out_ref, done, sems
 ):
     rows = keep_ref.shape[0]
-    count = 2.0 * rows
+    count = float(rows)
     parts = parts_ref[...]
     members = parts.shape[0]
     sums = parts[:, 0, :]
@@ -382,7 +381,7 @@
     sibling = lax.ppermute(mine, "feat", swap)
     other = other.reshape(-1, TILE, half)
     near, early = stage(features.reshape(-1, TILE, half), in_hbm(mine), adj)
-    keep, send, keep_stats, send_stats = aggregate(
+    keep, send, stats = aggregate(
         core_arg,
         tile_src,
         adj,
@@ -393,15 +392,10 @@
         near,
         early,
     )
-    got_stats = lax.ppermute(send_stats, "feat", swap)
-    got_stats, send = lax.optimization_barrier((got_stats, send))
     got = lax.ppermute(send, "feat", swap)
-    apart = keep_stats[0:1] - got_stats[0:1]
-    both = keep_stats + got_stats
-    spread = both[1:2] + apart * apart / (2.0 * keep.shape[0])
-    stats = jnp.concatenate([both[0:1], spread], axis=0)
     stats = jnp.broadcast_to(stats[None], (peers,) + stats.shape)
-    parts = lax.all_to_all(stats, "dom", split_axis=0, concat_axis=0, tiled=True)
+    stats = stats.reshape(2 * peers, 2, half)
+    parts = lax.all_to_all(stats, ("dom", "feat"), split_axis=0, concat_axis=0, tiled=True)
     return normalise(core_arg, keep, got, parts, gamma, beta)
 
 

time: 77.1 us -> 76.3 us (0.990)
  waiting for transfers between devices: 16.6 us -> 15.6 us
    ppermute x1 -> x0, waiting for transfers between devices: 1.01 us -> none  [local(): got_stats = lax.ppermute(send_stats, 'feat', swap)]
  transfers between devices with their start and end apart: 5 -> 4, of which waited for: 4 -> 3; matrix products, arithmetic and copies ran while one was open for 0% -> 0% of each run, Pallas kernels for 22% -> 22%
where the time goes in v9:
time: 76.3 us; the launch traced here: 75.3 us
  Pallas kernels  31.8 us (42%)
  waiting for transfers between devices  15.6 us (20%)
  blocking collectives  14.5 us (19%)
  starting transfers between devices  12 us (16%)
  local copies, waits for them, and re-layouts  1.14 us (1%)
    all_to_all x1, blocking collectives, local(): lax.all_to_all(stats, ('dom', 'feat'), split_axis=0, concat_axis=0, tiled...  14.5 us
    pallas_call x1, Pallas kernels, adjacency(): pl.pallas_call(adjacency_kernel, grid_spec=pltpu.PrefetchScalarGridSpec(n...  13.3 us
    all_to_all x1, waiting for transfers between devices, local(): lax.all_to_all(outgoing, 'dom', split_axis=0, concat_axis=0, tiled=True)  12.5 us
    all_to_all x1, starting transfers between devices, local(): lax.all_to_all(outgoing, 'dom', split_axis=0, concat_axis=0, tiled=True)  11.8 us
    pallas_call x1, Pallas kernels, pick_rows(): pl.pallas_call(pick_kernel, in_specs=[hbm, hbm, hbm], out_specs=hbm, out_...  7.01 us
    pallas_call x1, Pallas kernels, aggregate(): pl.pallas_call(aggregate_kernel, in_specs=[smem, smem, hbm, vmem, vmem, a...  6.66 us
    pallas_call x1, Pallas kernels, stage(): pl.pallas_call(stage_kernel, in_specs=[pl.BlockSpec(memory_space=pl.ANY),...  3.62 us
    ppermute x1, waiting for transfers between devices, local(): other = lax.ppermute(late_features, 'feat', swap)  2.46 us
  transfers between devices with their start and end apart: 4, of which 3 were waited for; matrix products, arithmetic and copies ran while one was open for 0% of the time, Pallas kernels for 22%

profile of v9, /device:TPU:0, one launch (start us, length us, event | category | flops | bytes accessed | tf_op | source)
XLA Modules:
  0.0 75.3 jit_solution(12995589169731516648)
XLA Ops:
  0.0 7.0 %pick_rows.1 = bf16[64,128,128]{2,1,0:T(8,128)(2,1)} custom-call(s32[1,64,128]{2,1,0:T(8,128)} %rows_ref.1, s32[1,64]{1,0:T(1,128)} %counts_ref.1, bf16[4096,128]{1,0:T(8,128)(2,1)} %own_ref.1), custom_call_target="tpu_custom_call" | custom-call | tf_op jit(solution)/shard_map/pick_rows/pallas_call | solution.py:96
  7.0 11.8 %all-to-all-start = ((bf16[64,128,128]{2,1,0:T(8,128)(2,1)}), bf16[64,128,128]{2,1,0:T(8,128)(2,1)}, u32[]{:S(2)}, u32[]{:S(2)}) async-start(bf16[64,128,128]{2,1,0:T(8,128)(2,1)} %pick_rows.1), calls=%async_computation | async-start | bytes 4194304 | tf_op jit(solution)/shard_map/all_to_all | solution.py:371
  18.8 0.0 copy-start
  18.8 0.0 copy-start.7
  18.8 0.0 copy-start.6
  18.8 13.3 %adjacency.1.adj_ref = bf16[16,128,3072]{2,1,0:T(8,128)(2,1)} custom-call(s32[1]{0:T(128)} %bitcast.core_ref, s32[32,24,512]{2,1,0:T(8,128)} %codes_ref.1), custom_call_target="tpu_custom_call" | custom-call | flops 12884901888 | bytes 13369344 | tf_op jit(solution)/shard_map/adjacency/pallas_call | solution.py:144
  32.1 0.0 copy-done
  32.1 0.0 copy-start.8
  32.1 0.0 collective-permute-start
  32.1 0.0 copy-done.7
  32.2 0.0 copy-done.6
  32.2 0.1 fusion.1
  32.3 2.5 %collective-permute-done = bf16[4096,128]{1,0:T(8,128)(2,1)S(1)} collective-permute-done((bf16[4096,128]{1,0:T(8,128)(2,1)S(1)}, bf16[4096,128]{1,0:T(8,128)(2,1)S(1)}, u32[]{:S(2)}, u32[]{:S(2)}) %collective-permute-start) | collective-permute-done | bytes 1048608 | tf_op jit(solution)/shard_map/ppermute | solution.py:374
  34.8 0.0 copy-start.1
  34.8 1.0 %copy-done.1 = bf16[4096,128]{1,0:T(8,128)(2,1)} copy-done((bf16[4096,128]{1,0:T(8,128)(2,1)}, bf16[4096,128]{1,0:T(8,128)(2,1)S(1)}, u32[]{:S(2)}) %copy-start.1) | copy-done | bytes 1048600
  35.7 12.5 %all-to-all-done.mine_ref = bf16[64,128,128]{2,1,0:T(8,128)(2,1)} async-done(((bf16[64,128,128]{2,1,0:T(8,128)(2,1)}), bf16[64,128,128]{2,1,0:T(8,128)(2,1)}, u32[]{:S(2)}, u32[]{:S(2)}) %all-to-all-start) | async-done | bytes 2097184 | tf_op jit(solution)/shard_map/all_to_all | solution.py:371
  48.3 0.0 collective-permute-start.1
  48.3 0.0 copy-done.8
  48.3 0.1 copy.11.tile_src_ref
  48.3 0.0 copy-start.2
  48.3 0.0 copy-start.3
  48.3 3.6 %stage.1 = (bf16[96,128,128]{2,1,0:T(8,128)(2,1)S(1)}, bf16[8,128,3072]{2,1,0:T(8,128)(2,1)S(1)}) custom-call(bf16[32,128,128]{2,1,0:T(8,128)(2,1)S(1)} %bitcast.7, bf16[64,128,128]{2,1,0:T(8,128)(2,1)} %all-to-all-done.mine_ref, bf16[16,128,3072]{2,1,0:T(8,128)(2,1)} %adjacency.1.adj_ref), custom_call_target="tpu_custom_call" | custom-call | tf_op jit(solution)/shard_map/stage/pallas_call | solution.py:186
  52.0 0.7 collective-permute-done.1.sibling_ref
  52.6 0.0 copy-done.2
  52.6 0.0 copy-done.3
  52.6 0.0 copy-start.4
  52.6 0.0 copy-start.5
  52.6 6.7 %aggregate.1 = (f32[2048,128]{1,0:T(8,128)S(1)}, f32[2048,128]{1,0:T(8,128)S(1)}, f32[2,2,128]{2,1,0:T(2,128)S(1)}) custom-call(s32[1]{0:T(128)} %bitcast.core_ref, s32[32,24]{1,0:T(8,128)S(1)} %copy.11.tile_src_ref, bf16[16,128,3072]{2,1,0:T(8,128)(2,1)} %adjacency.1.adj_ref, s32[32,1,128]{2,1,0:T(1,128)S(1)} %bitcast.9, ...), custom_call_target="tpu_custom_call" | custom-call | tf_op jit(solution)/shard_map/aggregate/pallas_call | solution.py:299
  59.3 0.2 collective-permute-start.2
  59.5 14.5 %all_to_all.10.parts_ref = f32[128,2,128]{2,1,0:T(2,128)S(1)} all-to-all(f32[128,2,128]{2,1,0:T(2,128)S(1)} %bitcast.12), channel_id=1, replica_groups=mesh['dom'=64,'feat'=2] {'dom','feat'}, dimensions={0} | all-to-all | bytes 262144 | tf_op jit(solution)/shard_map/all_to_all | solution.py:398
  74.0 0.0 collective-permute-done.2.got_ref
  74.0 0.0 copy-done.4
  74.0 0.0 copy-done.5
  74.0 1.3 %normalise.1 = bf16[4096,128]{1,0:T(8,128)(2,1)} custom-call(s32[1]{0:T(128)} %bitcast.core_ref, f32[2048,128]{1,0:T(8,128)S(1)} %get-tuple-element.24.keep_ref, f32[2048,128]{1,0:T(8,128)S(1)} %collective-permute-done.2.got_ref, f32[128,2,128]{2,1,0:T(2,128)S(1)} %all_to_all.10.parts_ref, f32[1,128]{1,0:T(1,128)S(1)} %bitcast.10, f32[1,128]{1,0:T(1,128)S(1)} %bitcast.11), custom_call_target="tpu_custom_call" | custom-call | tf_op jit(solution)/shard_map/normalise/pallas_call | solution.py:346
  (6 shorter events, 0.1 us)
Async XLA Ops:
  7.0 41.2 %all-to-all-start = ((bf16[64,128,128]{2,1,0:T(8,128)(2,1)}), bf16[64,128,128]{2,1,0:T(8,128)(2,1)}, u32[]{:S(2)}, u32[]{:S(2)}) async-start(bf16[64,128,128]{2,1,0:T(8,128)(2,1)} %pick_rows.1), calls=%async_computation | async-start | bytes 4194304 | tf_op jit(solution)/shard_map/all_to_all | solution.py:371
  18.8 13.3 %copy-start = (bf16[4096,128]{1,0:T(8,128)(2,1)S(1)}, bf16[4096,128]{1,0:T(8,128)(2,1)}, u32[]{:S(2)}) copy-start(bf16[4096,128]{1,0:T(8,128)(2,1)} %own_ref.1) | copy-start | bytes 3145732
  18.8 13.3 %copy-start.7 = (bf16[256,256]{1,0:T(8,128)(2,1)S(1)}, bf16[256,256]{1,0:T(8,128)(2,1)}, u32[]{:S(2)}) copy-start(bf16[256,256]{1,0:T(8,128)(2,1)} %param.16) | copy-start | bytes 393220
  18.8 13.3 %copy-start.6 = (bf16[256,256]{1,0:T(8,128)(2,1)S(1)}, bf16[256,256]{1,0:T(8,128)(2,1)}, u32[]{:S(2)}) copy-start(bf16[256,256]{1,0:T(8,128)(2,1)} %param.17) | copy-start | bytes 393220
  32.1 16.1 %copy-start.8 = (s32[32,24]{0,1:T(8,128)S(1)}, s32[32,24]{0,1:T(8,128)}, u32[]{:S(2)}) copy-start(s32[32,24]{0,1:T(8,128)} %param.13) | copy-start | bytes 9220
  32.1 2.7 %collective-permute-start = (bf16[4096,128]{1,0:T(8,128)(2,1)S(1)}, bf16[4096,128]{1,0:T(8,128)(2,1)S(1)}, u32[]{:S(2)}, u32[]{:S(2)}) collective-permute-start(bf16[4096,128]{1,0:T(8,128)(2,1)S(1)} %copy-done), channel_id=1, source_target_pairs={{0,1},{1,0},{2,3},{3,2},{4,5},{5,4},{6,7},{7,6},{8,9},{9,8},{10,11... | collective-permute-start | bytes 3145736 | tf_op jit(solution)/shard_map/ppermute | solution.py:374
  34.8 1.0 %copy-start.1 = (bf16[4096,128]{1,0:T(8,128)(2,1)}, bf16[4096,128]{1,0:T(8,128)(2,1)S(1)}, u32[]{:S(2)}) copy-start(bf16[4096,128]{1,0:T(8,128)(2,1)S(1)} %collective-permute-done) | copy-start | bytes 3145732
  48.3 4.4 %collective-permute-start.1 = (bf16[64,128,128]{2,1,0:T(8,128)(2,1)}, bf16[64,128,128]{2,1,0:T(8,128)(2,1)S(1)}, u32[]{:S(2)}, u32[]{:S(2)}) collective-permute-start(bf16[64,128,128]{2,1,0:T(8,128)(2,1)} %all-to-all-done.mine_ref), channel_id=1, source_target_pairs={{0,1},{1,0},{2,3},{3,2},{4,5},{5,4},{6,7},{7,6},{8,9},{9,8},{10,11... | collective-permute-start | bytes 6291464 | tf_op jit(solution)/shard_map/ppermute | solution.py:381
  48.3 4.3 %copy-start.2 = (bf16[4096,128]{1,0:T(8,128)(2,1)S(1)}, bf16[4096,128]{1,0:T(8,128)(2,1)}, u32[]{:S(2)}) copy-start(bf16[4096,128]{1,0:T(8,128)(2,1)} %copy-done.1) | copy-start | bytes 3145732
  48.3 4.3 %copy-start.3 = (s32[4096]{0:T(1024)S(1)}, s32[4096]{0:T(1024)}, u32[]{:S(2)}) copy-start(s32[4096]{0:T(1024)} %param.15) | copy-start | bytes 49156
  52.6 21.4 %copy-start.4 = (f32[128]{0:T(128)S(1)}, f32[128]{0:T(128)}, u32[]{:S(2)}) copy-start(f32[128]{0:T(128)} %param.18) | copy-start | bytes 1540
  52.6 21.4 %copy-start.5 = (f32[128]{0:T(128)S(1)}, f32[128]{0:T(128)}, u32[]{:S(2)}) copy-start(f32[128]{0:T(128)} %param.19) | copy-start | bytes 1540
  59.3 14.7 %collective-permute-start.2 = (f32[2048,128]{1,0:T(8,128)S(1)}, f32[2048,128]{1,0:T(8,128)S(1)}, u32[]{:S(2)}, u32[]{:S(2)}) collective-permute-start(f32[2048,128]{1,0:T(8,128)S(1)} %get-tuple-element.25), channel_id=1, source_target_pairs={{0,1},{1,0},{2,3},{3,2},{4,5},{5,4},{6,7},{7,6},{8,9},{9,8},{10,11... | collective-permute-start | bytes 3145736 | tf_op jit(solution)/shard_map/ppermute | solution.py:395

commit v10 on v9

--- a/solution.py
+++ b/solution.py
@@ -214,13 +214,11 @@
     keep_ref,
     send_ref,
     stats_ref,
-    far,
     late,
     sems,
 ):
     per_tile = tile_src_ref.shape[1]
     own_tiles, _, half = other_ref.shape
-    peers = sibling_ref.shape[0]
     tiles = adj_ref.shape[0]
     ahead = early.shape[0]
     core = core_ref[0]
@@ -228,19 +226,16 @@
     def late_copy(t):
         return pltpu.make_async_copy(adj_ref.at[ahead + t], late.at[t], sems.at[2 + t])
 
-    copies = [
-        pltpu.make_async_copy(other_ref, far.at[pl.ds(0, own_tiles)], sems.at[0]),
-        pltpu.make_async_copy(sibling_ref, far.at[pl.ds(own_tiles, peers)], sems.at[1]),
-    ]
-    for copy in copies:
-        copy.start()
-    for copy in copies:
-        copy.wait()
     for t in range(tiles - ahead):
         late_copy(t).start()
 
     def source(number):
-        return jnp.concatenate([near[number], far[number]], axis=1)
+        far = jnp.where(
+            number < own_tiles,
+            other_ref[jnp.minimum(number, own_tiles - 1)],
+            sibling_ref[jnp.maximum(number - own_tiles, 0)],
+        )
+        return jnp.concatenate([near[number], far], axis=1)
 
     def block(counts, base, at, sums):
         inputs = []
@@ -294,16 +289,14 @@
     rows = tiles * TILE
     smem = pl.BlockSpec(memory_space=pltpu.SMEM)
     vmem = pl.BlockSpec(memory_space=pltpu.VMEM)
-    anywhere = pl.BlockSpec(memory_space=pl.ANY)
     hbm = pl.BlockSpec(memory_space=pltpu.HBM)
     return pl.pallas_call(
         aggregate_kernel,
-        in_specs=[smem, smem, hbm, vmem, vmem, anywhere, anywhere, vmem, vmem],
+        in_specs=[smem, smem, hbm, vmem, vmem, vmem, vmem, vmem, vmem],
         out_specs=[vmem] * 3,
         out_shape=[jax.ShapeDtypeStruct((rows, half), F32)] * 2
         + [jax.ShapeDtypeStruct((2, 2, half), F32)],
         scratch_shapes=[
-            pltpu.VMEM(near.shape, BF16),
             pltpu.VMEM((late,) + adj.shape[1:], BF16),
             pltpu.SemaphoreType.DMA((2 + late,)),
         ],

time: 76.3 us -> 76.9 us (level)
  no operation moved by 1% of the time
where the time goes in v10:
time: 76.9 us; the launch traced here: 75.9 us
  Pallas kernels  32.5 us (42%)
  waiting for transfers between devices  15.6 us (20%)
  blocking collectives  14.5 us (19%)
  starting transfers between devices  12 us (16%)
  local copies, waits for them, and re-layouts  1.14 us (1%)
    all_to_all x1, blocking collectives, local(): lax.all_to_all(stats, ('dom', 'feat'), split_axis=0, concat_axis=0, tiled...  14.5 us
    pallas_call x1, Pallas kernels, adjacency(): pl.pallas_call(adjacency_kernel, grid_spec=pltpu.PrefetchScalarGridSpec(n...  13.3 us
    all_to_all x1, waiting for transfers between devices, local(): lax.all_to_all(outgoing, 'dom', split_axis=0, concat_axis=0, tiled=True)  12.5 us
    all_to_all x1, starting transfers between devices, local(): lax.all_to_all(outgoing, 'dom', split_axis=0, concat_axis=0, tiled=True)  11.8 us
    pallas_call x1, Pallas kernels, aggregate(): pl.pallas_call(aggregate_kernel, in_specs=[smem, smem, hbm, vmem, vmem, v...  7.3 us
    pallas_call x1, Pallas kernels, pick_rows(): pl.pallas_call(pick_kernel, in_specs=[hbm, hbm, hbm], out_specs=hbm, out_...  7.02 us
    pallas_call x1, Pallas kernels, stage(): pl.pallas_call(stage_kernel, in_specs=[pl.BlockSpec(memory_space=pl.ANY),...  3.62 us
    ppermute x1, waiting for transfers between devices, local(): other = lax.ppermute(late_features, 'feat', swap)  2.46 us
  transfers between devices with their start and end apart: 4, of which 3 were waited for; matrix products, arithmetic and copies ran while one was open for 0% of the time, Pallas kernels for 22%

profile of v10, /device:TPU:0, one launch (start us, length us, event | category | flops | bytes accessed | tf_op | source)
XLA Modules:
  0.0 75.9 jit_solution(438002572729910198)
XLA Ops:
  0.0 7.0 %pick_rows.1 = bf16[64,128,128]{2,1,0:T(8,128)(2,1)} custom-call(s32[1,64,128]{2,1,0:T(8,128)} %rows_ref.1, s32[1,64]{1,0:T(1,128)} %counts_ref.1, bf16[4096,128]{1,0:T(8,128)(2,1)} %own_ref.1), custom_call_target="tpu_custom_call" | custom-call | tf_op jit(solution)/shard_map/pick_rows/pallas_call | solution.py:96
  7.0 11.8 %all-to-all-start = ((bf16[64,128,128]{2,1,0:T(8,128)(2,1)}), bf16[64,128,128]{2,1,0:T(8,128)(2,1)}, u32[]{:S(2)}, u32[]{:S(2)}) async-start(bf16[64,128,128]{2,1,0:T(8,128)(2,1)} %pick_rows.1), calls=%async_computation | async-start | bytes 4194304 | tf_op jit(solution)/shard_map/all_to_all | solution.py:364
  18.8 0.0 copy-start
  18.8 0.0 copy-start.7
  18.8 0.0 copy-start.6
  18.8 13.3 %adjacency.1.adj_ref = bf16[16,128,3072]{2,1,0:T(8,128)(2,1)} custom-call(s32[1]{0:T(128)} %bitcast.core_ref, s32[32,24,512]{2,1,0:T(8,128)} %codes_ref.1), custom_call_target="tpu_custom_call" | custom-call | flops 12884901888 | bytes 13369344 | tf_op jit(solution)/shard_map/adjacency/pallas_call | solution.py:144
  32.1 0.0 copy-done
  32.1 0.0 copy-start.8
  32.1 0.0 collective-permute-start
  32.1 0.0 copy-done.7
  32.2 0.0 copy-done.6
  32.2 0.1 fusion.1
  32.3 2.5 %collective-permute-done = bf16[4096,128]{1,0:T(8,128)(2,1)S(1)} collective-permute-done((bf16[4096,128]{1,0:T(8,128)(2,1)S(1)}, bf16[4096,128]{1,0:T(8,128)(2,1)S(1)}, u32[]{:S(2)}, u32[]{:S(2)}) %collective-permute-start) | collective-permute-done | bytes 1048608 | tf_op jit(solution)/shard_map/ppermute | solution.py:367
  34.8 0.0 copy-start.1
  34.8 1.0 %copy-done.1 = bf16[4096,128]{1,0:T(8,128)(2,1)} copy-done((bf16[4096,128]{1,0:T(8,128)(2,1)}, bf16[4096,128]{1,0:T(8,128)(2,1)S(1)}, u32[]{:S(2)}) %copy-start.1) | copy-done | bytes 1048600
  35.7 12.5 %all-to-all-done.mine_ref = bf16[64,128,128]{2,1,0:T(8,128)(2,1)} async-done(((bf16[64,128,128]{2,1,0:T(8,128)(2,1)}), bf16[64,128,128]{2,1,0:T(8,128)(2,1)}, u32[]{:S(2)}, u32[]{:S(2)}) %all-to-all-start) | async-done | bytes 2097184 | tf_op jit(solution)/shard_map/all_to_all | solution.py:364
  48.2 0.0 collective-permute-start.1
  48.3 0.0 copy-done.8
  48.3 0.1 copy.11.tile_src_ref
  48.3 0.0 copy-start.2
  48.3 0.0 copy-start.3
  48.3 3.6 %stage.1 = (bf16[96,128,128]{2,1,0:T(8,128)(2,1)S(1)}, bf16[8,128,3072]{2,1,0:T(8,128)(2,1)S(1)}) custom-call(bf16[32,128,128]{2,1,0:T(8,128)(2,1)S(1)} %bitcast.7, bf16[64,128,128]{2,1,0:T(8,128)(2,1)} %all-to-all-done.mine_ref, bf16[16,128,3072]{2,1,0:T(8,128)(2,1)} %adjacency.1.adj_ref), custom_call_target="tpu_custom_call" | custom-call | tf_op jit(solution)/shard_map/stage/pallas_call | solution.py:186
  52.0 0.7 collective-permute-done.1.sibling_ref
  52.6 0.0 copy-done.2
  52.6 0.0 copy-done.3
  52.6 0.0 copy-start.4
  52.6 0.0 copy-start.5
  52.6 7.3 %aggregate.1 = (f32[2048,128]{1,0:T(8,128)S(1)}, f32[2048,128]{1,0:T(8,128)S(1)}, f32[2,2,128]{2,1,0:T(2,128)S(1)}) custom-call(s32[1]{0:T(128)} %bitcast.core_ref, s32[32,24]{1,0:T(8,128)S(1)} %copy.11.tile_src_ref, bf16[16,128,3072]{2,1,0:T(8,128)(2,1)} %adjacency.1.adj_ref, s32[32,1,128]{2,1,0:T(1,128)S(1)} %bitcast.9, ...), custom_call_target="tpu_custom_call" | custom-call | tf_op jit(solution)/shard_map/aggregate/pallas_call | solution.py:293
  59.9 0.2 collective-permute-start.2
  60.2 14.5 %all_to_all.10.parts_ref = f32[128,2,128]{2,1,0:T(2,128)S(1)} all-to-all(f32[128,2,128]{2,1,0:T(2,128)S(1)} %bitcast.12), channel_id=1, replica_groups=mesh['dom'=64,'feat'=2] {'dom','feat'}, dimensions={0} | all-to-all | bytes 262144 | tf_op jit(solution)/shard_map/all_to_all | solution.py:391
  74.7 0.0 collective-permute-done.2.got_ref
  74.7 0.0 copy-done.4
  74.7 0.0 copy-done.5
  74.7 1.3 %normalise.1 = bf16[4096,128]{1,0:T(8,128)(2,1)} custom-call(s32[1]{0:T(128)} %bitcast.core_ref, f32[2048,128]{1,0:T(8,128)S(1)} %get-tuple-element.24.keep_ref, f32[2048,128]{1,0:T(8,128)S(1)} %collective-permute-done.2.got_ref, f32[128,2,128]{2,1,0:T(2,128)S(1)} %all_to_all.10.parts_ref, f32[1,128]{1,0:T(1,128)S(1)} %bitcast.10, f32[1,128]{1,0:T(1,128)S(1)} %bitcast.11), custom_call_target="tpu_custom_call" | custom-call | tf_op jit(solution)/shard_map/normalise/pallas_call | solution.py:339
  (6 shorter events, 0.1 us)
Async XLA Ops:
  7.0 41.2 %all-to-all-start = ((bf16[64,128,128]{2,1,0:T(8,128)(2,1)}), bf16[64,128,128]{2,1,0:T(8,128)(2,1)}, u32[]{:S(2)}, u32[]{:S(2)}) async-start(bf16[64,128,128]{2,1,0:T(8,128)(2,1)} %pick_rows.1), calls=%async_computation | async-start | bytes 4194304 | tf_op jit(solution)/shard_map/all_to_all | solution.py:364
  18.8 13.3 %copy-start = (bf16[4096,128]{1,0:T(8,128)(2,1)S(1)}, bf16[4096,128]{1,0:T(8,128)(2,1)}, u32[]{:S(2)}) copy-start(bf16[4096,128]{1,0:T(8,128)(2,1)} %own_ref.1) | copy-start | bytes 3145732
  18.8 13.3 %copy-start.7 = (bf16[256,256]{1,0:T(8,128)(2,1)S(1)}, bf16[256,256]{1,0:T(8,128)(2,1)}, u32[]{:S(2)}) copy-start(bf16[256,256]{1,0:T(8,128)(2,1)} %param.16) | copy-start | bytes 393220
  18.8 13.3 %copy-start.6 = (bf16[256,256]{1,0:T(8,128)(2,1)S(1)}, bf16[256,256]{1,0:T(8,128)(2,1)}, u32[]{:S(2)}) copy-start(bf16[256,256]{1,0:T(8,128)(2,1)} %param.17) | copy-start | bytes 393220
  32.1 16.1 %copy-start.8 = (s32[32,24]{0,1:T(8,128)S(1)}, s32[32,24]{0,1:T(8,128)}, u32[]{:S(2)}) copy-start(s32[32,24]{0,1:T(8,128)} %param.13) | copy-start | bytes 9220
  32.1 2.7 %collective-permute-start = (bf16[4096,128]{1,0:T(8,128)(2,1)S(1)}, bf16[4096,128]{1,0:T(8,128)(2,1)S(1)}, u32[]{:S(2)}, u32[]{:S(2)}) collective-permute-start(bf16[4096,128]{1,0:T(8,128)(2,1)S(1)} %copy-done), channel_id=1, source_target_pairs={{0,1},{1,0},{2,3},{3,2},{4,5},{5,4},{6,7},{7,6},{8,9},{9,8},{10,11... | collective-permute-start | bytes 3145736 | tf_op jit(solution)/shard_map/ppermute | solution.py:367
  34.8 1.0 %copy-start.1 = (bf16[4096,128]{1,0:T(8,128)(2,1)}, bf16[4096,128]{1,0:T(8,128)(2,1)S(1)}, u32[]{:S(2)}) copy-start(bf16[4096,128]{1,0:T(8,128)(2,1)S(1)} %collective-permute-done) | copy-start | bytes 3145732
  48.2 4.4 %collective-permute-start.1 = (bf16[64,128,128]{2,1,0:T(8,128)(2,1)}, bf16[64,128,128]{2,1,0:T(8,128)(2,1)S(1)}, u32[]{:S(2)}, u32[]{:S(2)}) collective-permute-start(bf16[64,128,128]{2,1,0:T(8,128)(2,1)} %all-to-all-done.mine_ref), channel_id=1, source_target_pairs={{0,1},{1,0},{2,3},{3,2},{4,5},{5,4},{6,7},{7,6},{8,9},{9,8},{10,11... | collective-permute-start | bytes 6291464 | tf_op jit(solution)/shard_map/ppermute | solution.py:374
  48.3 4.3 %copy-start.2 = (bf16[4096,128]{1,0:T(8,128)(2,1)S(1)}, bf16[4096,128]{1,0:T(8,128)(2,1)}, u32[]{:S(2)}) copy-start(bf16[4096,128]{1,0:T(8,128)(2,1)} %copy-done.1) | copy-start | bytes 3145732
  48.3 4.3 %copy-start.3 = (s32[4096]{0:T(1024)S(1)}, s32[4096]{0:T(1024)}, u32[]{:S(2)}) copy-start(s32[4096]{0:T(1024)} %param.15) | copy-start | bytes 49156
  52.6 22.0 %copy-start.4 = (f32[128]{0:T(128)S(1)}, f32[128]{0:T(128)}, u32[]{:S(2)}) copy-start(f32[128]{0:T(128)} %param.18) | copy-start | bytes 1540
  52.6 22.0 %copy-start.5 = (f32[128]{0:T(128)S(1)}, f32[128]{0:T(128)}, u32[]{:S(2)}) copy-start(f32[128]{0:T(128)} %param.19) | copy-start | bytes 1540
  59.9 14.7 %collective-permute-start.2 = (f32[2048,128]{1,0:T(8,128)S(1)}, f32[2048,128]{1,0:T(8,128)S(1)}, u32[]{:S(2)}, u32[]{:S(2)}) collective-permute-start(f32[2048,128]{1,0:T(8,128)S(1)} %get-tuple-element.25), channel_id=1, source_target_pairs={{0,1},{1,0},{2,3},{3,2},{4,5},{5,4},{6,7},{7,6},{8,9},{9,8},{10,11... | collective-permute-start | bytes 3145736 | tf_op jit(solution)/shard_map/ppermute | solution.py:388
